TPU v7x, 512 devices: a whole 4x8x8 slice. The times are simulated.
512 devices in a mesh: field: 64 (over z, y), batch: 8 (over x, core).
Axes of the slice: x: 4, y: 8, z: 8, core: 2. Of those that a mesh axis runs over, the one named last changes fastest.
Arguments:
- pooled: bfloat16 [4096, 64, 1024], P('batch', 'field'), may hold values from -6 to 6
- counts: int32 [4096, 64], P('batch', 'field'), may hold values from 1 to 16
- w_pairs: bfloat16 [64, 504, 1024], P('field', None, 'batch'), may hold values from -0.03125 to 0.03125
- bias_terms: bfloat16 [1024], P('batch'), may hold values from -4 to 4
- grad_act: bfloat16 [4096, 1024], P('batch'), may hold values from -6 to 6
Outputs:
- entry_grad: bfloat16 [4096, 64, 1024], P('batch', 'field')
- weight_grad: float32 [64, 504, 1024], P('field', None, 'batch')
All inputs are finite; a program needn't handle non-finite values.
Results may differ from a plain program's by a relative error of at most 0.014.
Values may be sent and summed in bfloat16 or wider, within the bound.
No kernel may reach another device: no remote copies, remote signals or barrier semaphores. Data moves between devices by JAX's collectives and lax.ppermute only.
A program may use at most 64 MiB of HBM per device.

v0:
```python
import jax
import jax.numpy as jnp
from jax import lax
from jax.sharding import PartitionSpec as P


def body(pooled, counts, w_pairs, bias_terms, grad_act):
    sample_rows = pooled.shape[0]
    fields = lax.axis_size("field")
    depth = pooled.shape[2] // fields
    half_depth = depth // 2
    my_field = lax.axis_index("field")
    embedded = pooled.reshape(sample_rows, fields, depth)
    partner = jnp.arange(fields, dtype=jnp.int32)[None, :, None]
    upper_half = partner < my_field
    mine = jnp.where(upper_half, embedded[..., half_depth:], embedded[..., :half_depth])
    outbound = jnp.where(upper_half, embedded[..., :half_depth], embedded[..., half_depth:])
    received = lax.all_to_all(
        outbound.reshape(sample_rows, fields * half_depth),
        "field",
        split_axis=1,
        concat_axis=1,
        tiled=True,
    )
    received = received.reshape(sample_rows, fields, half_depth).astype(jnp.float32)
    product_all = (mine.astype(jnp.float32) * received).astype(jnp.bfloat16)
    slot_index = jnp.arange(fields - 1, dtype=jnp.int32)[None, :, None]
    pair_rows = jnp.where(slot_index >= my_field, product_all[:, 1:], product_all[:, :-1])
    pair_rows = pair_rows.reshape(sample_rows, (fields - 1) * half_depth)
    weight_cols, bias_wide = (
        lax.all_gather(w_pairs[0], "batch", axis=1, tiled=True),
        lax.all_gather(bias_terms, "batch", axis=0, tiled=True),
    )
    bias_float = bias_wide.astype(jnp.float32)
    partial_hidden = jnp.dot(pair_rows, weight_cols, preferred_element_type=jnp.float32)
    hidden = lax.psum(partial_hidden, "field")
    preact = hidden + bias_float
    gate_value = jax.nn.sigmoid(preact)
    slope_act = (
        grad_act.astype(jnp.float32) * gate_value * (1.0 + preact * (1.0 - gate_value))
    ).astype(jnp.bfloat16)
    pair_grad = lax.dot_general(
        slope_act, weight_cols, (((1,), (1,)), ((), ())), preferred_element_type=jnp.float32
    )
    pair_grad = pair_grad.reshape(sample_rows, fields - 1, half_depth)
    weight_term = lax.dot_general(
        pair_rows, slope_act, (((0,), (0,)), ((), ())), preferred_element_type=jnp.float32
    )
    weight_grad = lax.psum_scatter(
        weight_term.astype(jnp.bfloat16), "batch", scatter_dimension=1, tiled=True
    ).astype(jnp.float32)
    zero_slot = jnp.zeros((sample_rows, 1, half_depth), jnp.float32)
    below_slots = jnp.concatenate([pair_grad, zero_slot], 1)
    above_slots = jnp.concatenate([zero_slot, pair_grad], 1)
    dense_grad = jnp.where(
        partner < my_field, below_slots, jnp.where(partner > my_field, above_slots, 0.0)
    )
    local_part = dense_grad * received
    outgoing = (
        (dense_grad * mine.astype(jnp.float32))
        .astype(jnp.bfloat16)
        .reshape(sample_rows, fields * half_depth)
    )
    returned = (
        lax.all_to_all(outgoing, "field", split_axis=1, concat_axis=1, tiled=True)
        .reshape(sample_rows, fields, half_depth)
        .astype(jnp.float32)
    )
    full_grad = jnp.where(
        upper_half,
        jnp.concatenate([returned, local_part], -1),
        jnp.concatenate([local_part, returned], -1),
    )
    full_grad = full_grad / jnp.sqrt(counts.astype(jnp.float32))[:, :, None]
    return (
        full_grad.reshape(sample_rows, 1, fields * depth).astype(jnp.bfloat16),
        weight_grad[None],
    )


def solution(mesh):
    in_specs = (
        P("batch", "field", None),
        P("batch", "field"),
        P("field", None, "batch"),
        P("batch"),
        P("batch", None),
    )
    out_specs = (P("batch", "field", None), P("field", None, "batch"))
    return jax.shard_map(body, mesh=mesh, in_specs=in_specs, out_specs=out_specs, check_vma=False)
```

profile of v0, /device:TPU:8, one launch (start us, length us, event | category | flops | bytes accessed | tf_op | source)
XLA Modules:
  0.0 258.7 jit_solution(7724168560010889131)
XLA Ops:
  7.2 0.0 copy-start.1
  7.2 1.5 copy.13
  8.7 0.9 broadcast_select_fusion
  9.7 16.6 %all-to-all-start = ((bf16[512,64,8]{0,2,1:T(8,128)(2,1)}), bf16[512,64,8]{0,2,1:T(8,128)(2,1)S(1)}, u32[]{:S(2)}, u32[]{:S(2)}) async-start(bf16[512,64,8]{0,2,1:T(8,128)(2,1)} %broadcast_select_fusion), calls=%async_computation | async-start | bytes 1048576 | tf_op jit(solution)/shard_map/all_to_all | solution.py:18
  26.3 0.0 all-reduce.4.cloned.1.call-start
  26.3 0.0 copy-done.1
  26.3 14.5 %all-gather = bf16[1,504,1024]{2,1,0:T(8,128)(2,1)S(1)} all-gather(bf16[1,504,128]{2,1,0:T(8,128)(2,1)S(1)} %copy-done.1), channel_id=2, replica_groups=mesh['field'=64,'batch'=8] {'batch'}, dimensions={2}, use_global_device_ids=true | all-gather | bytes 1161216 | tf_op jit(solution)/shard_map/all_gather | solution.py:31
  40.8 4.8 %all-to-all-done = bf16[512,64,8]{0,2,1:T(8,128)(2,1)S(1)} async-done(((bf16[512,64,8]{0,2,1:T(8,128)(2,1)}), bf16[512,64,8]{0,2,1:T(8,128)(2,1)S(1)}, u32[]{:S(2)}, u32[]{:S(2)}) %all-to-all-start) | async-done | bytes 524320 | tf_op jit(solution)/shard_map/all_to_all | solution.py:18
  45.6 0.3 fusion.3
  45.9 0.0 copy-start.3
  45.9 2.2 fusion.5
  48.1 0.0 all-reduce.4.cloned.1.call-update
  48.1 0.0 reduce-scatter.4.cloned.1.call-start
  48.2 0.0 copy-done.3
  48.2 10.6 %all-gather.1 = bf16[8,1,128]{2,1,0:T(2,128)(2,1)S(1)} all-gather(bf16[1,1,128]{2,1,0:T(2,128)(2,1)S(1)} %bitcast.41), channel_id=1, replica_groups=mesh['field'=64,'batch'=8] {'batch'}, dimensions={0}, use_global_device_ids=true | all-gather | bytes 2304 | tf_op jit(solution)/shard_map/all_gather | solution.py:32
  58.7 149.0 %all-reduce.4.cloned.1.call-done = f32[512,1024]{1,0:T(8,128)} async-done(((f32[512,1024]{1,0:T(8,128)}), f32[512,1024]{1,0:T(8,128)}) %all-reduce.4.cloned.1.call-update) | async-done | bytes 2097168 | tf_op jit(solution)/shard_map/psum | solution.py:36
  207.7 2.7 %multiply_convert_fusion = bf16[512,1024]{1,0:T(8,128)(2,1)S(1)} fusion(f32[512,1024]{1,0:T(8,128)} %all-reduce.4.cloned.1.call-done, bf16[512,1024]{1,0:T(8,128)(2,1)} %param.9, f32[1024]{0:T(1024)S(1)} %bitcast.39), kind=kLoop, calls=%fused_computation.5 | loop fusion | flops 5767168 | bytes 4198400 | tf_op jit(solution)/shard_map/convert_element_type | solution.py:41
  210.4 0.0 copy-start
  210.4 1.0 copy-done
  211.4 1.8 convolution_convert_fusion
  213.1 2.3 copy.15
  215.4 0.0 reduce-scatter.4.cloned.1.call-update
  215.4 2.0 convolution_bitcast_fusion
  217.4 0.0 copy-start.2
  217.4 1.2 convert_multiply_fusion
  218.6 8.7 %all-to-all-start.1 = ((bf16[512,64,8]{0,2,1:T(8,128)(2,1)}), bf16[512,64,8]{0,2,1:T(8,128)(2,1)S(1)}, u32[]{:S(2)}, u32[]{:S(2)}) async-start(bf16[512,64,8]{0,2,1:T(8,128)(2,1)} %get-tuple-element.9), calls=%async_computation.1 | async-start | bytes 1048576 | tf_op jit(solution)/shard_map/all_to_all | solution.py:65
  227.3 0.1 broadcast_in_dim.60
  227.4 0.1 broadcast_in_dim.61
  227.4 0.0 copy-done.2
  227.5 15.2 %all-to-all-done.1 = bf16[512,64,8]{0,2,1:T(8,128)(2,1)S(1)} async-done(((bf16[512,64,8]{0,2,1:T(8,128)(2,1)}), bf16[512,64,8]{0,2,1:T(8,128)(2,1)S(1)}, u32[]{:S(2)}, u32[]{:S(2)}) %all-to-all-start.1) | async-done | bytes 524320 | tf_op jit(solution)/shard_map/all_to_all | solution.py:65
  242.7 0.1 convert_element_type.50
  242.8 0.6 pad_maximum_fusion
  243.4 0.3 fusion.1
  243.7 1.3 copy.14
  245.0 5.1 %reduce-scatter.4.cloned.1.call-done = bf16[128,504]{1,0:T(8,128)(2,1)} async-done(((bf16[1024,504]{1,0:T(8,128)(2,1)}), bf16[128,504]{1,0:T(8,128)(2,1)}) %reduce-scatter.4.cloned.1.call-update) | async-done | bytes 129040
  250.1 1.1 copy.16
  251.2 0.7 bitcast_convert_fusion
  (5 shorter events, 0.0 us)
Async XLA Ops:
  7.2 19.1 %copy-start.1 = (bf16[1,504,128]{2,1,0:T(8,128)(2,1)S(1)}, bf16[1,504,128]{2,1,0:T(8,128)(2,1)}, u32[]{:S(2)}) copy-start(bf16[1,504,128]{2,1,0:T(8,128)(2,1)} %param.7) | copy-start | bytes 387076
  9.7 36.0 %all-to-all-start = ((bf16[512,64,8]{0,2,1:T(8,128)(2,1)}), bf16[512,64,8]{0,2,1:T(8,128)(2,1)S(1)}, u32[]{:S(2)}, u32[]{:S(2)}) async-start(bf16[512,64,8]{0,2,1:T(8,128)(2,1)} %broadcast_select_fusion), calls=%async_computation | async-start | bytes 1048576 | tf_op jit(solution)/shard_map/all_to_all | solution.py:18
  26.3 181.5 %all-reduce.4.cloned.1.call-start = ((), (), s32[]{:S(2)}) async-start(), calls=%async_computation.3 | async-start | bytes 4194304 | tf_op jit(solution)/shard_map/psum | solution.py:36
  45.9 2.3 copy-start.3
  48.1 202.0 %reduce-scatter.4.cloned.1.call-start = ((), (), s32[]{:S(2)}) async-start(), calls=%async_computation.4 | async-start | bytes 1179648
  210.4 1.0 copy-start
  217.4 10.1 %copy-start.2 = (s32[512,1]{0,1:T(1,128)S(1)}, s32[512,1]{0,1:T(1,128)}, u32[]{:S(2)}) copy-start(s32[512,1]{0,1:T(1,128)} %param.6) | copy-start | bytes 6148
  218.6 24.1 %all-to-all-start.1 = ((bf16[512,64,8]{0,2,1:T(8,128)(2,1)}), bf16[512,64,8]{0,2,1:T(8,128)(2,1)S(1)}, u32[]{:S(2)}, u32[]{:S(2)}) async-start(bf16[512,64,8]{0,2,1:T(8,128)(2,1)} %get-tuple-element.9), calls=%async_computation.1 | async-start | bytes 1048576 | tf_op jit(solution)/shard_map/all_to_all | solution.py:65
Sparse Core Ops, SparseCore 0:
  48.2 159.4 all-reduce.3
  215.5 34.5 reduce-scatter.3
where the time goes:
time: 259 us
  waiting for transfers between devices  174 us (67%)
  starting transfers between devices  25.3 us (10%)
  blocking collectives  25 us (10%)
  between operations  14.2 us (5%)
  local copies, waits for them, and re-layouts  7.31 us (3%)
  other arithmetic  6.81 us (3%)
  matrix products  5.91 us (2%)
    psum x1, waiting for transfers between devices, body(): hidden = lax.psum(partial_hidden, 'field')  149 us
    all_to_all x1, starting transfers between devices, body(): lax.all_to_all(outbound.reshape(sample_rows, fields * half_depth), 'field...  16.6 us
    all_to_all x1, waiting for transfers between devices, body(): lax.all_to_all(outgoing, 'field', split_axis=1, concat_axis=1, tiled=True)  15.2 us
    all_gather x1, blocking collectives, body(): lax.all_gather(w_pairs[0], 'batch', axis=1, tiled=True)  14.5 us
    all_gather x1, blocking collectives, body(): lax.all_gather(bias_terms, 'batch', axis=0, tiled=True)  10.6 us
    all_to_all x1, starting transfers between devices, body(): lax.all_to_all(outgoing, 'field', split_axis=1, concat_axis=1, tiled=True)  8.66 us
    unnamed x12, local copies, waits for them, and re-layouts  7.14 us
  transfers between devices with their start and end apart: 4, of which 4 were waited for; matrix products, arithmetic and copies ran while one was open for 2% of the time, Pallas kernels for 0%

commit v1 on v0

v1 whole, which is shorter than its diff:
```python
import jax
import jax.numpy as jnp
from jax import lax
from jax.sharding import PartitionSpec as P


def body(pooled, counts, w_pairs, bias_terms, grad_act):
    sample_rows = pooled.shape[0]
    fields = lax.axis_size("field")
    shards = lax.axis_size("batch")
    depth = pooled.shape[2] // fields
    half_depth = depth // 2
    hidden_units = grad_act.shape[1]
    pair_count = w_pairs.shape[1]
    own_rows = sample_rows // fields
    my_field = lax.axis_index("field")
    f32, bf16 = jnp.float32, jnp.bfloat16

    embedded = pooled.reshape(sample_rows, fields, depth).transpose(1, 2, 0)
    partner = jnp.arange(fields, dtype=jnp.int32)[:, None, None]
    upper_half = partner < my_field
    mine = jnp.where(upper_half, embedded[:, half_depth:], embedded[:, :half_depth])
    outbound = jnp.where(upper_half, embedded[:, :half_depth], embedded[:, half_depth:])
    received = lax.all_to_all(outbound, "field", split_axis=0, concat_axis=0, tiled=True)

    bias_rows = jnp.pad(bias_terms[None, :], ((0, 0), (0, 0)))
    weight_bias = lax.all_gather(
        jnp.concatenate([w_pairs[0], bias_rows], 0), "batch", axis=1, tiled=True
    )
    weight_cols = weight_bias[:pair_count]
    bias_float = weight_bias[pair_count].astype(f32)

    received_wide = received.astype(f32)
    mine_wide = mine.astype(f32)
    product_all = (mine_wide * received_wide).astype(bf16)
    slot_index = jnp.arange(fields - 1, dtype=jnp.int32)[:, None, None]
    pair_rows = jnp.where(slot_index >= my_field, product_all[1:], product_all[:-1])
    pair_rows = pair_rows.reshape(pair_count, sample_rows)

    partial_hidden = lax.dot_general(
        pair_rows, weight_cols, (((0,), (0,)), ((), ())), preferred_element_type=f32
    )
    shares = lax.all_to_all(
        partial_hidden.astype(bf16).reshape(fields, own_rows, hidden_units),
        "field", split_axis=0, concat_axis=0, tiled=True,
    )
    preact = jnp.sum(shares.astype(f32), 0) + bias_float[None, :]
    gate_value = jax.nn.sigmoid(preact)
    own_grad = lax.dynamic_slice(grad_act, (my_field * own_rows, 0), (own_rows, hidden_units))
    own_slope = (
        own_grad.astype(f32) * gate_value * (1.0 + preact * (1.0 - gate_value))
    ).astype(bf16)
    slope_act = lax.all_to_all(
        jnp.broadcast_to(own_slope[None], (fields, own_rows, hidden_units)),
        "field", split_axis=0, concat_axis=0, tiled=True,
    ).reshape(sample_rows, hidden_units)

    pair_grad = lax.dot_general(
        weight_cols, slope_act, (((1,), (1,)), ((), ())), preferred_element_type=f32
    ).reshape(fields - 1, half_depth, sample_rows)
    zero_slot = jnp.zeros((1, half_depth, sample_rows), f32)
    below_slots = jnp.concatenate([pair_grad, zero_slot], 0)
    above_slots = jnp.concatenate([zero_slot, pair_grad], 0)
    dense_grad = jnp.where(
        partner < my_field, below_slots, jnp.where(partner > my_field, above_slots, 0.0)
    )
    returned = lax.all_to_all(
        (dense_grad * mine_wide).astype(bf16), "field", split_axis=0, concat_axis=0, tiled=True
    ).astype(f32)

    weight_term = lax.dot_general(
        pair_rows, slope_act, (((1,), (0,)), ((), ())), preferred_element_type=f32
    ).astype(bf16)
    unit_cols = hidden_units // shards
    weight_shares = lax.all_to_all(
        weight_term.reshape(pair_count, shards, unit_cols).transpose(1, 0, 2),
        "batch", split_axis=0, concat_axis=0, tiled=True,
    )
    weight_grad = jnp.sum(weight_shares.astype(f32), 0)

    local_part = dense_grad * received_wide
    full_grad = jnp.concatenate(
        [
            jnp.where(upper_half, returned, local_part),
            jnp.where(upper_half, local_part, returned),
        ],
        1,
    )
    full_grad = full_grad / jnp.sqrt(counts[:, 0].astype(f32))[None, None, :]
    entry_grad = full_grad.astype(bf16).reshape(fields * depth, sample_rows).T
    return entry_grad[:, None, :], weight_grad[None]


def solution(mesh):
    in_specs = (
        P("batch", "field", None),
        P("batch", "field"),
        P("field", None, "batch"),
        P("batch"),
        P("batch", None),
    )
    out_specs = (P("batch", "field", None), P("field", None, "batch"))
    return jax.shard_map(body, mesh=mesh, in_specs=in_specs, out_specs=out_specs, check_vma=False)
```

time: 259 us -> 170 us (0.66)
  waiting for transfers between devices: 174 us -> 63 us
  blocking collectives: 25 us -> 50.5 us
  between operations: 14.2 us -> 0.82 us
  starting transfers between devices: 25.3 us -> 35.5 us
  other arithmetic: 6.81 us -> 9.48 us
    psum x1 -> x0, waiting for transfers between devices: 149 us -> none  [body(): hidden = lax.psum(partial_hidden, 'field')]
    all_to_all x2 -> x4, waiting for transfers between devices: 20.1 us -> 63 us  [the longest x1 29 us: body(): lax.all_to_all(partial_hidden.astype(bf16).reshape(fields, own_rows, hidd...]
    all_to_all x0 -> x1, blocking collectives: none -> 35.8 us  [body(): lax.all_to_all(jnp.broadcast_to(own_slope[None], (fields, own_rows, hidde...]
    all_gather x2 -> x1, blocking collectives: 25 us -> 14.6 us  [body(): lax.all_gather(jnp.concatenate([w_pairs[0], bias_rows], 0), 'batch', axis...]
    all_to_all x2 -> x4, starting transfers between devices: 25.2 us -> 35.5 us  [the longest x1 16.6 us: body(): lax.all_to_all(outbound, 'field', split_axis=0, concat_axis=0, tiled=True)]
    unnamed x12 -> x11, local copies, waits for them, and re-layouts: 7.14 us -> 1.57 us
    unnamed x3 -> x0, waiting for transfers between devices: 5.11 us -> none
  transfers between devices with their start and end apart: 4 -> 4, of which waited for: 4 -> 4; matrix products, arithmetic and copies ran while one was open for 2% -> 4% of each run, Pallas kernels for 0% -> 0%
where the time goes in v1:
time: 170 us; the launch traced here: 169 us
  waiting for transfers between devices  63 us (37%)
  blocking collectives  50.5 us (30%)
  starting transfers between devices  35.5 us (21%)
  other arithmetic  9.48 us (6%)
  matrix products  4.84 us (3%)
  local copies, waits for them, and re-layouts  4.73 us (3%)
    all_to_all x1, blocking collectives, body(): lax.all_to_all(jnp.broadcast_to(own_slope[None], (fields, own_rows, hidde...  35.8 us
    all_to_all x1, waiting for transfers between devices, body(): lax.all_to_all(partial_hidden.astype(bf16).reshape(fields, own_rows, hidd...  29 us
    all_to_all x1, waiting for transfers between devices, body(): lax.all_to_all((dense_grad * mine_wide).astype(bf16), 'field', split_axis...  17 us
    all_to_all x1, starting transfers between devices, body(): lax.all_to_all(outbound, 'field', split_axis=0, concat_axis=0, tiled=True)  16.6 us
    all_gather x1, blocking collectives, body(): lax.all_gather(jnp.concatenate([w_pairs[0], bias_rows], 0), 'batch', axis...  14.6 us
    all_to_all x1, waiting for transfers between devices, body(): lax.all_to_all(weight_term.reshape(pair_count, shards, unit_cols).transpo...  12.3 us
    all_to_all x1, starting transfers between devices, body(): lax.all_to_all(partial_hidden.astype(bf16).reshape(fields, own_rows, hidd...  8.01 us
    all_to_all x1, starting transfers between devices, body(): lax.all_to_all((dense_grad * mine_wide).astype(bf16), 'field', split_axis...  6.67 us
  transfers between devices with their start and end apart: 4, of which 4 were waited for; matrix products, arithmetic and copies ran while one was open for 4% of the time, Pallas kernels for 0%

profile of v1, /device:TPU:8, one launch (start us, length us, event | category | flops | bytes accessed | tf_op | source)
XLA Modules:
  0.0 168.9 jit_solution(5860360318695180854)
XLA Ops:
  0.6 0.0 copy-start.2
  0.7 0.0 copy-start.4
  0.7 1.5 copy.9
  2.2 0.9 broadcast_select_fusion
  3.2 16.6 %all-to-all-start = ((bf16[64,8,512]{2,1,0:T(8,128)(2,1)}), bf16[64,8,512]{2,1,0:T(8,128)(2,1)S(1)}, u32[]{:S(2)}, u32[]{:S(2)}) async-start(bf16[64,8,512]{2,1,0:T(8,128)(2,1)} %broadcast_select_fusion), calls=%async_computation | async-start | bytes 1048576 | tf_op jit(solution)/shard_map/all_to_all | solution.py:24
  19.8 0.0 copy-done.2
  19.8 0.0 copy-done.4
  19.8 14.6 %all_gather.3 = bf16[505,1024]{1,0:T(8,128)(2,1)S(1)} all-gather(bf16[505,128]{1,0:T(8,128)(2,1)S(1)} %pad_maximum_fusion.1), channel_id=1, replica_groups=mesh['field'=64,'batch'=8] {'batch'}, dimensions={1}, use_global_device_ids=true | all-gather | bytes 1163520 | tf_op jit(solution)/shard_map/all_gather | solution.py:27
  34.4 0.0 copy-start
  34.4 4.7 %all-to-all-done = bf16[64,8,512]{2,1,0:T(8,128)(2,1)S(1)} async-done(((bf16[64,8,512]{2,1,0:T(8,128)(2,1)}), bf16[64,8,512]{2,1,0:T(8,128)(2,1)S(1)}, u32[]{:S(2)}, u32[]{:S(2)}) %all-to-all-start) | async-done | bytes 524320 | tf_op jit(solution)/shard_map/all_to_all | solution.py:24
  39.1 0.3 fusion.3
  39.4 1.8 %fusion = bf16[64,8,1024]{2,1,0:T(8,128)(2,1)} fusion(bf16[505,1024]{1,0:T(8,128)(2,1)S(1)} %all_gather.3, bf16[64,8,512]{2,1,0:T(8,128)(2,1)S(1)} %fusion.3, pred[63]{0:T(512)(128)(4,1)S(1)} %iota_compare_fusion.1), kind=kOutput, calls=%fused_computation.6 | convolution fusion | flops 529264640 | bytes 3113472 | tf_op jit(solution)/shard_map/dot_general | solution.py:40
  41.2 0.0 copy-done
  41.2 8.0 %all-to-all-start.1 = ((bf16[64,8,1024]{2,1,0:T(8,128)(2,1)}), bf16[64,8,1024]{2,1,0:T(8,128)(2,1)S(1)}, u32[]{:S(2)}, u32[]{:S(2)}) async-start(bf16[64,8,1024]{2,1,0:T(8,128)(2,1)} %fusion), calls=%async_computation.1 | async-start | bytes 2097152 | tf_op jit(solution)/shard_map/all_to_all | solution.py:43
  49.2 0.7 slice_convert_fusion
  50.0 29.0 %all-to-all-done.1 = bf16[64,8,1024]{2,1,0:T(8,128)(2,1)S(1)} async-done(((bf16[64,8,1024]{2,1,0:T(8,128)(2,1)}), bf16[64,8,1024]{2,1,0:T(8,128)(2,1)S(1)}, u32[]{:S(2)}, u32[]{:S(2)}) %all-to-all-start.1) | async-done | bytes 1048608 | tf_op jit(solution)/shard_map/all_to_all | solution.py:43
  79.0 0.2 convert_reduce_fusion
  79.2 0.7 multiply_convert_fusion
  79.9 0.1 broadcast_in_dim.66
  80.0 35.8 %all_to_all.25 = bf16[64,8,1024]{2,1,0:T(8,128)(2,1)S(1)} all-to-all(bf16[64,8,1024]{2,1,0:T(8,128)(2,1)S(1)} %broadcast_in_dim.66), channel_id=1, replica_groups=mesh['field'=64,'batch'=8] {'field'}, dimensions={0} | all-to-all | bytes 2097152 | tf_op jit(solution)/shard_map/all_to_all | solution.py:53
  115.9 0.0 copy-start.1
  115.9 0.7 fusion.1
  116.6 1.2 copy.14
  117.8 0.0 copy-done.1
  117.8 4.2 %all-to-all-start.4 = ((bf16[8,504,128]{2,1,0:T(8,128)(2,1)}), bf16[8,504,128]{2,1,0:T(8,128)(2,1)}, u32[]{:S(2)}, u32[]{:S(2)}) async-start(bf16[8,504,128]{2,1,0:T(8,128)(2,1)} %bitcast.36), calls=%async_computation.4 | async-start | bytes 2064384 | tf_op jit(solution)/shard_map/all_to_all | solution.py:75
  122.1 2.3 %fusion.4 = f32[63,8,512]{2,1,0:T(8,128)S(1)} fusion(bf16[64,8,1024]{2,1,0:T(8,128)(2,1)} %copy-done.1, bf16[505,1024]{1,0:T(8,128)(2,1)} %copy-done), kind=kOutput, calls=%fused_computation.15 | convolution fusion | flops 528482304 | bytes 3112960 | tf_op jit(solution)/shard_map/dot_general | solution.py:58
  124.3 0.0 copy-start.3
  124.4 1.1 fusion.2
  125.5 12.3 %all-to-all-done.4 = bf16[8,504,128]{2,1,0:T(8,128)(2,1)} async-done(((bf16[8,504,128]{2,1,0:T(8,128)(2,1)}), bf16[8,504,128]{2,1,0:T(8,128)(2,1)}, u32[]{:S(2)}, u32[]{:S(2)}) %all-to-all-start.4) | async-done | bytes 1032224 | tf_op jit(solution)/shard_map/all_to_all | solution.py:75
  137.8 6.7 %all-to-all-start.3 = ((bf16[64,8,512]{2,1,0:T(8,128)(2,1)}), bf16[64,8,512]{2,1,0:T(8,128)(2,1)S(1)}, u32[]{:S(2)}, u32[]{:S(2)}) async-start(bf16[64,8,512]{2,1,0:T(8,128)(2,1)} %fusion.2), calls=%async_computation.3 | async-start | bytes 1048576 | tf_op jit(solution)/shard_map/all_to_all | solution.py:67
  144.5 0.0 copy-done.3
  144.5 2.1 %convert_reduce_fusion.1 = f32[504,128]{1,0:T(8,128)} fusion(bf16[8,504,128]{2,1,0:T(8,128)(2,1)} %all-to-all-done.4), kind=kLoop, calls=%fused_computation.3 | loop fusion | flops 967680 | bytes 1290240 | tf_op jit(solution)/shard_map/reduce_sum | solution.py:79
  146.6 17.0 %all-to-all-done.3 = bf16[64,8,512]{2,1,0:T(8,128)(2,1)S(1)} async-done(((bf16[64,8,512]{2,1,0:T(8,128)(2,1)}), bf16[64,8,512]{2,1,0:T(8,128)(2,1)S(1)}, u32[]{:S(2)}, u32[]{:S(2)}) %all-to-all-start.3) | async-done | bytes 524320 | tf_op jit(solution)/shard_map/all_to_all | solution.py:67
  163.6 0.4 convert_select_fusion.1
  164.0 0.2 pad_maximum_fusion
  164.2 1.9 %copy.10 = f32[1024,512]{0,1:T(8,128)} copy(f32[1024,512]{1,0:T(8,128)S(1)} %bitcast.40) | data formatting | bytes 4194304 | tf_op jit(solution)/shard_map/concatenate | solution.py:82
  166.0 2.8 %fusion.7 = bf16[512,1,1024]{2,0,1:T(8,128)(2,1)} fusion(f32[1024,512]{0,1:T(8,128)} %copy.10, f32[512]{0:T(512)S(1)} %bitcast.44), kind=kLoop, calls=%fused_computation.19 | loop fusion | flops 1048576 | bytes 3147776 | tf_op jit(solution)/shard_map/broadcast_in_dim | solution.py:91
  (5 shorter events, 0.0 us)
Async XLA Ops:
  0.6 19.1 %copy-start.2 = (bf16[1,504,128]{2,1,0:T(8,128)(2,1)S(1)}, bf16[1,504,128]{2,1,0:T(8,128)(2,1)}, u32[]{:S(2)}) copy-start(bf16[1,504,128]{2,1,0:T(8,128)(2,1)} %param.7) | copy-start | bytes 387076
  0.7 19.1 %copy-start.4 = (bf16[128]{0:T(256)(128)(2,1)S(1)}, bf16[128]{0:T(256)(128)(2,1)}, u32[]{:S(2)}) copy-start(bf16[128]{0:T(256)(128)(2,1)} %param.8) | copy-start | bytes 772
  3.2 36.0 %all-to-all-start = ((bf16[64,8,512]{2,1,0:T(8,128)(2,1)}), bf16[64,8,512]{2,1,0:T(8,128)(2,1)S(1)}, u32[]{:S(2)}, u32[]{:S(2)}) async-start(bf16[64,8,512]{2,1,0:T(8,128)(2,1)} %broadcast_select_fusion), calls=%async_computation | async-start | bytes 1048576 | tf_op jit(solution)/shard_map/all_to_all | solution.py:24
  34.4 6.8 %copy-start = (bf16[505,1024]{1,0:T(8,128)(2,1)}, bf16[505,1024]{1,0:T(8,128)(2,1)S(1)}, u32[]{:S(2)}) copy-start(bf16[505,1024]{1,0:T(8,128)(2,1)S(1)} %all_gather.3) | copy-start | bytes 3102724
  41.2 37.8 %all-to-all-start.1 = ((bf16[64,8,1024]{2,1,0:T(8,128)(2,1)}), bf16[64,8,1024]{2,1,0:T(8,128)(2,1)S(1)}, u32[]{:S(2)}, u32[]{:S(2)}) async-start(bf16[64,8,1024]{2,1,0:T(8,128)(2,1)} %fusion), calls=%async_computation.1 | async-start | bytes 2097152 | tf_op jit(solution)/shard_map/all_to_all | solution.py:43
  115.9 1.9 %copy-start.1 = (bf16[64,8,1024]{2,1,0:T(8,128)(2,1)}, bf16[64,8,1024]{2,1,0:T(8,128)(2,1)S(1)}, u32[]{:S(2)}) copy-start(bf16[64,8,1024]{2,1,0:T(8,128)(2,1)S(1)} %all_to_all.25) | copy-start | bytes 3145732
  117.8 20.0 %all-to-all-start.4 = ((bf16[8,504,128]{2,1,0:T(8,128)(2,1)}), bf16[8,504,128]{2,1,0:T(8,128)(2,1)}, u32[]{:S(2)}, u32[]{:S(2)}) async-start(bf16[8,504,128]{2,1,0:T(8,128)(2,1)} %bitcast.36), calls=%async_computation.4 | async-start | bytes 2064384 | tf_op jit(solution)/shard_map/all_to_all | solution.py:75
  124.3 20.1 %copy-start.3 = (s32[512,1]{0,1:T(1,128)S(1)}, s32[512,1]{0,1:T(1,128)}, u32[]{:S(2)}) copy-start(s32[512,1]{0,1:T(1,128)} %param.6) | copy-start | bytes 6148
  137.8 25.8 %all-to-all-start.3 = ((bf16[64,8,512]{2,1,0:T(8,128)(2,1)}), bf16[64,8,512]{2,1,0:T(8,128)(2,1)S(1)}, u32[]{:S(2)}, u32[]{:S(2)}) async-start(bf16[64,8,512]{2,1,0:T(8,128)(2,1)} %fusion.2), calls=%async_computation.3 | async-start | bytes 1048576 | tf_op jit(solution)/shard_map/all_to_all | solution.py:67

commit v2 on v1

v2 whole, which is shorter than its diff:
```python
import jax
import jax.numpy as jnp
from jax import lax
from jax.experimental import pallas as pl
from jax.experimental.pallas import tpu as pltpu
from jax.sharding import Mesh
from jax.sharding import PartitionSpec as P

f32, bf16 = jnp.float32, jnp.bfloat16
GROUP = 8


def upper_of(field_ref, block):
    partner = lax.broadcasted_iota(jnp.int32, (GROUP, 1, 1), 0) + block * GROUP
    return partner < field_ref[0]


def split_kernel(field_ref, pooled_ref, outbound_ref, mine_ref):
    half = outbound_ref.shape[1]
    turned = pooled_ref[...].astype(f32).T.reshape(GROUP, 2 * half, -1)
    low, high = turned[:, :half], turned[:, half:]
    upper = upper_of(field_ref, pl.program_id(0))
    outbound_ref[...] = jnp.where(upper, low, high).astype(bf16)
    mine_ref[...] = jnp.where(upper, high, low).astype(bf16)


def join_kernel(field_ref, root_ref, returned_ref, local_ref, entry_ref):
    returned = returned_ref[...].astype(f32) / root_ref[...][None]
    local = local_ref[...].astype(f32)
    upper = upper_of(field_ref, pl.program_id(0))
    low, high = jnp.where(upper, returned, local), jnp.where(upper, local, returned)
    turned = jnp.concatenate([low, high], 1)
    entry_ref[...] = turned.reshape(-1, turned.shape[2]).T.astype(bf16)


def pair_grad_kernel(root_ref, weight_ref, slope_ref, mine_ref, received_ref, out_ref, local_ref):
    pair_grad = lax.dot_general(
        weight_ref[...], slope_ref[...], (((1,), (1,)), ((), ())), preferred_element_type=f32
    )
    out_ref[...] = (pair_grad * mine_ref[...].astype(f32)).astype(bf16)
    local = pair_grad * received_ref[...].astype(f32)
    local_ref[...] = (local / root_ref[...]).astype(bf16)


def weight_kernel(core_ref, product_ref, slope_ref, sent_ref, kept_ref):
    term = jnp.dot(product_ref[...], slope_ref[...], preferred_element_type=f32)
    cols = term.shape[1] // 2
    first = core_ref[0] == 0
    sent_ref[0] = jnp.where(first, term[:, cols:], term[:, :cols]).astype(bf16)
    kept_ref[0] = jnp.where(first, term[:, :cols], term[:, cols:])


def body(pooled, counts, w_pairs, bias_terms, grad_act):
    sample_rows = pooled.shape[0]
    fields = lax.axis_size("field")
    depth = pooled.shape[2] // fields
    half = depth // 2
    hidden_units = grad_act.shape[1]
    pair_count = w_pairs.shape[1]
    own_rows = sample_rows // fields
    rows = fields * half
    my_field = lax.axis_index("field")
    field_scalar = my_field.astype(jnp.int32).reshape(1)
    smem = pl.BlockSpec(memory_space=pltpu.SMEM)
    root = jnp.sqrt(counts[:, 0].astype(f32))[None, :]

    half_block = pl.BlockSpec((GROUP, half, sample_rows), lambda i: (i, 0, 0))
    wide_block = pl.BlockSpec((sample_rows, GROUP * depth), lambda i: (0, i))
    half_shape = jax.ShapeDtypeStruct((fields, half, sample_rows), bf16)
    outbound, mine = pl.pallas_call(
        split_kernel,
        grid=(fields // GROUP,),
        in_specs=[smem, wide_block],
        out_specs=[half_block, half_block],
        out_shape=[half_shape, half_shape],
        name="split",
    )(field_scalar, pooled[:, 0])
    received = lax.all_to_all(outbound, "field", split_axis=0, concat_axis=0, tiled=True)

    weight_bias = lax.all_gather(
        jnp.concatenate([w_pairs[0], bias_terms[None, :]], 0), ("x", "core"), axis=1, tiled=True
    )
    bias_float = weight_bias[pair_count].astype(f32)
    row = jnp.arange(rows, dtype=jnp.int32)[:, None]
    low_rows = jnp.pad(weight_bias[:pair_count], ((0, half), (0, 0)))
    high_rows = jnp.pad(weight_bias[:pair_count], ((half, 0), (0, 0)))
    own_start = my_field * half
    weight_rows = jnp.where(
        row < own_start, low_rows, jnp.where(row >= own_start + half, high_rows, 0)
    )

    mine = mine.reshape(rows, sample_rows)
    received = received.reshape(rows, sample_rows)
    products = (mine.astype(f32) * received.astype(f32)).astype(bf16)
    partial_hidden = lax.dot_general(
        products, weight_rows, (((0,), (0,)), ((), ())), preferred_element_type=f32
    )
    shares = lax.all_to_all(
        partial_hidden.astype(bf16).reshape(fields, own_rows, hidden_units),
        "field", split_axis=0, concat_axis=0, tiled=True,
    )
    preact = jnp.sum(shares.astype(f32), 0) + bias_float[None, :]
    gate_value = jax.nn.sigmoid(preact)
    own_grad = lax.dynamic_slice(grad_act, (my_field * own_rows, 0), (own_rows, hidden_units))
    own_slope = (
        own_grad.astype(f32) * gate_value * (1.0 + preact * (1.0 - gate_value))
    ).astype(bf16)
    slope_act = lax.all_to_all(
        jnp.broadcast_to(own_slope[None], (fields, own_rows, hidden_units)),
        "field", split_axis=0, concat_axis=0, tiled=True,
    ).reshape(sample_rows, hidden_units)

    tall = 256
    row_block = pl.BlockSpec((tall, sample_rows), lambda i: (i, 0))
    row_shape = jax.ShapeDtypeStruct((rows, sample_rows), bf16)
    outgoing, local = pl.pallas_call(
        pair_grad_kernel,
        grid=(rows // tall,),
        in_specs=[
            pl.BlockSpec((1, sample_rows), lambda i: (0, 0)),
            pl.BlockSpec((tall, hidden_units), lambda i: (i, 0)),
            pl.BlockSpec((sample_rows, hidden_units), lambda i: (0, 0)),
            row_block,
            row_block,
        ],
        out_specs=[row_block, row_block],
        out_shape=[row_shape, row_shape],
        name="pairgrad",
    )(root, weight_rows, slope_act, mine, received)
    returned = lax.all_to_all(
        outgoing.reshape(fields, half, sample_rows),
        "field", split_axis=0, concat_axis=0, tiled=True,
    )

    cores, chips = lax.axis_size("core"), lax.axis_size("x")
    my_core, my_chip = lax.axis_index("core"), lax.axis_index("x")
    unit_cols = hidden_units // (cores * chips)
    term_block = pl.BlockSpec((1, rows, unit_cols), lambda i: (i, 0, 0))
    core_sent, core_kept = pl.pallas_call(
        weight_kernel,
        grid=(chips,),
        in_specs=[
            smem,
            pl.BlockSpec((rows, sample_rows), lambda i: (0, 0)),
            pl.BlockSpec((sample_rows, cores * unit_cols), lambda i: (0, i)),
        ],
        out_specs=[term_block, term_block],
        out_shape=[
            jax.ShapeDtypeStruct((chips, rows, unit_cols), bf16),
            jax.ShapeDtypeStruct((chips, rows, unit_cols), f32),
        ],
        name="weightterm",
    )(my_core.astype(jnp.int32).reshape(1), products, slope_act)
    core_got = lax.ppermute(core_sent, "core", [(0, 1), (1, 0)])
    chip_sum = core_kept + core_got.astype(f32)
    weight_total = lax.dynamic_index_in_dim(chip_sum, my_chip, 0, keepdims=False)
    for step in range(1, chips):
        chip_sent = lax.dynamic_index_in_dim(
            chip_sum, (my_chip + step) % chips, 0, keepdims=False
        ).astype(bf16)
        chip_got = lax.ppermute(
            chip_sent, "x", [(i, (i + step) % chips) for i in range(chips)]
        )
        weight_total = weight_total + chip_got.astype(f32)
    pair_row = jnp.arange(pair_count, dtype=jnp.int32)[:, None]
    weight_grad = jnp.where(pair_row >= own_start, weight_total[half:], weight_total[:-half])

    entry_grad = pl.pallas_call(
        join_kernel,
        grid=(fields // GROUP,),
        in_specs=[
            smem,
            pl.BlockSpec((1, sample_rows), lambda i: (0, 0)),
            half_block,
            half_block,
        ],
        out_specs=wide_block,
        out_shape=jax.ShapeDtypeStruct((sample_rows, fields * depth), bf16),
        name="join",
    )(field_scalar, root, returned, local.reshape(fields, half, sample_rows))
    return entry_grad[:, None, :], weight_grad[None]


def solution(mesh):
    fields = mesh.shape["field"]
    split = Mesh(
        mesh.devices.reshape(fields, mesh.shape["batch"] // 2, 2), ("field", "x", "core")
    )
    batch = ("x", "core")
    in_specs = (
        P(batch, "field", None),
        P(batch, "field"),
        P("field", None, batch),
        P(batch),
        P(batch, None),
    )
    out_specs = (P(batch, "field", None), P("field", None, batch))
    return jax.shard_map(body, mesh=split, in_specs=in_specs, out_specs=out_specs, check_vma=False)
```

time: 170 us -> 167 us (0.982)
  the two profiles are of different devices: /device:TPU:8 before, /device:TPU:10 now
where the time goes in v2:
time: 167 us; the launch traced here: 166 us
  waiting for transfers between devices  72.6 us (43%)
  starting transfers between devices  50.1 us (30%)
  Pallas kernels  18.7 us (11%)
  blocking collectives  14.9 us (9%)
  other arithmetic  4.3 us (3%)
  local copies, waits for them, and re-layouts  3.08 us (2%)
  matrix products  1.73 us (1%)
    all_to_all x1, waiting for transfers between devices, body(): lax.all_to_all(partial_hidden.astype(bf16).reshape(fields, own_rows, hidd...  29.7 us
    all_to_all x1, waiting for transfers between devices, body(): lax.all_to_all(jnp.broadcast_to(own_slope[None], (fields, own_rows, hidde...  28.7 us
    all_to_all x1, starting transfers between devices, body(): lax.all_to_all(outbound, 'field', split_axis=0, concat_axis=0, tiled=True)  16.6 us
    all_gather x1, blocking collectives, body(): lax.all_gather(jnp.concatenate([w_pairs[0], bias_terms[None, :]], 0), ('x...  14.9 us
    all_to_all x1, starting transfers between devices, body(): lax.all_to_all(partial_hidden.astype(bf16).reshape(fields, own_rows, hidd...  8.96 us
    ppermute x3, starting transfers between devices, body(): lax.ppermute(chip_sent, 'x', [(i, (i + step) % chips) for i in range(chip...  8.52 us
    all_to_all x1, starting transfers between devices, body(): lax.all_to_all(jnp.broadcast_to(own_slope[None], (fields, own_rows, hidde...  7.32 us
    all_to_all x1, starting transfers between devices, body(): lax.all_to_all(outgoing.reshape(fields, half, sample_rows), 'field', spli...  6.79 us
  transfers between devices with their start and end apart: 8, of which 6 were waited for; matrix products, arithmetic and copies ran while one was open for 1% of the time, Pallas kernels for 2%

profile of v2, /device:TPU:10, one launch (start us, length us, event | category | flops | bytes accessed | tf_op | source)
XLA Modules:
  0.0 166.3 jit_solution(9549653678130476999)
XLA Ops:
  0.6 0.0 copy-start.6
  0.6 0.0 copy-start.8
  0.7 5.6 %split.1 = (bf16[64,8,512]{2,1,0:T(8,128)(2,1)}, bf16[64,8,512]{2,1,0:T(8,128)(2,1)}) custom-call(s32[1]{0:T(128)} %bitcast.field_ref, bf16[512,1024]{1,0:T(8,128)(2,1)} %bitcast.38), custom_call_target="tpu_custom_call" | custom-call | tf_op jit(solution)/shard_map/split/pallas_call | solution.py:70
  6.2 16.6 %all-to-all-start = ((bf16[64,8,512]{2,1,0:T(8,128)(2,1)}), bf16[64,8,512]{2,1,0:T(8,128)(2,1)S(1)}, u32[]{:S(2)}, u32[]{:S(2)}) async-start(bf16[64,8,512]{2,1,0:T(8,128)(2,1)} %get-tuple-element.9), calls=%async_computation | async-start | bytes 1048576 | tf_op jit(solution)/shard_map/all_to_all | solution.py:78
  22.8 0.0 copy-done.6
  22.8 0.0 copy-done.8
  22.9 14.9 %all_gather.3 = bf16[505,1024]{1,0:T(8,128)(2,1)S(1)} all-gather(bf16[505,128]{1,0:T(8,128)(2,1)S(1)} %pad_maximum_fusion), channel_id=1, replica_groups=mesh['field'=64,'x'=4,'core'=2] {'x','core'}, dimensions={1}, use_global_device_ids=true | all-gather | bytes 1163520 | tf_op jit(solution)/shard_map/all_gather | solution.py:80
  37.7 0.1 slice.17
  37.8 0.4 select_select_fusion.weight_ref
  38.2 0.0 copy-start.2
  38.3 4.0 %all-to-all-done = bf16[64,8,512]{2,1,0:T(8,128)(2,1)S(1)} async-done(((bf16[64,8,512]{2,1,0:T(8,128)(2,1)}), bf16[64,8,512]{2,1,0:T(8,128)(2,1)S(1)}, u32[]{:S(2)}, u32[]{:S(2)}) %all-to-all-start) | async-done | bytes 524320 | tf_op jit(solution)/shard_map/all_to_all | solution.py:78
  42.2 0.0 copy-start.1
  42.2 1.4 multiply_convert_fusion.product_ref
  43.6 0.0 copy-start.3
  43.6 1.7 %fusion = bf16[64,8,1024]{2,1,0:T(8,128)(2,1)} fusion(bf16[512,512]{1,0:T(8,128)(2,1)S(1)} %multiply_convert_fusion.product_ref, bf16[512,1024]{1,0:T(8,128)(2,1)S(1)} %select_select_fusion.weight_ref), kind=kOutput, calls=%fused_computation.2 | convolution fusion | flops 537395200 | bytes 2621440 | tf_op jit(solution)/shard_map/dot_general | solution.py:95
  45.3 0.0 copy-done.2
  45.3 0.0 copy-done.1
  45.3 0.0 copy-done.3
  45.3 9.0 %all-to-all-start.1 = ((bf16[64,8,1024]{2,1,0:T(8,128)(2,1)}), bf16[64,8,1024]{2,1,0:T(8,128)(2,1)S(1)}, u32[]{:S(2)}, u32[]{:S(2)}) async-start(bf16[64,8,1024]{2,1,0:T(8,128)(2,1)} %fusion), calls=%async_computation.1 | async-start | bytes 2097152 | tf_op jit(solution)/shard_map/all_to_all | solution.py:98
  54.3 29.7 %all-to-all-done.1 = bf16[64,8,1024]{2,1,0:T(8,128)(2,1)S(1)} async-done(((bf16[64,8,1024]{2,1,0:T(8,128)(2,1)}), bf16[64,8,1024]{2,1,0:T(8,128)(2,1)S(1)}, u32[]{:S(2)}, u32[]{:S(2)}) %all-to-all-start.1) | async-done | bytes 1048608 | tf_op jit(solution)/shard_map/all_to_all | solution.py:98
  84.1 0.2 convert_reduce_fusion
  84.2 0.7 multiply_convert_fusion.1
  85.0 1.1 broadcast_in_dim.51
  86.1 7.3 %all-to-all-start.2 = ((bf16[64,8,1024]{2,1,0:T(8,128)(2,1)}), bf16[64,8,1024]{2,1,0:T(8,128)(2,1)S(1)}, u32[]{:S(2)}, u32[]{:S(2)}) async-start(bf16[64,8,1024]{2,1,0:T(8,128)(2,1)} %broadcast_in_dim.51), calls=%async_computation.2 | async-start | bytes 2097152 | tf_op jit(solution)/shard_map/all_to_all | solution.py:108
  93.4 0.0 copy-start.7
  93.4 28.7 %all-to-all-done.2 = bf16[64,8,1024]{2,1,0:T(8,128)(2,1)S(1)} async-done(((bf16[64,8,1024]{2,1,0:T(8,128)(2,1)}), bf16[64,8,1024]{2,1,0:T(8,128)(2,1)S(1)}, u32[]{:S(2)}, u32[]{:S(2)}) %all-to-all-start.2) | async-done | bytes 1048608 | tf_op jit(solution)/shard_map/all_to_all | solution.py:108
  122.1 1.0 copy-done
  123.1 4.2 %weightterm.1 = (bf16[4,512,128]{2,1,0:T(8,128)(2,1)}, f32[4,512,128]{2,1,0:T(8,128)}) custom-call(s32[1]{0:T(128)} %bitcast.13.core_ref, bf16[512,512]{1,0:T(8,128)(2,1)} %copy-done.3, bf16[512,1024]{1,0:T(8,128)(2,1)} %bitcast.34), custom_call_target="tpu_custom_call" | custom-call | tf_op jit(solution)/shard_map/weightterm/pallas_call | solution.py:139
  127.3 1.9 %collective-permute-start = (bf16[4,512,128]{2,1,0:T(8,128)(2,1)}, bf16[4,512,128]{2,1,0:T(8,128)(2,1)S(1)}, u32[]{:S(2)}, u32[]{:S(2)}) collective-permute-start(bf16[4,512,128]{2,1,0:T(8,128)(2,1)} %get-tuple-element.13), channel_id=1, source_target_pairs={{0,1},{1,0},{2,3},{3,2},{4,5},{5,4},{6,7},{7,6},{8,9},{9,8},{10,11... | collective-permute-start | bytes 1572872 | tf_op jit(solution)/shard_map/ppermute | solution.py:154
  129.2 0.0 copy-done.7
  129.3 0.6 sqrt_bitcast_fusion.root_ref
  129.8 3.5 %pairgrad.1 = (bf16[512,512]{1,0:T(8,128)(2,1)}, bf16[512,512]{1,0:T(8,128)(2,1)}) custom-call(f32[1,512]{1,0:T(1,128)} %sqrt_bitcast_fusion.root_ref, bf16[512,1024]{1,0:T(8,128)(2,1)} %copy-done.2, bf16[512,1024]{1,0:T(8,128)(2,1)} %bitcast.35, bf16[512,512]{1,0:T(8,128)(2,1)} %bitcast.37, bf16[512,512]{1,0:T(8,128)(2,1)} %bitcast.36), custom_call_target="tpu_custom_call" | custom-call | tf_op jit(solution)/shard_map/pairgrad/pallas_call | solution.py:116
  133.3 6.8 %all-to-all-start.3 = ((bf16[64,8,512]{2,1,0:T(8,128)(2,1)}), bf16[64,8,512]{2,1,0:T(8,128)(2,1)S(1)}, u32[]{:S(2)}, u32[]{:S(2)}) async-start(bf16[64,8,512]{2,1,0:T(8,128)(2,1)} %bitcast.40), calls=%async_computation.3 | async-start | bytes 1048576 | tf_op jit(solution)/shard_map/all_to_all | solution.py:130
  140.2 0.0 collective-permute-done
  140.2 0.0 copy-done.5
  140.2 0.1 convert_add_fusion
  140.3 0.1 fusion.4
  140.4 2.8 %collective-permute-start.1 = (bf16[512,128]{1,0:T(8,128)(2,1)S(1)}, bf16[512,128]{1,0:T(8,128)(2,1)S(1)}, u32[]{:S(2)}, u32[]{:S(2)}) collective-permute-start(bf16[512,128]{1,0:T(8,128)(2,1)S(1)} %get-tuple-element.14), channel_id=1, source_target_pairs={{0,2},{2,4},{4,6},{6,0},{1,3},{3,5},{5,7},{7,1},{8,10},{10,12},{12... | collective-permute-start | bytes 393224 | tf_op jit(solution)/shard_map/ppermute | solution.py:161
  143.2 3.0 %collective-permute-start.3 = (bf16[512,128]{1,0:T(8,128)(2,1)S(1)}, bf16[512,128]{1,0:T(8,128)(2,1)S(1)}, u32[]{:S(2)}, u32[]{:S(2)}) collective-permute-start(bf16[512,128]{1,0:T(8,128)(2,1)S(1)} %get-tuple-element.15), channel_id=1, source_target_pairs={{0,6},{2,0},{4,2},{6,4},{1,7},{3,1},{5,3},{7,5},{8,14},{10,8},{12,... | collective-permute-start | bytes 393224 | tf_op jit(solution)/shard_map/ppermute | solution.py:161
  146.2 2.7 %collective-permute-start.2 = (bf16[512,128]{1,0:T(8,128)(2,1)S(1)}, bf16[512,128]{1,0:T(8,128)(2,1)S(1)}, u32[]{:S(2)}, u32[]{:S(2)}) collective-permute-start(bf16[512,128]{1,0:T(8,128)(2,1)S(1)} %get-tuple-element.16), channel_id=1, source_target_pairs={{0,4},{2,6},{4,0},{6,2},{1,5},{3,7},{5,1},{7,3},{8,12},{10,14},{12... | collective-permute-start | bytes 393224 | tf_op jit(solution)/shard_map/ppermute | solution.py:161
  148.9 0.0 collective-permute-done.1
  148.9 1.2 collective-permute-done.3
  150.2 4.4 %collective-permute-done.2 = bf16[512,128]{1,0:T(8,128)(2,1)S(1)} collective-permute-done((bf16[512,128]{1,0:T(8,128)(2,1)S(1)}, bf16[512,128]{1,0:T(8,128)(2,1)S(1)}, u32[]{:S(2)}, u32[]{:S(2)}) %collective-permute-start.2) | collective-permute-done | bytes 131104 | tf_op jit(solution)/shard_map/ppermute | solution.py:161
  154.6 0.1 fusion.2
  154.6 0.8 fusion.3
  155.5 4.6 %all-to-all-done.3.returned_ref = bf16[64,8,512]{2,1,0:T(8,128)(2,1)S(1)} async-done(((bf16[64,8,512]{2,1,0:T(8,128)(2,1)}), bf16[64,8,512]{2,1,0:T(8,128)(2,1)S(1)}, u32[]{:S(2)}, u32[]{:S(2)}) %all-to-all-start.3) | async-done | bytes 524320 | tf_op jit(solution)/shard_map/all_to_all | solution.py:130
  160.0 0.8 copy-done.4
  160.8 5.4 %join.1 = bf16[512,1024]{1,0:T(8,128)(2,1)} custom-call(s32[1]{0:T(128)} %bitcast.field_ref, f32[1,512]{1,0:T(1,128)} %sqrt_bitcast_fusion.root_ref, bf16[64,8,512]{2,1,0:T(8,128)(2,1)} %copy-done.4, bf16[64,8,512]{2,1,0:T(8,128)(2,1)} %bitcast.41), custom_call_target="tpu_custom_call" | custom-call | tf_op jit(solution)/shard_map/join/pallas_call | solution.py:168
  (7 shorter events, 0.0 us)
Async XLA Ops:
  0.6 22.2 %copy-start.6 = (bf16[1,504,128]{2,1,0:T(8,128)(2,1)S(1)}, bf16[1,504,128]{2,1,0:T(8,128)(2,1)}, u32[]{:S(2)}) copy-start(bf16[1,504,128]{2,1,0:T(8,128)(2,1)} %param.7) | copy-start | bytes 387076
  0.6 22.2 %copy-start.8 = (bf16[128]{0:T(256)(128)(2,1)S(1)}, bf16[128]{0:T(256)(128)(2,1)}, u32[]{:S(2)}) copy-start(bf16[128]{0:T(256)(128)(2,1)} %param.8) | copy-start | bytes 772
  6.2 36.0 %all-to-all-start = ((bf16[64,8,512]{2,1,0:T(8,128)(2,1)}), bf16[64,8,512]{2,1,0:T(8,128)(2,1)S(1)}, u32[]{:S(2)}, u32[]{:S(2)}) async-start(bf16[64,8,512]{2,1,0:T(8,128)(2,1)} %get-tuple-element.9), calls=%async_computation | async-start | bytes 1048576 | tf_op jit(solution)/shard_map/all_to_all | solution.py:78
  38.2 7.1 %copy-start.2 = (bf16[512,1024]{1,0:T(8,128)(2,1)}, bf16[512,1024]{1,0:T(8,128)(2,1)S(1)}, u32[]{:S(2)}) copy-start(bf16[512,1024]{1,0:T(8,128)(2,1)S(1)} %select_select_fusion.weight_ref) | copy-start | bytes 3145732
  42.2 3.1 %copy-start.1 = (bf16[64,8,512]{2,1,0:T(8,128)(2,1)}, bf16[64,8,512]{2,1,0:T(8,128)(2,1)S(1)}, u32[]{:S(2)}) copy-start(bf16[64,8,512]{2,1,0:T(8,128)(2,1)S(1)} %all-to-all-done) | copy-start | bytes 1572868
  43.6 1.7 %copy-start.3 = (bf16[512,512]{1,0:T(8,128)(2,1)}, bf16[512,512]{1,0:T(8,128)(2,1)S(1)}, u32[]{:S(2)}) copy-start(bf16[512,512]{1,0:T(8,128)(2,1)S(1)} %multiply_convert_fusion.product_ref) | copy-start | bytes 1572868
  45.3 38.7 %all-to-all-start.1 = ((bf16[64,8,1024]{2,1,0:T(8,128)(2,1)}), bf16[64,8,1024]{2,1,0:T(8,128)(2,1)S(1)}, u32[]{:S(2)}, u32[]{:S(2)}) async-start(bf16[64,8,1024]{2,1,0:T(8,128)(2,1)} %fusion), calls=%async_computation.1 | async-start | bytes 2097152 | tf_op jit(solution)/shard_map/all_to_all | solution.py:98
  86.1 36.0 %all-to-all-start.2 = ((bf16[64,8,1024]{2,1,0:T(8,128)(2,1)}), bf16[64,8,1024]{2,1,0:T(8,128)(2,1)S(1)}, u32[]{:S(2)}, u32[]{:S(2)}) async-start(bf16[64,8,1024]{2,1,0:T(8,128)(2,1)} %broadcast_in_dim.51), calls=%async_computation.2 | async-start | bytes 2097152 | tf_op jit(solution)/shard_map/all_to_all | solution.py:108
  93.4 35.8 %copy-start.7 = (s32[512,1]{0,1:T(1,128)S(1)}, s32[512,1]{0,1:T(1,128)}, u32[]{:S(2)}) copy-start(s32[512,1]{0,1:T(1,128)} %param.6) | copy-start | bytes 6148
  122.1 1.0 copy-start
  127.3 12.8 %collective-permute-start = (bf16[4,512,128]{2,1,0:T(8,128)(2,1)}, bf16[4,512,128]{2,1,0:T(8,128)(2,1)S(1)}, u32[]{:S(2)}, u32[]{:S(2)}) collective-permute-start(bf16[4,512,128]{2,1,0:T(8,128)(2,1)} %get-tuple-element.13), channel_id=1, source_target_pairs={{0,1},{1,0},{2,3},{3,2},{4,5},{5,4},{6,7},{7,6},{8,9},{9,8},{10,11... | collective-permute-start | bytes 1572872 | tf_op jit(solution)/shard_map/ppermute | solution.py:154
  133.3 6.9 %copy-start.5 = (f32[4,512,128]{2,1,0:T(8,128)S(1)}, f32[4,512,128]{2,1,0:T(8,128)}, u32[]{:S(2)}) copy-start(f32[4,512,128]{2,1,0:T(8,128)} %get-tuple-element.12) | copy-start | bytes 3145732
  133.3 26.7 %all-to-all-start.3 = ((bf16[64,8,512]{2,1,0:T(8,128)(2,1)}), bf16[64,8,512]{2,1,0:T(8,128)(2,1)S(1)}, u32[]{:S(2)}, u32[]{:S(2)}) async-start(bf16[64,8,512]{2,1,0:T(8,128)(2,1)} %bitcast.40), calls=%async_computation.3 | async-start | bytes 1048576 | tf_op jit(solution)/shard_map/all_to_all | solution.py:130
  140.4 8.6 %collective-permute-start.1 = (bf16[512,128]{1,0:T(8,128)(2,1)S(1)}, bf16[512,128]{1,0:T(8,128)(2,1)S(1)}, u32[]{:S(2)}, u32[]{:S(2)}) collective-permute-start(bf16[512,128]{1,0:T(8,128)(2,1)S(1)} %get-tuple-element.14), channel_id=1, source_target_pairs={{0,2},{2,4},{4,6},{6,0},{1,3},{3,5},{5,7},{7,1},{8,10},{10,12},{12... | collective-permute-start | bytes 393224 | tf_op jit(solution)/shard_map/ppermute | solution.py:161
  143.2 7.0 %collective-permute-start.3 = (bf16[512,128]{1,0:T(8,128)(2,1)S(1)}, bf16[512,128]{1,0:T(8,128)(2,1)S(1)}, u32[]{:S(2)}, u32[]{:S(2)}) collective-permute-start(bf16[512,128]{1,0:T(8,128)(2,1)S(1)} %get-tuple-element.15), channel_id=1, source_target_pairs={{0,6},{2,0},{4,2},{6,4},{1,7},{3,1},{5,3},{7,5},{8,14},{10,8},{12,... | collective-permute-start | bytes 393224 | tf_op jit(solution)/shard_map/ppermute | solution.py:161
  146.2 8.4 %collective-permute-start.2 = (bf16[512,128]{1,0:T(8,128)(2,1)S(1)}, bf16[512,128]{1,0:T(8,128)(2,1)S(1)}, u32[]{:S(2)}, u32[]{:S(2)}) collective-permute-start(bf16[512,128]{1,0:T(8,128)(2,1)S(1)} %get-tuple-element.16), channel_id=1, source_target_pairs={{0,4},{2,6},{4,0},{6,2},{1,5},{3,7},{5,1},{7,3},{8,12},{10,14},{12... | collective-permute-start | bytes 393224 | tf_op jit(solution)/shard_map/ppermute | solution.py:161
  160.0 0.8 copy-start.4

commit v3 on v1

v3 whole, which is shorter than its diff:
```python
import jax
import jax.numpy as jnp
from jax import lax
from jax.experimental.layout import Layout, with_layout_constraint
from jax.sharding import Mesh
from jax.sharding import PartitionSpec as P

f32, bf16 = jnp.float32, jnp.bfloat16


def row_major(array):
    return with_layout_constraint(array, Layout(major_to_minor=tuple(range(array.ndim))))


def exchange(blocks):
    return lax.all_to_all(blocks, "field", split_axis=0, concat_axis=0, tiled=True)


def body(pooled, counts, w_pairs, bias_terms, grad_act):
    sample_rows = pooled.shape[0]
    fields = lax.axis_size("field")
    depth = pooled.shape[2] // fields
    half = depth // 2
    hidden_units = grad_act.shape[1]
    pair_count = w_pairs.shape[1]
    own_units = hidden_units // fields
    my_field = lax.axis_index("field")

    embedded = pooled.reshape(sample_rows, fields, depth).transpose(1, 2, 0)
    partner = jnp.arange(fields, dtype=jnp.int32)[:, None, None]
    upper = partner < my_field
    mine = jnp.where(upper, embedded[:, half:], embedded[:, :half])
    outbound = jnp.where(upper, embedded[:, :half], embedded[:, half:])
    received = exchange(outbound)
    weight_turned = row_major(
        lax.all_gather(row_major(w_pairs[0].T), ("x", "core"), axis=0, tiled=True)
    )

    received_wide, mine_wide = received.astype(f32), mine.astype(f32)
    products = (mine_wide * received_wide).astype(bf16)
    slot = jnp.arange(fields - 1, dtype=jnp.int32)[:, None, None]
    pair_rows = jnp.where(slot >= my_field, products[1:], products[:-1])
    pair_rows = pair_rows.reshape(pair_count, sample_rows)

    partial_hidden = jnp.dot(weight_turned, pair_rows, preferred_element_type=f32)
    partial_hidden = row_major(partial_hidden.astype(bf16))
    shares = exchange(partial_hidden.reshape(fields, own_units, sample_rows))

    bias_wide = lax.all_gather(bias_terms, ("x", "core"), axis=0, tiled=True)
    own_start = my_field * own_units
    own_bias = lax.dynamic_slice(bias_wide.reshape(-1, 1), (own_start, 0), (own_units, 1))
    own_grad = lax.dynamic_slice(grad_act, (0, own_start), (sample_rows, own_units)).T
    slot_row = (jnp.arange(fields * half, dtype=jnp.int32) // half)[:, None]
    weight_pairs = weight_turned.T
    below = jnp.pad(weight_pairs, ((0, half), (0, 0)))
    above = jnp.pad(weight_pairs, ((half, 0), (0, 0)))
    weight_rows = row_major(
        jnp.where(slot_row < my_field, below, jnp.where(slot_row > my_field, above, 0))
    )

    preact = jnp.sum(shares.astype(f32), 0) + own_bias.astype(f32)
    gate_value = jax.nn.sigmoid(preact)
    own_slope = (
        own_grad.astype(f32) * gate_value * (1.0 + preact * (1.0 - gate_value))
    ).astype(bf16)
    slope_turned = exchange(
        jnp.broadcast_to(own_slope[None], (fields, own_units, sample_rows))
    ).reshape(hidden_units, sample_rows)

    pair_grad = jnp.dot(weight_rows, slope_turned, preferred_element_type=f32)
    pair_grad = pair_grad.reshape(fields, half, sample_rows)
    outgoing = (pair_grad * mine_wide).astype(bf16)
    returned = exchange(outgoing).astype(f32)

    cores, chips = lax.axis_size("core"), lax.axis_size("x")
    my_core, my_chip = lax.axis_index("core"), lax.axis_index("x")
    term = lax.dot_general(
        slope_turned, pair_rows, (((1,), (1,)), ((), ())), preferred_element_type=f32
    )
    term = term.reshape(chips, cores, hidden_units // (chips * cores), pair_count)
    core_sent = lax.dynamic_index_in_dim(term, 1 - my_core, 1, keepdims=False).astype(bf16)
    core_kept = lax.dynamic_index_in_dim(term, my_core, 1, keepdims=False)
    core_got = lax.ppermute(core_sent, "core", [(0, 1), (1, 0)])
    chip_sum = core_kept + core_got.astype(f32)
    weight_total = lax.dynamic_index_in_dim(chip_sum, my_chip, 0, keepdims=False)
    for step in range(1, chips):
        chip_sent = lax.dynamic_index_in_dim(
            chip_sum, (my_chip + step) % chips, 0, keepdims=False
        ).astype(bf16)
        chip_got = lax.ppermute(
            chip_sent, "x", [(i, (i + step) % chips) for i in range(chips)]
        )
        weight_total = weight_total + chip_got.astype(f32)

    local = pair_grad * received_wide
    full = jnp.concatenate(
        [jnp.where(upper, returned, local), jnp.where(upper, local, returned)], 1
    )
    full = full / jnp.sqrt(counts[:, 0].astype(f32))[None, None, :]
    turned = row_major(full.astype(bf16).reshape(fields * depth, sample_rows))
    return turned.T[:, None, :], weight_total.T[None]


def solution(mesh):
    fields = mesh.shape["field"]
    split = Mesh(
        mesh.devices.reshape(fields, mesh.shape["batch"] // 2, 2), ("field", "x", "core")
    )
    batch = ("x", "core")
    in_specs = (
        P(batch, "field", None),
        P(batch, "field"),
        P("field", None, batch),
        P(batch),
        P(batch, None),
    )
    out_specs = (P(batch, "field", None), P("field", None, batch))
    return jax.shard_map(body, mesh=split, in_specs=in_specs, out_specs=out_specs, check_vma=False)
```

time: 170 us -> 161 us (0.947)
  blocking collectives: 50.5 us -> 25.3 us
  starting transfers between devices: 35.5 us -> 50.7 us
  local copies, waits for them, and re-layouts: 4.73 us -> 9.96 us
  other arithmetic: 9.48 us -> 5.88 us
  waiting for transfers between devices: 63 us -> 60.3 us
  matrix products: 4.84 us -> 7.49 us
    all_to_all x1 -> x0, blocking collectives: 35.8 us -> none  [body(): lax.all_to_all(jnp.broadcast_to(own_slope[None], (fields, own_rows, hidde...]
    ppermute x0 -> x4, starting transfers between devices: none -> 10.9 us  [the longest x3 9.02 us: body(): lax.ppermute(chip_sent, 'x', [(i, (i + step) % chips) for i in range(chip...]
    all_gather x1 -> x2, blocking collectives: 14.6 us -> 25.3 us  [the longest x1 15.1 us: body(): lax.all_gather(row_major(w_pairs[0].T), ('x', 'core'), axis=0, tiled=True)]
    all_to_all x4, waiting for transfers between devices: 63 us -> 53.7 us  [exchange(): lax.all_to_all(blocks, 'field', split_axis=0, concat_axis=0, tiled=True)]
    ppermute x0 -> x4, waiting for transfers between devices: none -> 6.58 us  [the longest x3 6.57 us: body(): lax.ppermute(chip_sent, 'x', [(i, (i + step) % chips) for i in range(chip...]
    all_to_all x4, starting transfers between devices: 35.5 us -> 39.8 us  [exchange(): lax.all_to_all(blocks, 'field', split_axis=0, concat_axis=0, tiled=True)]
    unnamed x11 -> x18, local copies, waits for them, and re-layouts: 1.57 us -> 5.45 us
    dot_general x3, matrix products: 4.84 us -> 7.49 us  [the longest x1 3.76 us: body(): pair_grad = jnp.dot(weight_rows, slope_turned, preferred_element_type=f32)]
  transfers between devices with their start and end apart: 4 -> 8, of which waited for: 4 -> 7; matrix products, arithmetic and copies ran while one was open for 4% -> 6% of each run, Pallas kernels for 0% -> 0%
where the time goes in v3:
time: 161 us
  waiting for transfers between devices  60.3 us (37%)
  starting transfers between devices  50.7 us (31%)
  blocking collectives  25.3 us (16%)
  local copies, waits for them, and re-layouts  9.96 us (6%)
  matrix products  7.49 us (5%)
  other arithmetic  5.88 us (4%)
    all_to_all x4, waiting for transfers between devices, exchange(): lax.all_to_all(blocks, 'field', split_axis=0, concat_axis=0, tiled=True)  53.7 us
    all_to_all x4, starting transfers between devices, exchange(): lax.all_to_all(blocks, 'field', split_axis=0, concat_axis=0, tiled=True)  39.8 us
    all_gather x1, blocking collectives, body(): lax.all_gather(row_major(w_pairs[0].T), ('x', 'core'), axis=0, tiled=True)  15.1 us
    all_gather x1, blocking collectives, body(): bias_wide = lax.all_gather(bias_terms, ('x', 'core'), axis=0, tiled=True)  10.2 us
    ppermute x3, starting transfers between devices, body(): lax.ppermute(chip_sent, 'x', [(i, (i + step) % chips) for i in range(chip...  9.02 us
    ppermute x3, waiting for transfers between devices, body(): lax.ppermute(chip_sent, 'x', [(i, (i + step) % chips) for i in range(chip...  6.57 us
    unnamed x18, local copies, waits for them, and re-layouts  5.45 us
    dot_general x1, matrix products, body(): pair_grad = jnp.dot(weight_rows, slope_turned, preferred_element_type=f32)  3.76 us
  transfers between devices with their start and end apart: 8, of which 7 were waited for; matrix products, arithmetic and copies ran while one was open for 6% of the time, Pallas kernels for 0%

profile of v3, /device:TPU:8, one launch (start us, length us, event | category | flops | bytes accessed | tf_op | source)
XLA Modules:
  0.0 160.5 jit_solution(1778284519050941130)
XLA Ops:
  0.6 0.0 copy-start
  0.6 0.0 copy-start.4
  0.7 1.6 %copy.20 = bf16[512,1,1024]{0,2,1:T(8,128)(2,1)S(1)} copy(bf16[512,1,1024]{2,0,1:T(8,128)(2,1)} %param.5) | data formatting | bytes 2097152 | tf_op args[0]
  2.3 0.9 broadcast_select_fusion
  3.2 16.6 %all-to-all-start = ((bf16[64,8,512]{2,1,0:T(8,128)(2,1)}), bf16[64,8,512]{2,1,0:T(8,128)(2,1)S(1)}, u32[]{:S(2)}, u32[]{:S(2)}) async-start(bf16[64,8,512]{2,1,0:T(8,128)(2,1)} %broadcast_select_fusion), calls=%async_computation | async-start | bytes 1048576 | tf_op jit(solution)/shard_map/all_to_all | solution.py:16
  19.8 0.0 copy-done.4
  19.8 0.1 copy.17
  20.0 15.1 %all_gather.6 = bf16[1024,504]{1,0:T(8,128)(2,1)} all-gather(bf16[128,504]{1,0:T(8,128)(2,1)S(1)} %bitcast.75), channel_id=1, replica_groups=mesh['field'=64,'x'=4,'core'=2] {'x','core'}, dimensions={0}, use_global_device_ids=true | all-gather | bytes 1161216 | tf_op jit(solution)/shard_map/all_gather | solution.py:36
  35.1 4.1 %all-to-all-done = bf16[64,8,512]{2,1,0:T(8,128)(2,1)S(1)} async-done(((bf16[64,8,512]{2,1,0:T(8,128)(2,1)}), bf16[64,8,512]{2,1,0:T(8,128)(2,1)S(1)}, u32[]{:S(2)}, u32[]{:S(2)}) %all-to-all-start) | async-done | bytes 524320 | tf_op jit(solution)/shard_map/all_to_all | solution.py:16
  39.2 0.3 fusion.2
  39.5 1.0 copy-done.2
  40.4 1.8 %convolution_convert_fusion = bf16[512,1024]{0,1:T(8,128)(2,1)} fusion(bf16[1024,504]{1,0:T(8,128)(2,1)S(1)} %copy-done.2, bf16[64,8,512]{2,1,0:T(8,128)(2,1)S(1)} %fusion.2, pred[63]{0:T(512)(128)(4,1)S(1)} %iota_compare_fusion), kind=kOutput, calls=%fused_computation.4 | convolution fusion | flops 529264640 | bytes 3129856 | tf_op jit(solution)/shard_map/dot_general | solution.py:45
  42.2 8.9 %all-to-all-start.1 = ((bf16[64,16,512]{2,1,0:T(8,128)(2,1)}), bf16[64,16,512]{2,1,0:T(8,128)(2,1)}, u32[]{:S(2)}, u32[]{:S(2)}) async-start(bf16[64,16,512]{2,1,0:T(8,128)(2,1)} %bitcast.73), calls=%async_computation.1 | async-start | bytes 2097152 | tf_op jit(solution)/shard_map/all_to_all | solution.py:16
  51.1 0.0 copy-done
  51.1 0.1 constant_dynamic-slice_fusion
  51.2 0.1 copy.23
  51.3 0.0 copy-done.6
  51.3 10.2 %all-gather = bf16[8,1,128]{2,1,0:T(2,128)(2,1)S(1)} all-gather(bf16[1,1,128]{2,1,0:T(2,128)(2,1)S(1)} %bitcast.78), channel_id=1, replica_groups=mesh['field'=64,'x'=4,'core'=2] {'x','core'}, dimensions={0}, use_global_device_ids=true | all-gather | bytes 2304 | tf_op jit(solution)/shard_map/all_gather | solution.py:49
  61.5 0.1 dynamic-slice_convert_fusion.4
  61.6 19.2 %all-to-all-done.1 = bf16[64,16,512]{2,1,0:T(8,128)(2,1)} async-done(((bf16[64,16,512]{2,1,0:T(8,128)(2,1)}), bf16[64,16,512]{2,1,0:T(8,128)(2,1)}, u32[]{:S(2)}, u32[]{:S(2)}) %all-to-all-start.1) | async-done | bytes 1048608 | tf_op jit(solution)/shard_map/all_to_all | solution.py:16
  80.8 1.4 convert_reduce_fusion
  82.2 0.1 fusion.23
  82.3 1.1 broadcast_in_dim.69
  83.4 7.5 %all-to-all-start.2 = ((bf16[64,16,512]{2,1,0:T(8,128)(2,1)}), bf16[64,16,512]{2,1,0:T(8,128)(2,1)}, u32[]{:S(2)}, u32[]{:S(2)}) async-start(bf16[64,16,512]{2,1,0:T(8,128)(2,1)} %broadcast_in_dim.69), calls=%async_computation.2 | async-start | bytes 2097152 | tf_op jit(solution)/shard_map/all_to_all | solution.py:16
  90.9 28.6 %all-to-all-done.2 = bf16[64,16,512]{2,1,0:T(8,128)(2,1)} async-done(((bf16[64,16,512]{2,1,0:T(8,128)(2,1)}), bf16[64,16,512]{2,1,0:T(8,128)(2,1)}, u32[]{:S(2)}, u32[]{:S(2)}) %all-to-all-start.2) | async-done | bytes 1048608 | tf_op jit(solution)/shard_map/all_to_all | solution.py:16
  119.5 2.0 %fusion.13 = f32[4,2,128,504]{2,3,1,0:T(8,128)S(1)} fusion(bf16[4,2,128,512]{3,2,1,0:T(8,128)(2,1)} %bitcast.18, bf16[64,8,512]{2,1,0:T(8,128)(2,1)S(1)} %fusion.2, pred[63]{0:T(512)(128)(4,1)S(1)} %iota_compare_fusion), kind=kOutput, calls=%fused_computation.27 | convolution fusion | flops 528740352 | bytes 4145664 | tf_op jit(solution)/shard_map/dot_general | solution.py:77
  121.5 1.3 copy-done.1
  122.8 0.9 fusion.12
  123.7 1.9 %collective-permute-start = (bf16[4,128,504]{1,2,0:T(8,128)(2,1)}, bf16[4,128,504]{1,2,0:T(8,128)(2,1)}, u32[]{:S(2)}, u32[]{:S(2)}) collective-permute-start(bf16[4,128,504]{1,2,0:T(8,128)(2,1)} %fusion.12), channel_id=1, source_target_pairs={{0,1},{1,0},{2,3},{3,2},{4,5},{5,4},{6,7},{7,6},{8,9},{9,8},{10,11... | collective-permute-start | bytes 1548296 | tf_op jit(solution)/shard_map/ppermute | solution.py:83
  125.6 2.4 %copy.18 = bf16[1024,504]{0,1:T(8,128)(2,1)} copy(bf16[1024,504]{1,0:T(8,128)(2,1)} %all_gather.6) | data formatting | bytes 2064384 | tf_op jit(solution)/shard_map/layout_constraint | solution.py:12
  128.0 3.8 %fusion.1 = (bf16[64,8,512]{2,1,0:T(8,128)(2,1)}, f32[64,8,512]{2,1,0:T(8,128)}) fusion(bf16[64,16,512]{2,1,0:T(8,128)(2,1)S(1)} %bitcast.71, pred[64]{0:T(512)(128)(4,1)S(1)} %iota_compare_fusion.1, bf16[1024,512,1]{1,0,2:T(8,128)(2,1)} %bitcast.13, bf16[504,1024]{1,0:T(8,128)(2,1)} %bitcast.74, pred[512]{0:T(512)(128)(4,1)S(1)} %get-tuple-element.15, ...), kind=kOutput, calls=%fused_computation.10 | convolution fusion | flops 538968064 | bytes 4703296 | tf_op jit(solution)/shard_map/dot_general | solution.py:70
  131.7 6.8 %all-to-all-start.3 = ((bf16[64,8,512]{2,1,0:T(8,128)(2,1)}), bf16[64,8,512]{2,1,0:T(8,128)(2,1)S(1)}, u32[]{:S(2)}, u32[]{:S(2)}) async-start(bf16[64,8,512]{2,1,0:T(8,128)(2,1)} %get-tuple-element.13), calls=%async_computation.3 | async-start | bytes 1048576 | tf_op jit(solution)/shard_map/all_to_all | solution.py:16
  138.6 0.0 copy-start.3
  138.6 0.0 collective-permute-done
  138.6 1.6 bitcast_add_fusion
  140.2 0.1 fusion.19
  140.2 4.3 %collective-permute-start.3 = (bf16[128,504]{0,1:T(8,128)(2,1)S(1)}, bf16[128,504]{0,1:T(8,128)(2,1)S(1)}, u32[]{:S(2)}, u32[]{:S(2)}) collective-permute-start(bf16[128,504]{0,1:T(8,128)(2,1)S(1)} %get-tuple-element.11), channel_id=1, source_target_pairs={{0,6},{2,0},{4,2},{6,4},{1,7},{3,1},{5,3},{7,5},{8,14},{10,8},{12,... | collective-permute-start | bytes 387080 | tf_op jit(solution)/shard_map/ppermute | solution.py:90
  144.6 2.8 %collective-permute-start.2 = (bf16[128,504]{0,1:T(8,128)(2,1)S(1)}, bf16[128,504]{0,1:T(8,128)(2,1)S(1)}, u32[]{:S(2)}, u32[]{:S(2)}) collective-permute-start(bf16[128,504]{0,1:T(8,128)(2,1)S(1)} %get-tuple-element.12), channel_id=1, source_target_pairs={{0,4},{2,6},{4,0},{6,2},{1,5},{3,7},{5,1},{7,3},{8,12},{10,14},{12... | collective-permute-start | bytes 387080 | tf_op jit(solution)/shard_map/ppermute | solution.py:90
  147.3 1.9 %collective-permute-start.1 = (bf16[128,504]{0,1:T(8,128)(2,1)S(1)}, bf16[128,504]{0,1:T(8,128)(2,1)S(1)}, u32[]{:S(2)}, u32[]{:S(2)}) collective-permute-start(bf16[128,504]{0,1:T(8,128)(2,1)S(1)} %get-tuple-element.10), channel_id=1, source_target_pairs={{0,2},{2,4},{4,6},{6,0},{1,3},{3,5},{5,7},{7,1},{8,10},{10,12},{12... | collective-permute-start | bytes 387080 | tf_op jit(solution)/shard_map/ppermute | solution.py:90
  149.3 0.8 collective-permute-done.3
  150.1 3.7 %collective-permute-done.2 = bf16[128,504]{0,1:T(8,128)(2,1)S(1)} collective-permute-done((bf16[128,504]{0,1:T(8,128)(2,1)S(1)}, bf16[128,504]{0,1:T(8,128)(2,1)S(1)}, u32[]{:S(2)}, u32[]{:S(2)}) %collective-permute-start.2) | collective-permute-done | bytes 129056 | tf_op jit(solution)/shard_map/ppermute | solution.py:90
  153.8 2.1 %collective-permute-done.1 = bf16[128,504]{0,1:T(8,128)(2,1)S(1)} collective-permute-done((bf16[128,504]{0,1:T(8,128)(2,1)S(1)}, bf16[128,504]{0,1:T(8,128)(2,1)S(1)}, u32[]{:S(2)}, u32[]{:S(2)}) %collective-permute-start.1) | collective-permute-done | bytes 129056 | tf_op jit(solution)/shard_map/ppermute | solution.py:90
  155.9 0.8 fusion.18
  156.6 1.8 %all-to-all-done.3 = bf16[64,8,512]{2,1,0:T(8,128)(2,1)S(1)} async-done(((bf16[64,8,512]{2,1,0:T(8,128)(2,1)}), bf16[64,8,512]{2,1,0:T(8,128)(2,1)S(1)}, u32[]{:S(2)}, u32[]{:S(2)}) %all-to-all-start.3) | async-done | bytes 524320 | tf_op jit(solution)/shard_map/all_to_all | solution.py:16
  158.5 0.2 convert_select_fusion.1
  158.7 0.2 pad_maximum_fusion
  158.9 0.3 fusion
  159.2 1.3 copy.21
  (11 shorter events, 0.1 us)
Async XLA Ops:
  0.6 50.5 %copy-start = (bf16[512,1024]{1,0:T(8,128)(2,1)S(1)}, bf16[512,1024]{1,0:T(8,128)(2,1)}, u32[]{:S(2)}) copy-start(bf16[512,1024]{1,0:T(8,128)(2,1)} %param.9) | copy-start | bytes 3145732
  0.6 19.2 %copy-start.4 = (bf16[1,504,128]{2,1,0:T(8,128)(2,1)S(1)}, bf16[1,504,128]{2,1,0:T(8,128)(2,1)}, u32[]{:S(2)}) copy-start(bf16[1,504,128]{2,1,0:T(8,128)(2,1)} %param.7) | copy-start | bytes 387076
  3.2 36.0 %all-to-all-start = ((bf16[64,8,512]{2,1,0:T(8,128)(2,1)}), bf16[64,8,512]{2,1,0:T(8,128)(2,1)S(1)}, u32[]{:S(2)}, u32[]{:S(2)}) async-start(bf16[64,8,512]{2,1,0:T(8,128)(2,1)} %broadcast_select_fusion), calls=%async_computation | async-start | bytes 1048576 | tf_op jit(solution)/shard_map/all_to_all | solution.py:16
  39.2 1.2 copy-start.2
  42.2 9.1 %copy-start.6 = (bf16[128]{0:T(256)(128)(2,1)S(1)}, bf16[128]{0:T(256)(128)(2,1)}, u32[]{:S(2)}) copy-start(bf16[128]{0:T(256)(128)(2,1)} %param.8) | copy-start | bytes 772
  42.2 38.6 %all-to-all-start.1 = ((bf16[64,16,512]{2,1,0:T(8,128)(2,1)}), bf16[64,16,512]{2,1,0:T(8,128)(2,1)}, u32[]{:S(2)}, u32[]{:S(2)}) async-start(bf16[64,16,512]{2,1,0:T(8,128)(2,1)} %bitcast.73), calls=%async_computation.1 | async-start | bytes 2097152 | tf_op jit(solution)/shard_map/all_to_all | solution.py:16
  83.4 36.1 %all-to-all-start.2 = ((bf16[64,16,512]{2,1,0:T(8,128)(2,1)}), bf16[64,16,512]{2,1,0:T(8,128)(2,1)}, u32[]{:S(2)}, u32[]{:S(2)}) async-start(bf16[64,16,512]{2,1,0:T(8,128)(2,1)} %broadcast_in_dim.69), calls=%async_computation.2 | async-start | bytes 2097152 | tf_op jit(solution)/shard_map/all_to_all | solution.py:16
  121.5 1.3 copy-start.1
  123.7 14.9 %collective-permute-start = (bf16[4,128,504]{1,2,0:T(8,128)(2,1)}, bf16[4,128,504]{1,2,0:T(8,128)(2,1)}, u32[]{:S(2)}, u32[]{:S(2)}) collective-permute-start(bf16[4,128,504]{1,2,0:T(8,128)(2,1)} %fusion.12), channel_id=1, source_target_pairs={{0,1},{1,0},{2,3},{3,2},{4,5},{5,4},{6,7},{7,6},{8,9},{9,8},{10,11... | collective-permute-start | bytes 1548296 | tf_op jit(solution)/shard_map/ppermute | solution.py:83
  131.7 17.5 %copy-start.5 = (s32[512,1]{0,1:T(1,128)S(1)}, s32[512,1]{0,1:T(1,128)}, u32[]{:S(2)}) copy-start(s32[512,1]{0,1:T(1,128)} %param.6) | copy-start | bytes 6148
  131.7 26.7 %all-to-all-start.3 = ((bf16[64,8,512]{2,1,0:T(8,128)(2,1)}), bf16[64,8,512]{2,1,0:T(8,128)(2,1)S(1)}, u32[]{:S(2)}, u32[]{:S(2)}) async-start(bf16[64,8,512]{2,1,0:T(8,128)(2,1)} %get-tuple-element.13), calls=%async_computation.3 | async-start | bytes 1048576 | tf_op jit(solution)/shard_map/all_to_all | solution.py:16
  138.6 19.9 %copy-start.3 = (f32[64,8,512]{2,1,0:T(8,128)S(1)}, f32[64,8,512]{2,1,0:T(8,128)}, u32[]{:S(2)}) copy-start(f32[64,8,512]{2,1,0:T(8,128)} %get-tuple-element.14) | copy-start | bytes 3145732
  140.2 9.9 %collective-permute-start.3 = (bf16[128,504]{0,1:T(8,128)(2,1)S(1)}, bf16[128,504]{0,1:T(8,128)(2,1)S(1)}, u32[]{:S(2)}, u32[]{:S(2)}) collective-permute-start(bf16[128,504]{0,1:T(8,128)(2,1)S(1)} %get-tuple-element.11), channel_id=1, source_target_pairs={{0,6},{2,0},{4,2},{6,4},{1,7},{3,1},{5,3},{7,5},{8,14},{10,8},{12,... | collective-permute-start | bytes 387080 | tf_op jit(solution)/shard_map/ppermute | solution.py:90
  144.6 9.2 %collective-permute-start.2 = (bf16[128,504]{0,1:T(8,128)(2,1)S(1)}, bf16[128,504]{0,1:T(8,128)(2,1)S(1)}, u32[]{:S(2)}, u32[]{:S(2)}) collective-permute-start(bf16[128,504]{0,1:T(8,128)(2,1)S(1)} %get-tuple-element.12), channel_id=1, source_target_pairs={{0,4},{2,6},{4,0},{6,2},{1,5},{3,7},{5,1},{7,3},{8,12},{10,14},{12... | collective-permute-start | bytes 387080 | tf_op jit(solution)/shard_map/ppermute | solution.py:90
  147.3 8.5 %collective-permute-start.1 = (bf16[128,504]{0,1:T(8,128)(2,1)S(1)}, bf16[128,504]{0,1:T(8,128)(2,1)S(1)}, u32[]{:S(2)}, u32[]{:S(2)}) collective-permute-start(bf16[128,504]{0,1:T(8,128)(2,1)S(1)} %get-tuple-element.10), channel_id=1, source_target_pairs={{0,2},{2,4},{4,6},{6,0},{1,3},{3,5},{5,7},{7,1},{8,10},{10,12},{12... | collective-permute-start | bytes 387080 | tf_op jit(solution)/shard_map/ppermute | solution.py:90

commit v4 on v3

--- a/solution.py
+++ b/solution.py
@@ -2,6 +2,8 @@
 import jax.numpy as jnp
 from jax import lax
 from jax.experimental.layout import Layout, with_layout_constraint
+from jax.experimental import pallas as pl
+from jax.experimental.pallas import tpu as pltpu
 from jax.sharding import Mesh
 from jax.sharding import PartitionSpec as P
 
@@ -14,6 +16,28 @@
 
 def exchange(blocks):
     return lax.all_to_all(blocks, "field", split_axis=0, concat_axis=0, tiled=True)
+
+
+def grad_kernel(place_ref, grad_ref, own_ref, turned_ref):
+    turned_ref[...] = grad_ref[...].astype(f32).T
+    rows = own_ref.shape[0]
+    own_ref[...] = turned_ref[pl.ds(pl.multiple_of(place_ref[1] * rows, rows), rows), :]
+
+
+def own_columns(grad_act, shard, place, units, shard_units):
+    samples = grad_act.shape[0]
+    return pl.pallas_call(
+        grad_kernel,
+        grid_spec=pltpu.PrefetchScalarGridSpec(
+            num_scalar_prefetch=1,
+            grid=(1,),
+            in_specs=[pl.BlockSpec((samples, shard_units), lambda i, place: (0, place[0]))],
+            out_specs=pl.BlockSpec((units, samples), lambda i, place: (0, 0)),
+            scratch_shapes=[pltpu.VMEM((shard_units, samples), f32)],
+        ),
+        out_shape=jax.ShapeDtypeStruct((units, samples), f32),
+        name="owngrad",
+    )(jnp.stack([shard, place]).astype(jnp.int32), grad_act)
 
 
 def body(pooled, counts, w_pairs, bias_terms, grad_act):
@@ -32,8 +56,9 @@
     mine = jnp.where(upper, embedded[:, half:], embedded[:, :half])
     outbound = jnp.where(upper, embedded[:, :half], embedded[:, half:])
     received = exchange(outbound)
+    chip_weights = lax.all_gather(row_major(w_pairs[0].T), "x", axis=0, tiled=True)
     weight_turned = row_major(
-        lax.all_gather(row_major(w_pairs[0].T), ("x", "core"), axis=0, tiled=True)
+        lax.all_gather(row_major(chip_weights), "core", axis=0, tiled=True)
     )
 
     received_wide, mine_wide = received.astype(f32), mine.astype(f32)
@@ -45,43 +70,56 @@
     partial_hidden = jnp.dot(weight_turned, pair_rows, preferred_element_type=f32)
     partial_hidden = row_major(partial_hidden.astype(bf16))
     shares = exchange(partial_hidden.reshape(fields, own_units, sample_rows))
+    other_rows = lax.ppermute(pair_rows, "core", [(0, 1), (1, 0)])
 
     bias_wide = lax.all_gather(bias_terms, ("x", "core"), axis=0, tiled=True)
-    own_start = my_field * own_units
+    cores, chips = lax.axis_size("core"), lax.axis_size("x")
+    my_core, my_chip = lax.axis_index("core"), lax.axis_index("x")
+    shard_units = hidden_units // (cores * chips)
+    own_place = my_field * own_units
+    own_shard = own_place // shard_units
+    own_shard = (own_shard % chips) * cores + own_shard // chips
+    own_start = own_shard * shard_units + own_place % shard_units
     own_bias = lax.dynamic_slice(bias_wide.reshape(-1, 1), (own_start, 0), (own_units, 1))
-    own_grad = lax.dynamic_slice(grad_act, (0, own_start), (sample_rows, own_units)).T
+    own_grad = own_columns(
+        grad_act, own_shard, own_place % shard_units // own_units, own_units, shard_units
+    )
     slot_row = (jnp.arange(fields * half, dtype=jnp.int32) // half)[:, None]
     weight_pairs = weight_turned.T
     below = jnp.pad(weight_pairs, ((0, half), (0, 0)))
     above = jnp.pad(weight_pairs, ((half, 0), (0, 0)))
-    weight_rows = row_major(
-        jnp.where(slot_row < my_field, below, jnp.where(slot_row > my_field, above, 0))
+    weight_rows = lax.optimization_barrier(
+        row_major(
+            jnp.where(slot_row < my_field, below, jnp.where(slot_row > my_field, above, 0))
+        )
     )
 
     preact = jnp.sum(shares.astype(f32), 0) + own_bias.astype(f32)
     gate_value = jax.nn.sigmoid(preact)
     own_slope = (
-        own_grad.astype(f32) * gate_value * (1.0 + preact * (1.0 - gate_value))
+        own_grad * gate_value * (1.0 + preact * (1.0 - gate_value))
     ).astype(bf16)
     slope_turned = exchange(
         jnp.broadcast_to(own_slope[None], (fields, own_units, sample_rows))
     ).reshape(hidden_units, sample_rows)
 
-    pair_grad = jnp.dot(weight_rows, slope_turned, preferred_element_type=f32)
+    pair_grad = lax.optimization_barrier(
+        jnp.dot(weight_rows, slope_turned, preferred_element_type=f32)
+    )
     pair_grad = pair_grad.reshape(fields, half, sample_rows)
     outgoing = (pair_grad * mine_wide).astype(bf16)
     returned = exchange(outgoing).astype(f32)
 
-    cores, chips = lax.axis_size("core"), lax.axis_size("x")
-    my_core, my_chip = lax.axis_index("core"), lax.axis_index("x")
-    term = lax.dot_general(
-        slope_turned, pair_rows, (((1,), (1,)), ((), ())), preferred_element_type=f32
+    halves = slope_turned.reshape(cores, chips, shard_units, sample_rows)
+    kept = lax.dynamic_index_in_dim(halves, my_core, 0, keepdims=False)
+    sent = lax.dynamic_index_in_dim(halves, 1 - my_core, 0, keepdims=False)
+    got = lax.ppermute(sent, "core", [(0, 1), (1, 0)])
+    chip_sum = lax.dot_general(
+        kept, pair_rows, (((2,), (1,)), ((), ())), preferred_element_type=f32
     )
-    term = term.reshape(chips, cores, hidden_units // (chips * cores), pair_count)
-    core_sent = lax.dynamic_index_in_dim(term, 1 - my_core, 1, keepdims=False).astype(bf16)
-    core_kept = lax.dynamic_index_in_dim(term, my_core, 1, keepdims=False)
-    core_got = lax.ppermute(core_sent, "core", [(0, 1), (1, 0)])
-    chip_sum = core_kept + core_got.astype(f32)
+    chip_sum = chip_sum + lax.dot_general(
+        got, other_rows, (((2,), (1,)), ((), ())), preferred_element_type=f32
+    )
     weight_total = lax.dynamic_index_in_dim(chip_sum, my_chip, 0, keepdims=False)
     for step in range(1, chips):
         chip_sent = lax.dynamic_index_in_dim(
@@ -98,7 +136,8 @@
     )
     full = full / jnp.sqrt(counts[:, 0].astype(f32))[None, None, :]
     turned = row_major(full.astype(bf16).reshape(fields * depth, sample_rows))
-    return turned.T[:, None, :], weight_total.T[None]
+    entry_grad = turned.T[:, None, :]
+    return entry_grad, weight_total.T[None]
 
 
 def solution(mesh):

time: 161 us -> 158 us (0.981)
  the two profiles are of different devices: /device:TPU:8 before, /device:TPU:1 now
where the time goes in v4:
time: 158 us; the launch traced here: 157 us
  starting transfers between devices  62.4 us (39%)
  waiting for transfers between devices  37.8 us (24%)
  blocking collectives  27.5 us (17%)
  other arithmetic  11.7 us (7%)
  local copies, waits for them, and re-layouts  7.46 us (5%)
  matrix products  7.2 us (5%)
  Pallas kernels  2.29 us (1%)
    all_to_all x4, starting transfers between devices, exchange(): lax.all_to_all(blocks, 'field', split_axis=0, concat_axis=0, tiled=True)  43 us
    all_to_all x4, waiting for transfers between devices, exchange(): lax.all_to_all(blocks, 'field', split_axis=0, concat_axis=0, tiled=True)  31.2 us
    all_gather x1, blocking collectives, body(): lax.all_gather(row_major(w_pairs[0].T), 'x', axis=0, tiled=True)  11.8 us
    all_gather x1, blocking collectives, body(): bias_wide = lax.all_gather(bias_terms, ('x', 'core'), axis=0, tiled=True)  11.2 us
    ppermute x3, starting transfers between devices, body(): lax.ppermute(chip_sent, 'x', [(i, (i + step) % chips) for i in range(chip...  9.03 us
    ppermute x3, waiting for transfers between devices, body(): lax.ppermute(chip_sent, 'x', [(i, (i + step) % chips) for i in range(chip...  6.66 us
    ppermute x1, starting transfers between devices, body(): got = lax.ppermute(sent, 'core', [(0, 1), (1, 0)])  6.49 us
    all_gather x1, blocking collectives, body(): lax.all_gather(row_major(chip_weights), 'core', axis=0, tiled=True)  4.45 us
  transfers between devices with their start and end apart: 9, of which 5 were waited for; matrix products, arithmetic and copies ran while one was open for 10% of the time, Pallas kernels for 1%

profile of v4, /device:TPU:1, one launch (start us, length us, event | category | flops | bytes accessed | tf_op | source)
XLA Modules:
  0.0 157.3 jit_solution(7507533333532182818)
XLA Ops:
  0.6 0.0 copy-start
  0.7 1.5 copy.17
  2.2 0.9 broadcast_select_fusion
  3.1 17.1 %all-to-all-start = ((bf16[64,8,512]{2,1,0:T(8,128)(2,1)}), bf16[64,8,512]{2,1,0:T(8,128)(2,1)S(1)}, u32[]{:S(2)}, u32[]{:S(2)}) async-start(bf16[64,8,512]{2,1,0:T(8,128)(2,1)} %broadcast_select_fusion), calls=%async_computation | async-start | bytes 1048576 | tf_op jit(solution)/shard_map/all_to_all | solution.py:18
  20.3 0.1 copy.15
  20.4 11.8 %all_gather.9 = bf16[512,504]{1,0:T(8,128)(2,1)S(1)} all-gather(bf16[128,504]{1,0:T(8,128)(2,1)S(1)} %bitcast.75), channel_id=1, replica_groups=mesh['field'=64,'x'=4,'core'=2] {'x'}, dimensions={0}, use_global_device_ids=true | all-gather | bytes 645120 | tf_op jit(solution)/shard_map/all_gather | solution.py:59
  32.2 4.5 %all_gather.10 = bf16[1024,504]{1,0:T(8,128)(2,1)S(1)} all-gather(bf16[512,504]{1,0:T(8,128)(2,1)S(1)} %all_gather.9), channel_id=1, replica_groups=mesh['field'=64,'x'=4,'core'=2] {'core'}, dimensions={0}, use_global_device_ids=true | all-gather | bytes 1548288 | tf_op jit(solution)/shard_map/all_gather | solution.py:61
  36.7 1.0 all-to-all-done
  37.7 0.3 fusion.2
  38.0 1.8 %convolution_convert_fusion = bf16[512,1024]{0,1:T(8,128)(2,1)} fusion(bf16[1024,504]{1,0:T(8,128)(2,1)S(1)} %all_gather.10, bf16[64,8,512]{2,1,0:T(8,128)(2,1)S(1)} %fusion.2, pred[63]{0:T(512)(128)(4,1)S(1)} %iota_compare_fusion), kind=kOutput, calls=%fused_computation.4 | convolution fusion | flops 529264640 | bytes 3129856 | tf_op jit(solution)/shard_map/dot_general | solution.py:70
  39.7 11.8 %all-to-all-start.1 = ((bf16[64,16,512]{2,1,0:T(8,128)(2,1)}), bf16[64,16,512]{2,1,0:T(8,128)(2,1)}, u32[]{:S(2)}, u32[]{:S(2)}) async-start(bf16[64,16,512]{2,1,0:T(8,128)(2,1)} %bitcast.74), calls=%async_computation.1 | async-start | bytes 2097152 | tf_op jit(solution)/shard_map/all_to_all | solution.py:18
  51.6 0.7 pad_add_fusion.place_ref
  52.3 2.3 %owngrad.1 = f32[16,512]{1,0:T(8,128)} custom-call(s32[2]{0:T(128)} %pad_add_fusion.place_ref, bf16[512,1024]{1,0:T(8,128)(2,1)} %grad_ref.1), custom_call_target="tpu_custom_call" | custom-call | tf_op jit(solution)/shard_map/owngrad/pallas_call | solution.py:29
  54.6 11.2 %all-gather = bf16[8,1,128]{2,1,0:T(2,128)(2,1)S(1)} all-gather(bf16[1,1,128]{2,1,0:T(2,128)(2,1)S(1)} %bitcast.78), channel_id=1, replica_groups=mesh['field'=64,'x'=4,'core'=2] {'x','core'}, dimensions={0}, use_global_device_ids=true | all-gather | bytes 2304 | tf_op jit(solution)/shard_map/all_gather | solution.py:75
  65.8 0.1 dynamic-slice_convert_fusion.3
  65.9 13.2 %all-to-all-done.1 = bf16[64,16,512]{2,1,0:T(8,128)(2,1)} async-done(((bf16[64,16,512]{2,1,0:T(8,128)(2,1)}), bf16[64,16,512]{2,1,0:T(8,128)(2,1)}, u32[]{:S(2)}, u32[]{:S(2)}) %all-to-all-start.1) | async-done | bytes 1048608 | tf_op jit(solution)/shard_map/all_to_all | solution.py:18
  79.2 1.4 convert_reduce_fusion
  80.6 0.8 multiply_convert_fusion
  81.4 1.1 broadcast_in_dim.69
  82.5 7.8 %all-to-all-start.2 = ((bf16[64,16,512]{2,1,0:T(8,128)(2,1)}), bf16[64,16,512]{2,1,0:T(8,128)(2,1)}, u32[]{:S(2)}, u32[]{:S(2)}) async-start(bf16[64,16,512]{2,1,0:T(8,128)(2,1)} %broadcast_in_dim.69), calls=%async_computation.2 | async-start | bytes 2097152 | tf_op jit(solution)/shard_map/all_to_all | solution.py:18
  90.4 1.4 copy.16
  91.7 2.9 %select_select_fusion = bf16[512,1024]{1,0:T(8,128)(2,1)} fusion(bf16[504,1024]{1,0:T(8,128)(2,1)} %bitcast.73, pred[512]{0:T(512)(128)(4,1)S(1)} %get-tuple-element.13, pred[512]{0:T(512)(128)(4,1)S(1)} %get-tuple-element.14), kind=kLoop, calls=%fused_computation.13 | loop fusion | flops 1048576 | bytes 2081792 | tf_op jit(solution)/shard_map/jit(_where)/select_n | solution.py:93
  94.6 1.0 fusion.26
  95.6 3.9 %collective-permute-start.1 = (bf16[504,512]{1,0:T(8,128)(2,1)}, bf16[504,512]{1,0:T(8,128)(2,1)}, u32[]{:S(2)}, u32[]{:S(2)}) collective-permute-start(bf16[504,512]{1,0:T(8,128)(2,1)} %fusion.26), channel_id=1, source_target_pairs={{0,1},{1,0},{2,3},{3,2},{4,5},{5,4},{6,7},{7,6},{8,9},{9,8},{10,11... | collective-permute-start | bytes 1548296 | tf_op jit(solution)/shard_map/ppermute | solution.py:73
  99.5 17.0 %all-to-all-done.2 = bf16[64,16,512]{2,1,0:T(8,128)(2,1)} async-done(((bf16[64,16,512]{2,1,0:T(8,128)(2,1)}), bf16[64,16,512]{2,1,0:T(8,128)(2,1)}, u32[]{:S(2)}, u32[]{:S(2)}) %all-to-all-start.2) | async-done | bytes 1048608 | tf_op jit(solution)/shard_map/all_to_all | solution.py:18
  116.5 2.2 %fusion.21 = f32[512,512]{1,0:T(8,128)S(1)} fusion(bf16[512,1024]{1,0:T(8,128)(2,1)} %select_select_fusion, bf16[1024,512]{1,0:T(8,128)(2,1)} %bitcast.12), kind=kOutput, calls=%fused_computation.50 | convolution fusion | flops 536870912 | bytes 3145728 | tf_op jit(solution)/shard_map/dot_general | solution.py:107
  118.7 1.9 %dynamic-slice_bitcast_fusion = bf16[4,128,512]{2,1,0:T(8,128)(2,1)} fusion(bf16[2,4,128,512]{3,2,1,0:T(8,128)(2,1)} %bitcast.18, s32[]{:T(128)S(6)} %select_n.113), kind=kLoop, calls=%fused_computation.16 | loop fusion | bytes 1048580 | tf_op jit(solution)/shard_map/jit(dynamic_index_in_dim)/squeeze | solution.py:115
  120.6 6.5 %collective-permute-start = (bf16[4,128,512]{2,1,0:T(8,128)(2,1)}, bf16[4,128,512]{2,1,0:T(8,128)(2,1)}, u32[]{:S(2)}, u32[]{:S(2)}) collective-permute-start(bf16[4,128,512]{2,1,0:T(8,128)(2,1)} %dynamic-slice_bitcast_fusion), channel_id=1, source_target_pairs={{0,1},{1,0},{2,3},{3,2},{4,5},{5,4},{6,7},{7,6},{8,9},{9,8},{10,11... | collective-permute-start | bytes 1572872 | tf_op jit(solution)/shard_map/ppermute | solution.py:116
  127.1 1.0 fusion.1
  128.1 6.2 %all-to-all-start.3 = ((bf16[64,8,512]{2,1,0:T(8,128)(2,1)}), bf16[64,8,512]{2,1,0:T(8,128)(2,1)}, u32[]{:S(2)}, u32[]{:S(2)}) async-start(bf16[64,8,512]{2,1,0:T(8,128)(2,1)} %fusion.1), calls=%async_computation.3 | async-start | bytes 1048576 | tf_op jit(solution)/shard_map/all_to_all | solution.py:18
  134.4 1.5 fusion.3
  135.9 0.0 copy-start.1
  135.9 0.0 collective-permute-done.1
  135.9 0.0 collective-permute-done
  135.9 1.7 %convolution_add_fusion = f32[4,128,504]{1,2,0:T(8,128)S(1)} fusion(f32[4,128,504]{1,2,0:T(8,128)S(1)} %fusion.3, bf16[4,128,512]{2,1,0:T(8,128)(2,1)} %collective-permute-done, bf16[504,512]{1,0:T(8,128)(2,1)} %collective-permute-done.1), kind=kOutput, calls=%fused_computation.5 | convolution fusion | flops 264499200 | bytes 3104768 | tf_op jit(solution)/shard_map/dot_general | solution.py:120
  137.6 0.1 fusion.11
  137.7 4.6 %collective-permute-start.4 = (bf16[128,504]{0,1:T(8,128)(2,1)S(1)}, bf16[128,504]{0,1:T(8,128)(2,1)S(1)}, u32[]{:S(2)}, u32[]{:S(2)}) collective-permute-start(bf16[128,504]{0,1:T(8,128)(2,1)S(1)} %get-tuple-element.11), channel_id=1, source_target_pairs={{0,6},{2,0},{4,2},{6,4},{1,7},{3,1},{5,3},{7,5},{8,14},{10,8},{12,... | collective-permute-start | bytes 387080 | tf_op jit(solution)/shard_map/ppermute | solution.py:128
  142.3 2.5 %collective-permute-start.3 = (bf16[128,504]{0,1:T(8,128)(2,1)S(1)}, bf16[128,504]{0,1:T(8,128)(2,1)S(1)}, u32[]{:S(2)}, u32[]{:S(2)}) collective-permute-start(bf16[128,504]{0,1:T(8,128)(2,1)S(1)} %get-tuple-element.12), channel_id=1, source_target_pairs={{0,4},{2,6},{4,0},{6,2},{1,5},{3,7},{5,1},{7,3},{8,12},{10,14},{12... | collective-permute-start | bytes 387080 | tf_op jit(solution)/shard_map/ppermute | solution.py:128
  144.8 1.9 %collective-permute-start.2 = (bf16[128,504]{0,1:T(8,128)(2,1)S(1)}, bf16[128,504]{0,1:T(8,128)(2,1)S(1)}, u32[]{:S(2)}, u32[]{:S(2)}) collective-permute-start(bf16[128,504]{0,1:T(8,128)(2,1)S(1)} %get-tuple-element.10), channel_id=1, source_target_pairs={{0,2},{2,4},{4,6},{6,0},{1,3},{3,5},{5,7},{7,1},{8,10},{10,12},{12... | collective-permute-start | bytes 387080 | tf_op jit(solution)/shard_map/ppermute | solution.py:128
  146.7 0.0 collective-permute-done.4
  146.7 3.5 %collective-permute-done.3 = bf16[128,504]{0,1:T(8,128)(2,1)S(1)} collective-permute-done((bf16[128,504]{0,1:T(8,128)(2,1)S(1)}, bf16[128,504]{0,1:T(8,128)(2,1)S(1)}, u32[]{:S(2)}, u32[]{:S(2)}) %collective-permute-start.3) | collective-permute-done | bytes 129056 | tf_op jit(solution)/shard_map/ppermute | solution.py:128
  150.2 3.2 %collective-permute-done.2 = bf16[128,504]{0,1:T(8,128)(2,1)S(1)} collective-permute-done((bf16[128,504]{0,1:T(8,128)(2,1)S(1)}, bf16[128,504]{0,1:T(8,128)(2,1)S(1)}, u32[]{:S(2)}, u32[]{:S(2)}) %collective-permute-start.2) | collective-permute-done | bytes 129056 | tf_op jit(solution)/shard_map/ppermute | solution.py:128
  153.4 0.8 fusion.10
  154.2 0.0 all-to-all-done.3
  154.2 1.3 convert_select_fusion.1
  155.4 0.2 pad_maximum_fusion
  155.7 0.3 fusion
  156.0 1.3 copy.18
  (9 shorter events, 0.1 us)
Async XLA Ops:
  0.6 19.6 %copy-start = (bf16[1,504,128]{2,1,0:T(8,128)(2,1)S(1)}, bf16[1,504,128]{2,1,0:T(8,128)(2,1)}, u32[]{:S(2)}) copy-start(bf16[1,504,128]{2,1,0:T(8,128)(2,1)} %param.7) | copy-start | bytes 387076
  3.1 34.6 %all-to-all-start = ((bf16[64,8,512]{2,1,0:T(8,128)(2,1)}), bf16[64,8,512]{2,1,0:T(8,128)(2,1)S(1)}, u32[]{:S(2)}, u32[]{:S(2)}) async-start(bf16[64,8,512]{2,1,0:T(8,128)(2,1)} %broadcast_select_fusion), calls=%async_computation | async-start | bytes 1048576 | tf_op jit(solution)/shard_map/all_to_all | solution.py:18
  39.7 14.9 %copy-start.2 = (bf16[128]{0:T(256)(128)(2,1)S(1)}, bf16[128]{0:T(256)(128)(2,1)}, u32[]{:S(2)}) copy-start(bf16[128]{0:T(256)(128)(2,1)} %param.8) | copy-start | bytes 772
  39.7 39.4 %all-to-all-start.1 = ((bf16[64,16,512]{2,1,0:T(8,128)(2,1)}), bf16[64,16,512]{2,1,0:T(8,128)(2,1)}, u32[]{:S(2)}, u32[]{:S(2)}) async-start(bf16[64,16,512]{2,1,0:T(8,128)(2,1)} %bitcast.74), calls=%async_computation.1 | async-start | bytes 2097152 | tf_op jit(solution)/shard_map/all_to_all | solution.py:18
  82.5 33.9 %all-to-all-start.2 = ((bf16[64,16,512]{2,1,0:T(8,128)(2,1)}), bf16[64,16,512]{2,1,0:T(8,128)(2,1)}, u32[]{:S(2)}, u32[]{:S(2)}) async-start(bf16[64,16,512]{2,1,0:T(8,128)(2,1)} %broadcast_in_dim.69), calls=%async_computation.2 | async-start | bytes 2097152 | tf_op jit(solution)/shard_map/all_to_all | solution.py:18
  95.6 40.3 %collective-permute-start.1 = (bf16[504,512]{1,0:T(8,128)(2,1)}, bf16[504,512]{1,0:T(8,128)(2,1)}, u32[]{:S(2)}, u32[]{:S(2)}) collective-permute-start(bf16[504,512]{1,0:T(8,128)(2,1)} %fusion.26), channel_id=1, source_target_pairs={{0,1},{1,0},{2,3},{3,2},{4,5},{5,4},{6,7},{7,6},{8,9},{9,8},{10,11... | collective-permute-start | bytes 1548296 | tf_op jit(solution)/shard_map/ppermute | solution.py:73
  120.6 15.3 %collective-permute-start = (bf16[4,128,512]{2,1,0:T(8,128)(2,1)}, bf16[4,128,512]{2,1,0:T(8,128)(2,1)}, u32[]{:S(2)}, u32[]{:S(2)}) collective-permute-start(bf16[4,128,512]{2,1,0:T(8,128)(2,1)} %dynamic-slice_bitcast_fusion), channel_id=1, source_target_pairs={{0,1},{1,0},{2,3},{3,2},{4,5},{5,4},{6,7},{7,6},{8,9},{9,8},{10,11... | collective-permute-start | bytes 1572872 | tf_op jit(solution)/shard_map/ppermute | solution.py:116
  128.1 26.0 %all-to-all-start.3 = ((bf16[64,8,512]{2,1,0:T(8,128)(2,1)}), bf16[64,8,512]{2,1,0:T(8,128)(2,1)}, u32[]{:S(2)}, u32[]{:S(2)}) async-start(bf16[64,8,512]{2,1,0:T(8,128)(2,1)} %fusion.1), calls=%async_computation.3 | async-start | bytes 1048576 | tf_op jit(solution)/shard_map/all_to_all | solution.py:18
  135.9 10.8 %copy-start.1 = (s32[512,1]{0,1:T(1,128)S(1)}, s32[512,1]{0,1:T(1,128)}, u32[]{:S(2)}) copy-start(s32[512,1]{0,1:T(1,128)} %param.6) | copy-start | bytes 6148
  137.7 9.1 %collective-permute-start.4 = (bf16[128,504]{0,1:T(8,128)(2,1)S(1)}, bf16[128,504]{0,1:T(8,128)(2,1)S(1)}, u32[]{:S(2)}, u32[]{:S(2)}) collective-permute-start(bf16[128,504]{0,1:T(8,128)(2,1)S(1)} %get-tuple-element.11), channel_id=1, source_target_pairs={{0,6},{2,0},{4,2},{6,4},{1,7},{3,1},{5,3},{7,5},{8,14},{10,8},{12,... | collective-permute-start | bytes 387080 | tf_op jit(solution)/shard_map/ppermute | solution.py:128
  142.3 7.9 %collective-permute-start.3 = (bf16[128,504]{0,1:T(8,128)(2,1)S(1)}, bf16[128,504]{0,1:T(8,128)(2,1)S(1)}, u32[]{:S(2)}, u32[]{:S(2)}) collective-permute-start(bf16[128,504]{0,1:T(8,128)(2,1)S(1)} %get-tuple-element.12), channel_id=1, source_target_pairs={{0,4},{2,6},{4,0},{6,2},{1,5},{3,7},{5,1},{7,3},{8,12},{10,14},{12... | collective-permute-start | bytes 387080 | tf_op jit(solution)/shard_map/ppermute | solution.py:128
  144.8 8.6 %collective-permute-start.2 = (bf16[128,504]{0,1:T(8,128)(2,1)S(1)}, bf16[128,504]{0,1:T(8,128)(2,1)S(1)}, u32[]{:S(2)}, u32[]{:S(2)}) collective-permute-start(bf16[128,504]{0,1:T(8,128)(2,1)S(1)} %get-tuple-element.10), channel_id=1, source_target_pairs={{0,2},{2,4},{4,6},{6,0},{1,3},{3,5},{5,7},{7,1},{8,10},{10,12},{12... | collective-permute-start | bytes 387080 | tf_op jit(solution)/shard_map/ppermute | solution.py:128

commit v5 on v4

--- a/solution.py
+++ b/solution.py
@@ -120,13 +120,16 @@
     chip_sum = chip_sum + lax.dot_general(
         got, other_rows, (((2,), (1,)), ((), ())), preferred_element_type=f32
     )
-    weight_total = lax.dynamic_index_in_dim(chip_sum, my_chip, 0, keepdims=False)
-    for step in range(1, chips):
-        chip_sent = lax.dynamic_index_in_dim(
-            chip_sum, (my_chip + step) % chips, 0, keepdims=False
-        ).astype(bf16)
+    blocks = [
+        lax.dynamic_index_in_dim(chip_sum, (my_chip + step) % chips, 0, keepdims=False)
+        for step in range(chips)
+    ]
+    weight_total, *blocks = lax.optimization_barrier(
+        (blocks[0], *[block.astype(bf16) for block in blocks[1:]])
+    )
+    for step, block in enumerate(blocks, 1):
         chip_got = lax.ppermute(
-            chip_sent, "x", [(i, (i + step) % chips) for i in range(chips)]
+            block, "x", [(i, (i + step) % chips) for i in range(chips)]
         )
         weight_total = weight_total + chip_got.astype(f32)
 

time: 158 us -> 158 us (level)
  no operation moved by 1% of the time
where the time goes in v5:
time: 158 us; the launch traced here: 157 us
  starting transfers between devices  62.4 us (39%)
  waiting for transfers between devices  37.8 us (24%)
  blocking collectives  27.5 us (17%)
  other arithmetic  11.7 us (7%)
  local copies, waits for them, and re-layouts  7.48 us (5%)
  matrix products  7.19 us (5%)
  Pallas kernels  2.29 us (1%)
    all_to_all x4, starting transfers between devices, exchange(): lax.all_to_all(blocks, 'field', split_axis=0, concat_axis=0, tiled=True)  43 us
    all_to_all x4, waiting for transfers between devices, exchange(): lax.all_to_all(blocks, 'field', split_axis=0, concat_axis=0, tiled=True)  31.2 us
    all_gather x1, blocking collectives, body(): lax.all_gather(row_major(w_pairs[0].T), 'x', axis=0, tiled=True)  11.8 us
    all_gather x1, blocking collectives, body(): bias_wide = lax.all_gather(bias_terms, ('x', 'core'), axis=0, tiled=True)  11.2 us
    ppermute x3, starting transfers between devices, body(): lax.ppermute(block, 'x', [(i, (i + step) % chips) for i in range(chips)])  9.02 us
    ppermute x3, waiting for transfers between devices, body(): lax.ppermute(block, 'x', [(i, (i + step) % chips) for i in range(chips)])  6.66 us
    ppermute x1, starting transfers between devices, body(): got = lax.ppermute(sent, 'core', [(0, 1), (1, 0)])  6.49 us
    all_gather x1, blocking collectives, body(): lax.all_gather(row_major(chip_weights), 'core', axis=0, tiled=True)  4.45 us
  transfers between devices with their start and end apart: 9, of which 5 were waited for; matrix products, arithmetic and copies ran while one was open for 10% of the time, Pallas kernels for 1%

profile of v5, /device:TPU:1, one launch (start us, length us, event | category | flops | bytes accessed | tf_op | source)
XLA Modules:
  0.0 157.3 jit_solution(15128568130514238008)
XLA Ops:
  0.6 0.0 copy-start
  0.7 1.5 copy.17
  2.2 0.9 broadcast_select_fusion
  3.1 17.1 %all-to-all-start = ((bf16[64,8,512]{2,1,0:T(8,128)(2,1)}), bf16[64,8,512]{2,1,0:T(8,128)(2,1)S(1)}, u32[]{:S(2)}, u32[]{:S(2)}) async-start(bf16[64,8,512]{2,1,0:T(8,128)(2,1)} %broadcast_select_fusion), calls=%async_computation | async-start | bytes 1048576 | tf_op jit(solution)/shard_map/all_to_all | solution.py:18
  20.3 0.1 copy.15
  20.4 11.8 %all_gather.9 = bf16[512,504]{1,0:T(8,128)(2,1)S(1)} all-gather(bf16[128,504]{1,0:T(8,128)(2,1)S(1)} %bitcast.69), channel_id=1, replica_groups=mesh['field'=64,'x'=4,'core'=2] {'x'}, dimensions={0}, use_global_device_ids=true | all-gather | bytes 645120 | tf_op jit(solution)/shard_map/all_gather | solution.py:59
  32.2 4.5 %all_gather.10 = bf16[1024,504]{1,0:T(8,128)(2,1)S(1)} all-gather(bf16[512,504]{1,0:T(8,128)(2,1)S(1)} %all_gather.9), channel_id=1, replica_groups=mesh['field'=64,'x'=4,'core'=2] {'core'}, dimensions={0}, use_global_device_ids=true | all-gather | bytes 1548288 | tf_op jit(solution)/shard_map/all_gather | solution.py:61
  36.7 1.0 all-to-all-done
  37.7 0.3 fusion.2
  38.0 1.8 %convolution_convert_fusion = bf16[512,1024]{0,1:T(8,128)(2,1)} fusion(bf16[1024,504]{1,0:T(8,128)(2,1)S(1)} %all_gather.10, bf16[64,8,512]{2,1,0:T(8,128)(2,1)S(1)} %fusion.2, pred[63]{0:T(512)(128)(4,1)S(1)} %iota_compare_fusion), kind=kOutput, calls=%fused_computation.4 | convolution fusion | flops 529264640 | bytes 3129856 | tf_op jit(solution)/shard_map/dot_general | solution.py:70
  39.7 11.8 %all-to-all-start.1 = ((bf16[64,16,512]{2,1,0:T(8,128)(2,1)}), bf16[64,16,512]{2,1,0:T(8,128)(2,1)}, u32[]{:S(2)}, u32[]{:S(2)}) async-start(bf16[64,16,512]{2,1,0:T(8,128)(2,1)} %bitcast.68), calls=%async_computation.1 | async-start | bytes 2097152 | tf_op jit(solution)/shard_map/all_to_all | solution.py:18
  51.6 0.7 pad_add_fusion.place_ref
  52.3 2.3 %owngrad.1 = f32[16,512]{1,0:T(8,128)} custom-call(s32[2]{0:T(128)} %pad_add_fusion.place_ref, bf16[512,1024]{1,0:T(8,128)(2,1)} %grad_ref.1), custom_call_target="tpu_custom_call" | custom-call | tf_op jit(solution)/shard_map/owngrad/pallas_call | solution.py:29
  54.6 11.2 %all-gather = bf16[8,1,128]{2,1,0:T(2,128)(2,1)S(1)} all-gather(bf16[1,1,128]{2,1,0:T(2,128)(2,1)S(1)} %bitcast.72), channel_id=1, replica_groups=mesh['field'=64,'x'=4,'core'=2] {'x','core'}, dimensions={0}, use_global_device_ids=true | all-gather | bytes 2304 | tf_op jit(solution)/shard_map/all_gather | solution.py:75
  65.9 0.1 dynamic-slice_convert_fusion.3
  65.9 13.2 %all-to-all-done.1 = bf16[64,16,512]{2,1,0:T(8,128)(2,1)} async-done(((bf16[64,16,512]{2,1,0:T(8,128)(2,1)}), bf16[64,16,512]{2,1,0:T(8,128)(2,1)}, u32[]{:S(2)}, u32[]{:S(2)}) %all-to-all-start.1) | async-done | bytes 1048608 | tf_op jit(solution)/shard_map/all_to_all | solution.py:18
  79.2 1.4 convert_reduce_fusion
  80.6 0.8 multiply_convert_fusion
  81.4 1.1 broadcast_in_dim.69
  82.5 7.8 %all-to-all-start.2 = ((bf16[64,16,512]{2,1,0:T(8,128)(2,1)}), bf16[64,16,512]{2,1,0:T(8,128)(2,1)}, u32[]{:S(2)}, u32[]{:S(2)}) async-start(bf16[64,16,512]{2,1,0:T(8,128)(2,1)} %broadcast_in_dim.69), calls=%async_computation.2 | async-start | bytes 2097152 | tf_op jit(solution)/shard_map/all_to_all | solution.py:18
  90.4 1.4 copy.16
  91.7 2.9 %select_select_fusion = bf16[512,1024]{1,0:T(8,128)(2,1)} fusion(bf16[504,1024]{1,0:T(8,128)(2,1)} %bitcast.67, pred[512]{0:T(512)(128)(4,1)S(1)} %get-tuple-element.21, pred[512]{0:T(512)(128)(4,1)S(1)} %get-tuple-element.22), kind=kLoop, calls=%fused_computation.13 | loop fusion | flops 1048576 | bytes 2081792 | tf_op jit(solution)/shard_map/jit(_where)/select_n | solution.py:93
  94.6 1.0 fusion.23
  95.6 3.9 %collective-permute-start.1 = (bf16[504,512]{1,0:T(8,128)(2,1)}, bf16[504,512]{1,0:T(8,128)(2,1)}, u32[]{:S(2)}, u32[]{:S(2)}) collective-permute-start(bf16[504,512]{1,0:T(8,128)(2,1)} %fusion.23), channel_id=1, source_target_pairs={{0,1},{1,0},{2,3},{3,2},{4,5},{5,4},{6,7},{7,6},{8,9},{9,8},{10,11... | collective-permute-start | bytes 1548296 | tf_op jit(solution)/shard_map/ppermute | solution.py:73
  99.5 17.0 %all-to-all-done.2 = bf16[64,16,512]{2,1,0:T(8,128)(2,1)} async-done(((bf16[64,16,512]{2,1,0:T(8,128)(2,1)}), bf16[64,16,512]{2,1,0:T(8,128)(2,1)}, u32[]{:S(2)}, u32[]{:S(2)}) %all-to-all-start.2) | async-done | bytes 1048608 | tf_op jit(solution)/shard_map/all_to_all | solution.py:18
  116.5 2.2 %fusion.18 = f32[512,512]{1,0:T(8,128)S(1)} fusion(bf16[512,1024]{1,0:T(8,128)(2,1)} %select_select_fusion, bf16[1024,512]{1,0:T(8,128)(2,1)} %bitcast.12), kind=kOutput, calls=%fused_computation.48 | convolution fusion | flops 536870912 | bytes 3145728 | tf_op jit(solution)/shard_map/dot_general | solution.py:107
  118.7 1.9 %dynamic-slice_bitcast_fusion = bf16[4,128,512]{2,1,0:T(8,128)(2,1)} fusion(bf16[2,4,128,512]{3,2,1,0:T(8,128)(2,1)} %bitcast.18, s32[]{:T(128)S(6)} %select_n.117), kind=kLoop, calls=%fused_computation.16 | loop fusion | bytes 1048580 | tf_op jit(solution)/shard_map/jit(dynamic_index_in_dim)/squeeze | solution.py:115
  120.6 6.5 %collective-permute-start = (bf16[4,128,512]{2,1,0:T(8,128)(2,1)}, bf16[4,128,512]{2,1,0:T(8,128)(2,1)}, u32[]{:S(2)}, u32[]{:S(2)}) collective-permute-start(bf16[4,128,512]{2,1,0:T(8,128)(2,1)} %dynamic-slice_bitcast_fusion), channel_id=1, source_target_pairs={{0,1},{1,0},{2,3},{3,2},{4,5},{5,4},{6,7},{7,6},{8,9},{9,8},{10,11... | collective-permute-start | bytes 1572872 | tf_op jit(solution)/shard_map/ppermute | solution.py:116
  127.1 1.0 fusion.1
  128.1 6.2 %all-to-all-start.3 = ((bf16[64,8,512]{2,1,0:T(8,128)(2,1)}), bf16[64,8,512]{2,1,0:T(8,128)(2,1)}, u32[]{:S(2)}, u32[]{:S(2)}) async-start(bf16[64,8,512]{2,1,0:T(8,128)(2,1)} %fusion.1), calls=%async_computation.3 | async-start | bytes 1048576 | tf_op jit(solution)/shard_map/all_to_all | solution.py:18
  134.4 1.5 fusion.3
  135.9 0.0 copy-start.1
  135.9 0.0 collective-permute-done.1
  135.9 0.0 collective-permute-done
  135.9 1.7 %convolution_add_fusion = f32[4,128,504]{1,2,0:T(8,128)S(1)} fusion(f32[4,128,504]{1,2,0:T(8,128)S(1)} %fusion.3, bf16[4,128,512]{2,1,0:T(8,128)(2,1)} %collective-permute-done, bf16[504,512]{1,0:T(8,128)(2,1)} %collective-permute-done.1), kind=kOutput, calls=%fused_computation.5 | convolution fusion | flops 264499200 | bytes 3104768 | tf_op jit(solution)/shard_map/dot_general | solution.py:120
  137.6 0.1 fusion.10
  137.7 4.6 %collective-permute-start.4 = (bf16[128,504]{0,1:T(8,128)(2,1)S(1)}, bf16[128,504]{0,1:T(8,128)(2,1)S(1)}, u32[]{:S(2)}, u32[]{:S(2)}) collective-permute-start(bf16[128,504]{0,1:T(8,128)(2,1)S(1)} %get-tuple-element.9), channel_id=1, source_target_pairs={{0,6},{2,0},{4,2},{6,4},{1,7},{3,1},{5,3},{7,5},{8,14},{10,8},{12,... | collective-permute-start | bytes 387080 | tf_op jit(solution)/shard_map/ppermute | solution.py:131
  142.3 2.5 %collective-permute-start.3 = (bf16[128,504]{0,1:T(8,128)(2,1)S(1)}, bf16[128,504]{0,1:T(8,128)(2,1)S(1)}, u32[]{:S(2)}, u32[]{:S(2)}) collective-permute-start(bf16[128,504]{0,1:T(8,128)(2,1)S(1)} %get-tuple-element.8), channel_id=1, source_target_pairs={{0,4},{2,6},{4,0},{6,2},{1,5},{3,7},{5,1},{7,3},{8,12},{10,14},{12... | collective-permute-start | bytes 387080 | tf_op jit(solution)/shard_map/ppermute | solution.py:131
  144.8 1.9 %collective-permute-start.2 = (bf16[128,504]{0,1:T(8,128)(2,1)S(1)}, bf16[128,504]{0,1:T(8,128)(2,1)S(1)}, u32[]{:S(2)}, u32[]{:S(2)}) collective-permute-start(bf16[128,504]{0,1:T(8,128)(2,1)S(1)} %get-tuple-element.7), channel_id=1, source_target_pairs={{0,2},{2,4},{4,6},{6,0},{1,3},{3,5},{5,7},{7,1},{8,10},{10,12},{12... | collective-permute-start | bytes 387080 | tf_op jit(solution)/shard_map/ppermute | solution.py:131
  146.8 0.0 collective-permute-done.4
  146.8 3.5 %collective-permute-done.3 = bf16[128,504]{0,1:T(8,128)(2,1)S(1)} collective-permute-done((bf16[128,504]{0,1:T(8,128)(2,1)S(1)}, bf16[128,504]{0,1:T(8,128)(2,1)S(1)}, u32[]{:S(2)}, u32[]{:S(2)}) %collective-permute-start.3) | collective-permute-done | bytes 129056 | tf_op jit(solution)/shard_map/ppermute | solution.py:131
  150.2 3.2 %collective-permute-done.2 = bf16[128,504]{0,1:T(8,128)(2,1)S(1)} collective-permute-done((bf16[128,504]{0,1:T(8,128)(2,1)S(1)}, bf16[128,504]{0,1:T(8,128)(2,1)S(1)}, u32[]{:S(2)}, u32[]{:S(2)}) %collective-permute-start.2) | collective-permute-done | bytes 129056 | tf_op jit(solution)/shard_map/ppermute | solution.py:131
  153.4 0.8 add_bitcast_fusion
  154.2 0.0 all-to-all-done.3
  154.2 1.3 convert_select_fusion.1
  155.5 0.2 pad_maximum_fusion
  155.7 0.3 fusion
  156.0 1.3 copy.18
  (10 shorter events, 0.1 us)
Async XLA Ops:
  0.6 19.6 %copy-start = (bf16[1,504,128]{2,1,0:T(8,128)(2,1)S(1)}, bf16[1,504,128]{2,1,0:T(8,128)(2,1)}, u32[]{:S(2)}) copy-start(bf16[1,504,128]{2,1,0:T(8,128)(2,1)} %param.7) | copy-start | bytes 387076
  3.1 34.6 %all-to-all-start = ((bf16[64,8,512]{2,1,0:T(8,128)(2,1)}), bf16[64,8,512]{2,1,0:T(8,128)(2,1)S(1)}, u32[]{:S(2)}, u32[]{:S(2)}) async-start(bf16[64,8,512]{2,1,0:T(8,128)(2,1)} %broadcast_select_fusion), calls=%async_computation | async-start | bytes 1048576 | tf_op jit(solution)/shard_map/all_to_all | solution.py:18
  39.7 14.9 %copy-start.2 = (bf16[128]{0:T(256)(128)(2,1)S(1)}, bf16[128]{0:T(256)(128)(2,1)}, u32[]{:S(2)}) copy-start(bf16[128]{0:T(256)(128)(2,1)} %param.8) | copy-start | bytes 772
  39.7 39.4 %all-to-all-start.1 = ((bf16[64,16,512]{2,1,0:T(8,128)(2,1)}), bf16[64,16,512]{2,1,0:T(8,128)(2,1)}, u32[]{:S(2)}, u32[]{:S(2)}) async-start(bf16[64,16,512]{2,1,0:T(8,128)(2,1)} %bitcast.68), calls=%async_computation.1 | async-start | bytes 2097152 | tf_op jit(solution)/shard_map/all_to_all | solution.py:18
  82.5 33.9 %all-to-all-start.2 = ((bf16[64,16,512]{2,1,0:T(8,128)(2,1)}), bf16[64,16,512]{2,1,0:T(8,128)(2,1)}, u32[]{:S(2)}, u32[]{:S(2)}) async-start(bf16[64,16,512]{2,1,0:T(8,128)(2,1)} %broadcast_in_dim.69), calls=%async_computation.2 | async-start | bytes 2097152 | tf_op jit(solution)/shard_map/all_to_all | solution.py:18
  95.6 40.3 %collective-permute-start.1 = (bf16[504,512]{1,0:T(8,128)(2,1)}, bf16[504,512]{1,0:T(8,128)(2,1)}, u32[]{:S(2)}, u32[]{:S(2)}) collective-permute-start(bf16[504,512]{1,0:T(8,128)(2,1)} %fusion.23), channel_id=1, source_target_pairs={{0,1},{1,0},{2,3},{3,2},{4,5},{5,4},{6,7},{7,6},{8,9},{9,8},{10,11... | collective-permute-start | bytes 1548296 | tf_op jit(solution)/shard_map/ppermute | solution.py:73
  120.6 15.3 %collective-permute-start = (bf16[4,128,512]{2,1,0:T(8,128)(2,1)}, bf16[4,128,512]{2,1,0:T(8,128)(2,1)}, u32[]{:S(2)}, u32[]{:S(2)}) collective-permute-start(bf16[4,128,512]{2,1,0:T(8,128)(2,1)} %dynamic-slice_bitcast_fusion), channel_id=1, source_target_pairs={{0,1},{1,0},{2,3},{3,2},{4,5},{5,4},{6,7},{7,6},{8,9},{9,8},{10,11... | collective-permute-start | bytes 1572872 | tf_op jit(solution)/shard_map/ppermute | solution.py:116
  128.1 26.1 %all-to-all-start.3 = ((bf16[64,8,512]{2,1,0:T(8,128)(2,1)}), bf16[64,8,512]{2,1,0:T(8,128)(2,1)}, u32[]{:S(2)}, u32[]{:S(2)}) async-start(bf16[64,8,512]{2,1,0:T(8,128)(2,1)} %fusion.1), calls=%async_computation.3 | async-start | bytes 1048576 | tf_op jit(solution)/shard_map/all_to_all | solution.py:18
  135.9 10.9 %copy-start.1 = (s32[512,1]{0,1:T(1,128)S(1)}, s32[512,1]{0,1:T(1,128)}, u32[]{:S(2)}) copy-start(s32[512,1]{0,1:T(1,128)} %param.6) | copy-start | bytes 6148
  137.7 9.1 %collective-permute-start.4 = (bf16[128,504]{0,1:T(8,128)(2,1)S(1)}, bf16[128,504]{0,1:T(8,128)(2,1)S(1)}, u32[]{:S(2)}, u32[]{:S(2)}) collective-permute-start(bf16[128,504]{0,1:T(8,128)(2,1)S(1)} %get-tuple-element.9), channel_id=1, source_target_pairs={{0,6},{2,0},{4,2},{6,4},{1,7},{3,1},{5,3},{7,5},{8,14},{10,8},{12,... | collective-permute-start | bytes 387080 | tf_op jit(solution)/shard_map/ppermute | solution.py:131
  142.3 7.9 %collective-permute-start.3 = (bf16[128,504]{0,1:T(8,128)(2,1)S(1)}, bf16[128,504]{0,1:T(8,128)(2,1)S(1)}, u32[]{:S(2)}, u32[]{:S(2)}) collective-permute-start(bf16[128,504]{0,1:T(8,128)(2,1)S(1)} %get-tuple-element.8), channel_id=1, source_target_pairs={{0,4},{2,6},{4,0},{6,2},{1,5},{3,7},{5,1},{7,3},{8,12},{10,14},{12... | collective-permute-start | bytes 387080 | tf_op jit(solution)/shard_map/ppermute | solution.py:131
  144.8 8.6 %collective-permute-start.2 = (bf16[128,504]{0,1:T(8,128)(2,1)S(1)}, bf16[128,504]{0,1:T(8,128)(2,1)S(1)}, u32[]{:S(2)}, u32[]{:S(2)}) collective-permute-start(bf16[128,504]{0,1:T(8,128)(2,1)S(1)} %get-tuple-element.7), channel_id=1, source_target_pairs={{0,2},{2,4},{4,6},{6,0},{1,3},{3,5},{5,7},{7,1},{8,10},{10,12},{12... | collective-permute-start | bytes 387080 | tf_op jit(solution)/shard_map/ppermute | solution.py:131

commit v6 on v5

v6 whole, which is shorter than its diff:
```python
import jax
import jax.numpy as jnp
from jax import lax
from jax.experimental.layout import Layout, with_layout_constraint
from jax.experimental import pallas as pl
from jax.experimental.pallas import tpu as pltpu
from jax.sharding import Mesh
from jax.sharding import PartitionSpec as P

f32, bf16 = jnp.float32, jnp.bfloat16


def row_major(array):
    return with_layout_constraint(array, Layout(major_to_minor=tuple(range(array.ndim))))


FIELD = ("z1", "z0", "y1", "y0")
NEAR, FAR = ("z0", "y0"), ("z1", "y1")


def exchange(blocks, axes=FIELD):
    return lax.all_to_all(blocks, axes, split_axis=0, concat_axis=0, tiled=True)


def grad_kernel(place_ref, grad_ref, own_ref, turned_ref):
    turned_ref[...] = grad_ref[...].astype(f32).T
    rows = own_ref.shape[0]
    start = pl.multiple_of(place_ref[1] * rows, rows)
    own_ref[...] = turned_ref[pl.ds(start, rows), :].astype(bf16)


def own_columns(grad_act, shard, place, units, shard_units):
    samples = grad_act.shape[0]
    return pl.pallas_call(
        grad_kernel,
        grid_spec=pltpu.PrefetchScalarGridSpec(
            num_scalar_prefetch=1,
            grid=(1,),
            in_specs=[pl.BlockSpec((samples, shard_units), lambda i, place: (0, place[0]))],
            out_specs=pl.BlockSpec((units, samples), lambda i, place: (0, 0)),
            scratch_shapes=[pltpu.VMEM((shard_units, samples), f32)],
        ),
        out_shape=jax.ShapeDtypeStruct((units, samples), bf16),
        name="owngrad",
    )(jnp.stack([shard, place]).astype(jnp.int32), grad_act)


def body(pooled, counts, w_pairs, bias_terms, grad_act):
    sample_rows = pooled.shape[0]
    fields = lax.axis_size(FIELD)
    depth = pooled.shape[2] // fields
    half = depth // 2
    hidden_units = grad_act.shape[1]
    pair_count = w_pairs.shape[1]
    own_units = hidden_units // fields
    my_field = lax.axis_index(FIELD)

    embedded = pooled.reshape(sample_rows, fields, depth).transpose(1, 2, 0)
    partner = jnp.arange(fields, dtype=jnp.int32)[:, None, None]
    upper = partner < my_field
    mine = jnp.where(upper, embedded[:, half:], embedded[:, :half])
    outbound = jnp.where(upper, embedded[:, :half], embedded[:, half:])
    received = exchange(outbound)
    shard = jnp.concatenate([w_pairs[0], bias_terms[None, :]], 0).T
    weight_turned = row_major(
        lax.all_gather(row_major(shard), ("x", "core"), axis=0, tiled=True)
    )

    received_wide, mine_wide = received.astype(f32), mine.astype(f32)
    products = (mine_wide * received_wide).astype(bf16)
    slot = jnp.arange(fields - 1, dtype=jnp.int32)[:, None, None]
    pair_rows = jnp.where(slot >= my_field, products[1:], products[:-1])
    pair_rows = pair_rows.reshape(pair_count, sample_rows)

    biased_rows = jnp.concatenate([pair_rows, jnp.zeros((1, sample_rows), bf16)], 0)
    partial_hidden = jnp.dot(weight_turned, biased_rows, preferred_element_type=f32)
    partial_hidden = row_major(partial_hidden.astype(bf16))
    near, far = lax.axis_size(NEAR), lax.axis_size(FAR)
    near_shares = exchange(partial_hidden.reshape(near, -1, sample_rows), NEAR)
    near_sum = jnp.sum(near_shares.astype(f32), 0).astype(bf16)
    shares = exchange(near_sum.reshape(far, own_units, sample_rows), FAR)
    other_rows = lax.ppermute(pair_rows, "core", [(0, 1), (1, 0)])

    cores, chips = lax.axis_size("core"), lax.axis_size("x")
    my_core, my_chip = lax.axis_index("core"), lax.axis_index("x")
    shard_units = hidden_units // (cores * chips)
    own_start = (lax.axis_index(NEAR) * far + lax.axis_index(FAR)) * own_units
    own_bias = lax.dynamic_slice(weight_turned, (own_start, pair_count), (own_units, 1))
    own_bias = lax.optimization_barrier(own_bias.astype(f32))
    own_grad = own_columns(
        grad_act,
        own_start // shard_units,
        own_start % shard_units // own_units,
        own_units,
        shard_units,
    )
    own_grad = lax.optimization_barrier(own_grad.astype(f32))
    slot_row = (jnp.arange(fields * half, dtype=jnp.int32) // half)[:, None]
    weight_pairs = weight_turned[:, :pair_count].T
    below = jnp.pad(weight_pairs, ((0, half), (0, 0)))
    above = jnp.pad(weight_pairs, ((half, 0), (0, 0)))
    weight_rows = lax.optimization_barrier(
        row_major(
            jnp.where(slot_row < my_field, below, jnp.where(slot_row > my_field, above, 0))
        )
    )

    preact = jnp.sum(shares.astype(f32), 0) + own_bias
    gate_value = jax.nn.sigmoid(preact)
    own_slope = (
        own_grad * gate_value * (1.0 + preact * (1.0 - gate_value))
    ).astype(bf16)
    far_slope = exchange(
        jnp.broadcast_to(own_slope[None], (far, own_units, sample_rows)), FAR
    ).reshape(1, far * own_units, sample_rows)
    slope_turned = exchange(
        jnp.broadcast_to(far_slope, (near, far * own_units, sample_rows)), NEAR
    ).reshape(hidden_units, sample_rows)

    pair_grad = lax.optimization_barrier(
        jnp.dot(weight_rows, slope_turned, preferred_element_type=f32)
    )
    pair_grad = pair_grad.reshape(fields, half, sample_rows)
    outgoing = (pair_grad * mine_wide).astype(bf16)
    returned = exchange(outgoing).astype(f32)

    halves = slope_turned.reshape(chips, cores, shard_units, sample_rows)
    kept = lax.dynamic_index_in_dim(halves, my_core, 1, keepdims=False)
    sent = lax.dynamic_index_in_dim(halves, 1 - my_core, 1, keepdims=False)
    got = lax.ppermute(sent, "core", [(0, 1), (1, 0)])
    chip_sum = lax.dot_general(
        kept, pair_rows, (((2,), (1,)), ((), ())), preferred_element_type=f32
    )
    chip_sum = chip_sum + lax.dot_general(
        got, other_rows, (((2,), (1,)), ((), ())), preferred_element_type=f32
    )
    blocks = [
        lax.dynamic_index_in_dim(chip_sum, (my_chip + step) % chips, 0, keepdims=False)
        for step in range(chips)
    ]
    weight_total, *blocks = lax.optimization_barrier(
        (blocks[0], *[block.astype(bf16) for block in blocks[1:]])
    )
    for step, block in enumerate(blocks, 1):
        chip_got = lax.ppermute(
            block, "x", [(i, (i + step) % chips) for i in range(chips)]
        )
        weight_total = weight_total + chip_got.astype(f32)

    local = pair_grad * received_wide
    full = jnp.concatenate(
        [jnp.where(upper, returned, local), jnp.where(upper, local, returned)], 1
    )
    full = full / jnp.sqrt(counts[:, 0].astype(f32))[None, None, :]
    turned = row_major(full.astype(bf16).reshape(fields * depth, sample_rows))
    entry_grad = turned.T[:, None, :]
    return entry_grad, weight_total.T[None]


def solution(mesh):
    split = Mesh(
        mesh.devices.reshape(4, 2, 4, 2, mesh.shape["batch"] // 2, 2), (*FIELD, "x", "core")
    )
    batch = ("x", "core")
    in_specs = (
        P(batch, FIELD, None),
        P(batch, FIELD),
        P(FIELD, None, batch),
        P(batch),
        P(batch, None),
    )
    out_specs = (P(batch, FIELD, None), P(FIELD, None, batch))
    return jax.shard_map(body, mesh=split, in_specs=in_specs, out_specs=out_specs, check_vma=False)
```

time: 158 us -> 158 us (level)
  the two profiles are of different devices: /device:TPU:1 before, /device:TPU:10 now
where the time goes in v6:
time: 158 us; the launch traced here: 157 us
  starting transfers between devices  52.7 us (33%)
  blocking collectives  46.8 us (30%)
  waiting for transfers between devices  26.3 us (17%)
  other arithmetic  12.6 us (8%)
  local copies, waits for them, and re-layouts  7.63 us (5%)
  matrix products  7.19 us (5%)
  Pallas kernels  2.28 us (1%)
    all_to_all x4, starting transfers between devices, exchange(): return lax.all_to_all(blocks, axes, split_axis=0, concat_axis=0, tiled=True)  38.5 us
    all_to_all x2, blocking collectives, exchange(): return lax.all_to_all(blocks, axes, split_axis=0, concat_axis=0, tiled=True)  32.9 us
    all_to_all x4, waiting for transfers between devices, exchange(): return lax.all_to_all(blocks, axes, split_axis=0, concat_axis=0, tiled=True)  23.4 us
    all_gather x1, blocking collectives, body(): lax.all_gather(row_major(shard), ('x', 'core'), axis=0, tiled=True)  13.9 us
    ppermute x3, starting transfers between devices, body(): lax.ppermute(block, 'x', [(i, (i + step) % chips) for i in range(chips)])  10.4 us
    unnamed x10, local copies, waits for them, and re-layouts  4.4 us
  transfers between devices with their start and end apart: 9, of which 6 were waited for; matrix products, arithmetic and copies ran while one was open for 10% of the time, Pallas kernels for 1%

profile of v6, /device:TPU:10, one launch (start us, length us, event | category | flops | bytes accessed | tf_op | source)
XLA Modules:
  0.0 156.5 jit_solution(10052274639824124411)
XLA Ops:
  0.7 0.0 copy-start
  0.7 1.5 copy.20
  2.2 0.9 broadcast_select_fusion
  3.2 16.6 %all-to-all-start = ((bf16[64,8,512]{2,1,0:T(8,128)(2,1)}), bf16[64,8,512]{2,1,0:T(8,128)(2,1)S(1)}, u32[]{:S(2)}, u32[]{:S(2)}) async-start(bf16[64,8,512]{2,1,0:T(8,128)(2,1)} %broadcast_select_fusion), calls=%async_computation | async-start | bytes 1048576 | tf_op jit(solution)/shard_map/all_to_all | solution.py:22
  19.8 0.1 copy.17
  19.9 0.1 copy.18
  20.1 0.1 maximum_bitcast_fusion
  20.2 13.9 %all_gather.3 = bf16[1024,505]{1,0:T(8,128)(2,1)S(1)} all-gather(bf16[128,505]{1,0:T(8,128)(2,1)S(1)} %maximum_bitcast_fusion), channel_id=1, replica_groups=mesh['z1'=4,'z0'=2,'y1'=4,'y0'=2,'x'=4,'core'=2] {'x','core'}, dimensions={0}, use_global_device_ids=true | all-gather | bytes 1163520 | tf_op jit(solution)/shard_map/all_gather | solution.py:66
  34.1 5.1 %all-to-all-done = bf16[64,8,512]{2,1,0:T(8,128)(2,1)S(1)} async-done(((bf16[64,8,512]{2,1,0:T(8,128)(2,1)}), bf16[64,8,512]{2,1,0:T(8,128)(2,1)S(1)}, u32[]{:S(2)}, u32[]{:S(2)}) %all-to-all-start) | async-done | bytes 524320 | tf_op jit(solution)/shard_map/all_to_all | solution.py:22
  39.2 0.3 fusion.2
  39.4 0.9 fusion.19
  40.4 1.7 %convolution_convert_fusion = bf16[1024,512]{1,0:T(8,128)(2,1)S(1)} fusion(bf16[1024,505]{1,0:T(8,128)(2,1)S(1)} %all_gather.3, bf16[504,512]{1,0:T(8,128)(2,1)} %fusion.19), kind=kOutput, calls=%fused_computation.3 | convolution fusion | flops 530055168 | bytes 2598912 | tf_op jit(solution)/shard_map/dot_general | solution.py:76
  42.1 14.7 %all_to_all.30 = bf16[4,256,512]{2,1,0:T(8,128)(2,1)} all-to-all(bf16[4,256,512]{2,1,0:T(8,128)(2,1)S(1)} %bitcast.68), channel_id=1, replica_groups=mesh['z1'=4,'z0'=2,'y1'=4,'y0'=2,'x'=4,'core'=2] {'z0','y0'}, dimensions={0} | all-to-all | bytes 2097152 | tf_op jit(solution)/shard_map/all_to_all | solution.py:22
  56.8 2.2 %reduce_sum.21 = bf16[256,512]{1,0:T(8,128)(2,1)} reduce(bf16[4,256,512]{2,1,0:T(8,128)(2,1)} %all_to_all.30, bf16[]{:T(256)} %constant.123.clone.1), dimensions={0}, to_apply=%region_0.1 | reduce | flops 393216 | bytes 1310722 | tf_op jit(solution)/shard_map/reduce_sum | solution.py:80
  58.9 9.5 %all-to-all-start.2 = ((bf16[16,16,512]{2,1,0:T(8,128)(2,1)}), bf16[16,16,512]{2,1,0:T(8,128)(2,1)S(1)}, u32[]{:S(2)}, u32[]{:S(2)}) async-start(bf16[16,16,512]{2,1,0:T(8,128)(2,1)} %bitcast.11), calls=%async_computation.2 | async-start | bytes 524288 | tf_op jit(solution)/shard_map/all_to_all | solution.py:22
  68.4 0.7 pad_add_fusion.place_ref
  69.1 2.3 %owngrad.1 = bf16[16,512]{1,0:T(8,128)(2,1)} custom-call(s32[2]{0:T(128)} %pad_add_fusion.place_ref, bf16[512,1024]{1,0:T(8,128)(2,1)} %grad_ref.1), custom_call_target="tpu_custom_call" | custom-call | tf_op jit(solution)/shard_map/owngrad/pallas_call | solution.py:34
  71.4 0.7 convert_element_type.77
  72.1 0.1 dynamic-slice_convert_fusion.3
  72.2 0.1 reduce.1
  72.3 9.7 %all-to-all-done.2 = bf16[16,16,512]{2,1,0:T(8,128)(2,1)S(1)} async-done(((bf16[16,16,512]{2,1,0:T(8,128)(2,1)}), bf16[16,16,512]{2,1,0:T(8,128)(2,1)S(1)}, u32[]{:S(2)}, u32[]{:S(2)}) %all-to-all-start.2) | async-done | bytes 262176 | tf_op jit(solution)/shard_map/all_to_all | solution.py:22
  82.0 0.1 multiply_convert_fusion
  82.2 18.3 %all_to_all.31 = bf16[16,16,512]{2,1,0:T(8,128)(2,1)S(1)} all-to-all(bf16[16,16,512]{2,1,0:T(8,128)(2,1)S(1)} %broadcast_in_dim.81), channel_id=1, replica_groups=mesh['z1'=4,'z0'=2,'y1'=4,'y0'=2,'x'=4,'core'=2] {'z1','y1'}, dimensions={0} | all-to-all | bytes 524288 | tf_op jit(solution)/shard_map/all_to_all | solution.py:22
  100.4 1.1 broadcast_in_dim.83
  101.5 5.0 %all-to-all-start.4 = ((bf16[4,256,512]{2,1,0:T(8,128)(2,1)}), bf16[4,256,512]{2,1,0:T(8,128)(2,1)}, u32[]{:S(2)}, u32[]{:S(2)}) async-start(bf16[4,256,512]{2,1,0:T(8,128)(2,1)} %broadcast_in_dim.83), calls=%async_computation.4 | async-start | bytes 2097152 | tf_op jit(solution)/shard_map/all_to_all | solution.py:22
  106.5 1.4 copy.22
  107.9 2.9 %select_select_fusion = bf16[512,1024]{1,0:T(8,128)(2,1)} fusion(bf16[504,1024]{1,0:T(8,128)(2,1)} %bitcast.66, pred[512]{0:T(512)(128)(4,1)S(1)} %get-tuple-element.21, pred[512]{0:T(512)(128)(4,1)S(1)} %get-tuple-element.22), kind=kLoop, calls=%fused_computation.12 | loop fusion | flops 1048576 | bytes 2081792 | tf_op jit(solution)/shard_map/jit(_where)/select_n | solution.py:104
  110.8 1.9 %collective-permute-start.1 = (bf16[504,512]{1,0:T(8,128)(2,1)}, bf16[504,512]{1,0:T(8,128)(2,1)}, u32[]{:S(2)}, u32[]{:S(2)}) collective-permute-start(bf16[504,512]{1,0:T(8,128)(2,1)} %fusion.19), channel_id=1, source_target_pairs={{0,1},{1,0},{2,3},{3,2},{4,5},{5,4},{6,7},{7,6},{8,9},{9,8},{10,11... | collective-permute-start | bytes 1548296 | tf_op jit(solution)/shard_map/ppermute | solution.py:82
  112.7 6.3 %all-to-all-done.4 = bf16[4,256,512]{2,1,0:T(8,128)(2,1)} async-done(((bf16[4,256,512]{2,1,0:T(8,128)(2,1)}), bf16[4,256,512]{2,1,0:T(8,128)(2,1)}, u32[]{:S(2)}, u32[]{:S(2)}) %all-to-all-start.4) | async-done | bytes 1048608 | tf_op jit(solution)/shard_map/all_to_all | solution.py:22
  119.0 1.9 %dynamic-slice_bitcast_fusion = bf16[4,128,512]{2,1,0:T(8,128)(2,1)} fusion(bf16[4,2,128,512]{3,2,1,0:T(8,128)(2,1)} %bitcast.19, s32[]{:T(128)S(6)} %select_n.106), kind=kLoop, calls=%fused_computation.15 | loop fusion | bytes 1048580 | tf_op jit(solution)/shard_map/jit(dynamic_index_in_dim)/squeeze | solution.py:129
  120.9 1.9 %collective-permute-start = (bf16[4,128,512]{2,1,0:T(8,128)(2,1)}, bf16[4,128,512]{2,1,0:T(8,128)(2,1)}, u32[]{:S(2)}, u32[]{:S(2)}) collective-permute-start(bf16[4,128,512]{2,1,0:T(8,128)(2,1)} %dynamic-slice_bitcast_fusion), channel_id=1, source_target_pairs={{0,1},{1,0},{2,3},{3,2},{4,5},{5,4},{6,7},{7,6},{8,9},{9,8},{10,11... | collective-permute-start | bytes 1572872 | tf_op jit(solution)/shard_map/ppermute | solution.py:130
  122.8 2.2 %fusion.20 = f32[512,512]{1,0:T(8,128)S(1)} fusion(bf16[512,1024]{1,0:T(8,128)(2,1)} %select_select_fusion, bf16[1024,512]{1,0:T(8,128)(2,1)} %bitcast.13), kind=kOutput, calls=%fused_computation.51 | convolution fusion | flops 536870912 | bytes 3145728 | tf_op jit(solution)/shard_map/dot_general | solution.py:121
  125.1 1.0 fusion.1
  126.1 7.4 %all-to-all-start.5 = ((bf16[64,8,512]{2,1,0:T(8,128)(2,1)}), bf16[64,8,512]{2,1,0:T(8,128)(2,1)}, u32[]{:S(2)}, u32[]{:S(2)}) async-start(bf16[64,8,512]{2,1,0:T(8,128)(2,1)} %fusion.1), calls=%async_computation.5 | async-start | bytes 1048576 | tf_op jit(solution)/shard_map/all_to_all | solution.py:22
  133.5 1.5 fusion.3
  135.1 1.7 %convolution_add_fusion = f32[4,128,504]{1,2,0:T(8,128)S(1)} fusion(f32[4,128,504]{1,2,0:T(8,128)S(1)} %fusion.3, bf16[4,128,512]{2,1,0:T(8,128)(2,1)} %collective-permute-done, bf16[504,512]{1,0:T(8,128)(2,1)} %collective-permute-done.1), kind=kOutput, calls=%fused_computation.4 | convolution fusion | flops 264499200 | bytes 3104768 | tf_op jit(solution)/shard_map/dot_general | solution.py:134
  136.8 0.1 fusion.11
  136.9 1.9 %collective-permute-start.2 = (bf16[128,504]{0,1:T(8,128)(2,1)S(1)}, bf16[128,504]{0,1:T(8,128)(2,1)S(1)}, u32[]{:S(2)}, u32[]{:S(2)}) collective-permute-start(bf16[128,504]{0,1:T(8,128)(2,1)S(1)} %get-tuple-element.7), channel_id=1, source_target_pairs={{0,2},{2,4},{4,6},{6,0},{1,3},{3,5},{5,7},{7,1},{8,10},{10,12},{12... | collective-permute-start | bytes 387080 | tf_op jit(solution)/shard_map/ppermute | solution.py:145
  138.8 4.0 %collective-permute-start.3 = (bf16[128,504]{0,1:T(8,128)(2,1)S(1)}, bf16[128,504]{0,1:T(8,128)(2,1)S(1)}, u32[]{:S(2)}, u32[]{:S(2)}) collective-permute-start(bf16[128,504]{0,1:T(8,128)(2,1)S(1)} %get-tuple-element.8), channel_id=1, source_target_pairs={{0,4},{2,6},{4,0},{6,2},{1,5},{3,7},{5,1},{7,3},{8,12},{10,14},{12... | collective-permute-start | bytes 387080 | tf_op jit(solution)/shard_map/ppermute | solution.py:145
  142.8 4.5 %collective-permute-start.4 = (bf16[128,504]{0,1:T(8,128)(2,1)S(1)}, bf16[128,504]{0,1:T(8,128)(2,1)S(1)}, u32[]{:S(2)}, u32[]{:S(2)}) collective-permute-start(bf16[128,504]{0,1:T(8,128)(2,1)S(1)} %get-tuple-element.9), channel_id=1, source_target_pairs={{0,6},{2,0},{4,2},{6,4},{1,7},{3,1},{5,3},{7,5},{8,14},{10,8},{12,... | collective-permute-start | bytes 387080 | tf_op jit(solution)/shard_map/ppermute | solution.py:145
  147.4 0.2 collective-permute-done.3
  147.6 2.7 %collective-permute-done.4 = bf16[128,504]{0,1:T(8,128)(2,1)S(1)} collective-permute-done((bf16[128,504]{0,1:T(8,128)(2,1)S(1)}, bf16[128,504]{0,1:T(8,128)(2,1)S(1)}, u32[]{:S(2)}, u32[]{:S(2)}) %collective-permute-start.4) | collective-permute-done | bytes 129056 | tf_op jit(solution)/shard_map/ppermute | solution.py:145
  150.3 0.8 add_bitcast_fusion
  151.0 2.3 %all-to-all-done.5 = bf16[64,8,512]{2,1,0:T(8,128)(2,1)} async-done(((bf16[64,8,512]{2,1,0:T(8,128)(2,1)}), bf16[64,8,512]{2,1,0:T(8,128)(2,1)}, u32[]{:S(2)}, u32[]{:S(2)}) %all-to-all-start.5) | async-done | bytes 524320 | tf_op jit(solution)/shard_map/all_to_all | solution.py:22
  153.4 1.3 convert_select_fusion.1
  154.6 0.2 pad_maximum_fusion
  154.9 0.3 fusion
  155.2 1.3 copy.21
  (15 shorter events, 0.1 us)
Async XLA Ops:
  0.7 19.1 %copy-start = (bf16[1,504,128]{2,1,0:T(8,128)(2,1)S(1)}, bf16[1,504,128]{2,1,0:T(8,128)(2,1)}, u32[]{:S(2)}) copy-start(bf16[1,504,128]{2,1,0:T(8,128)(2,1)} %param.7) | copy-start | bytes 387076
  0.7 19.3 %copy-start.2 = (bf16[128]{0:T(256)(128)(2,1)S(1)}, bf16[128]{0:T(256)(128)(2,1)}, u32[]{:S(2)}) copy-start(bf16[128]{0:T(256)(128)(2,1)} %param.8) | copy-start | bytes 772
  3.2 36.0 %all-to-all-start = ((bf16[64,8,512]{2,1,0:T(8,128)(2,1)}), bf16[64,8,512]{2,1,0:T(8,128)(2,1)S(1)}, u32[]{:S(2)}, u32[]{:S(2)}) async-start(bf16[64,8,512]{2,1,0:T(8,128)(2,1)} %broadcast_select_fusion), calls=%async_computation | async-start | bytes 1048576 | tf_op jit(solution)/shard_map/all_to_all | solution.py:22
  58.9 23.1 %all-to-all-start.2 = ((bf16[16,16,512]{2,1,0:T(8,128)(2,1)}), bf16[16,16,512]{2,1,0:T(8,128)(2,1)S(1)}, u32[]{:S(2)}, u32[]{:S(2)}) async-start(bf16[16,16,512]{2,1,0:T(8,128)(2,1)} %bitcast.11), calls=%async_computation.2 | async-start | bytes 524288 | tf_op jit(solution)/shard_map/all_to_all | solution.py:22
  101.5 17.5 %all-to-all-start.4 = ((bf16[4,256,512]{2,1,0:T(8,128)(2,1)}), bf16[4,256,512]{2,1,0:T(8,128)(2,1)}, u32[]{:S(2)}, u32[]{:S(2)}) async-start(bf16[4,256,512]{2,1,0:T(8,128)(2,1)} %broadcast_in_dim.83), calls=%async_computation.4 | async-start | bytes 2097152 | tf_op jit(solution)/shard_map/all_to_all | solution.py:22
  110.8 24.3 %collective-permute-start.1 = (bf16[504,512]{1,0:T(8,128)(2,1)}, bf16[504,512]{1,0:T(8,128)(2,1)}, u32[]{:S(2)}, u32[]{:S(2)}) collective-permute-start(bf16[504,512]{1,0:T(8,128)(2,1)} %fusion.19), channel_id=1, source_target_pairs={{0,1},{1,0},{2,3},{3,2},{4,5},{5,4},{6,7},{7,6},{8,9},{9,8},{10,11... | collective-permute-start | bytes 1548296 | tf_op jit(solution)/shard_map/ppermute | solution.py:82
  120.9 14.2 %collective-permute-start = (bf16[4,128,512]{2,1,0:T(8,128)(2,1)}, bf16[4,128,512]{2,1,0:T(8,128)(2,1)}, u32[]{:S(2)}, u32[]{:S(2)}) collective-permute-start(bf16[4,128,512]{2,1,0:T(8,128)(2,1)} %dynamic-slice_bitcast_fusion), channel_id=1, source_target_pairs={{0,1},{1,0},{2,3},{3,2},{4,5},{5,4},{6,7},{7,6},{8,9},{9,8},{10,11... | collective-permute-start | bytes 1572872 | tf_op jit(solution)/shard_map/ppermute | solution.py:130
  126.1 27.3 %all-to-all-start.5 = ((bf16[64,8,512]{2,1,0:T(8,128)(2,1)}), bf16[64,8,512]{2,1,0:T(8,128)(2,1)}, u32[]{:S(2)}, u32[]{:S(2)}) async-start(bf16[64,8,512]{2,1,0:T(8,128)(2,1)} %fusion.1), calls=%async_computation.5 | async-start | bytes 1048576 | tf_op jit(solution)/shard_map/all_to_all | solution.py:22
  135.1 12.3 %copy-start.1 = (s32[512,1]{0,1:T(1,128)S(1)}, s32[512,1]{0,1:T(1,128)}, u32[]{:S(2)}) copy-start(s32[512,1]{0,1:T(1,128)} %param.6) | copy-start | bytes 6148
  136.9 10.5 %collective-permute-start.2 = (bf16[128,504]{0,1:T(8,128)(2,1)S(1)}, bf16[128,504]{0,1:T(8,128)(2,1)S(1)}, u32[]{:S(2)}, u32[]{:S(2)}) collective-permute-start(bf16[128,504]{0,1:T(8,128)(2,1)S(1)} %get-tuple-element.7), channel_id=1, source_target_pairs={{0,2},{2,4},{4,6},{6,0},{1,3},{3,5},{5,7},{7,1},{8,10},{10,12},{12... | collective-permute-start | bytes 387080 | tf_op jit(solution)/shard_map/ppermute | solution.py:145
  138.8 8.8 %collective-permute-start.3 = (bf16[128,504]{0,1:T(8,128)(2,1)S(1)}, bf16[128,504]{0,1:T(8,128)(2,1)S(1)}, u32[]{:S(2)}, u32[]{:S(2)}) collective-permute-start(bf16[128,504]{0,1:T(8,128)(2,1)S(1)} %get-tuple-element.8), channel_id=1, source_target_pairs={{0,4},{2,6},{4,0},{6,2},{1,5},{3,7},{5,1},{7,3},{8,12},{10,14},{12... | collective-permute-start | bytes 387080 | tf_op jit(solution)/shard_map/ppermute | solution.py:145
  142.8 7.5 %collective-permute-start.4 = (bf16[128,504]{0,1:T(8,128)(2,1)S(1)}, bf16[128,504]{0,1:T(8,128)(2,1)S(1)}, u32[]{:S(2)}, u32[]{:S(2)}) collective-permute-start(bf16[128,504]{0,1:T(8,128)(2,1)S(1)} %get-tuple-element.9), channel_id=1, source_target_pairs={{0,6},{2,0},{4,2},{6,4},{1,7},{3,1},{5,3},{7,5},{8,14},{10,8},{12,... | collective-permute-start | bytes 387080 | tf_op jit(solution)/shard_map/ppermute | solution.py:145

commit v7 on v5

--- a/solution.py
+++ b/solution.py
@@ -21,7 +21,8 @@
 def grad_kernel(place_ref, grad_ref, own_ref, turned_ref):
     turned_ref[...] = grad_ref[...].astype(f32).T
     rows = own_ref.shape[0]
-    own_ref[...] = turned_ref[pl.ds(pl.multiple_of(place_ref[1] * rows, rows), rows), :]
+    start = pl.multiple_of(place_ref[1] * rows, rows)
+    own_ref[...] = turned_ref[pl.ds(start, rows), :].astype(bf16)
 
 
 def own_columns(grad_act, shard, place, units, shard_units):
@@ -35,7 +36,7 @@
             out_specs=pl.BlockSpec((units, samples), lambda i, place: (0, 0)),
             scratch_shapes=[pltpu.VMEM((shard_units, samples), f32)],
         ),
-        out_shape=jax.ShapeDtypeStruct((units, samples), f32),
+        out_shape=jax.ShapeDtypeStruct((units, samples), bf16),
         name="owngrad",
     )(jnp.stack([shard, place]).astype(jnp.int32), grad_act)
 
@@ -56,9 +57,8 @@
     mine = jnp.where(upper, embedded[:, half:], embedded[:, :half])
     outbound = jnp.where(upper, embedded[:, :half], embedded[:, half:])
     received = exchange(outbound)
-    chip_weights = lax.all_gather(row_major(w_pairs[0].T), "x", axis=0, tiled=True)
     weight_turned = row_major(
-        lax.all_gather(row_major(chip_weights), "core", axis=0, tiled=True)
+        lax.all_gather(row_major(w_pairs[0].T), ("x", "core"), axis=0, tiled=True)
     )
 
     received_wide, mine_wide = received.astype(f32), mine.astype(f32)
@@ -76,14 +76,16 @@
     cores, chips = lax.axis_size("core"), lax.axis_size("x")
     my_core, my_chip = lax.axis_index("core"), lax.axis_index("x")
     shard_units = hidden_units // (cores * chips)
-    own_place = my_field * own_units
-    own_shard = own_place // shard_units
-    own_shard = (own_shard % chips) * cores + own_shard // chips
-    own_start = own_shard * shard_units + own_place % shard_units
+    own_start = my_field * own_units
     own_bias = lax.dynamic_slice(bias_wide.reshape(-1, 1), (own_start, 0), (own_units, 1))
     own_grad = own_columns(
-        grad_act, own_shard, own_place % shard_units // own_units, own_units, shard_units
+        grad_act,
+        own_start // shard_units,
+        own_start % shard_units // own_units,
+        own_units,
+        shard_units,
     )
+    own_grad = lax.optimization_barrier(own_grad.astype(f32))
     slot_row = (jnp.arange(fields * half, dtype=jnp.int32) // half)[:, None]
     weight_pairs = weight_turned.T
     below = jnp.pad(weight_pairs, ((0, half), (0, 0)))
@@ -110,9 +112,9 @@
     outgoing = (pair_grad * mine_wide).astype(bf16)
     returned = exchange(outgoing).astype(f32)
 
-    halves = slope_turned.reshape(cores, chips, shard_units, sample_rows)
-    kept = lax.dynamic_index_in_dim(halves, my_core, 0, keepdims=False)
-    sent = lax.dynamic_index_in_dim(halves, 1 - my_core, 0, keepdims=False)
+    halves = slope_turned.reshape(chips, cores, shard_units, sample_rows)
+    kept = lax.dynamic_index_in_dim(halves, my_core, 1, keepdims=False)
+    sent = lax.dynamic_index_in_dim(halves, 1 - my_core, 1, keepdims=False)
     got = lax.ppermute(sent, "core", [(0, 1), (1, 0)])
     chip_sum = lax.dot_general(
         kept, pair_rows, (((2,), (1,)), ((), ())), preferred_element_type=f32

time: 158 us -> 156 us (0.987)
  blocking collectives: 27.5 us -> 25.4 us
  waiting for transfers between devices: 37.8 us -> 39.9 us
  starting transfers between devices: 62.4 us -> 60.4 us
    all_to_all x4, waiting for transfers between devices: 31.2 us -> 33.2 us  [exchange(): lax.all_to_all(blocks, 'field', split_axis=0, concat_axis=0, tiled=True)]
    all_gather x2 -> x1, blocking collectives: 16.3 us -> 14.8 us  [body(): lax.all_gather(row_major(w_pairs[0].T), ('x', 'core'), axis=0, tiled=True)]
where the time goes in v7:
time: 156 us; the launch traced here: 155 us
  starting transfers between devices  60.4 us (39%)
  waiting for transfers between devices  39.9 us (26%)
  blocking collectives  25.4 us (16%)
  other arithmetic  11.7 us (8%)
  local copies, waits for them, and re-layouts  7.49 us (5%)
  matrix products  7.2 us (5%)
  Pallas kernels  2.28 us (1%)
    all_to_all x4, starting transfers between devices, exchange(): lax.all_to_all(blocks, 'field', split_axis=0, concat_axis=0, tiled=True)  41.7 us
    all_to_all x4, waiting for transfers between devices, exchange(): lax.all_to_all(blocks, 'field', split_axis=0, concat_axis=0, tiled=True)  33.2 us
    all_gather x1, blocking collectives, body(): lax.all_gather(row_major(w_pairs[0].T), ('x', 'core'), axis=0, tiled=True)  14.8 us
    all_gather x1, blocking collectives, body(): bias_wide = lax.all_gather(bias_terms, ('x', 'core'), axis=0, tiled=True)  10.6 us
    ppermute x3, starting transfers between devices, body(): lax.ppermute(block, 'x', [(i, (i + step) % chips) for i in range(chips)])  8.62 us
    ppermute x3, waiting for transfers between devices, body(): lax.ppermute(block, 'x', [(i, (i + step) % chips) for i in range(chips)])  6.76 us
    ppermute x1, starting transfers between devices, body(): got = lax.ppermute(sent, 'core', [(0, 1), (1, 0)])  6.45 us
    ppermute x1, starting transfers between devices, body(): other_rows = lax.ppermute(pair_rows, 'core', [(0, 1), (1, 0)])  3.64 us
  transfers between devices with their start and end apart: 9, of which 5 were waited for; matrix products, arithmetic and copies ran while one was open for 10% of the time, Pallas kernels for 1%

profile of v7, /device:TPU:1, one launch (start us, length us, event | category | flops | bytes accessed | tf_op | source)
XLA Modules:
  0.0 155.3 jit_solution(13256886807697722988)
XLA Ops:
  0.6 0.0 copy-start
  0.7 1.5 copy.17
  2.2 0.9 broadcast_select_fusion
  3.1 17.1 %all-to-all-start = ((bf16[64,8,512]{2,1,0:T(8,128)(2,1)}), bf16[64,8,512]{2,1,0:T(8,128)(2,1)S(1)}, u32[]{:S(2)}, u32[]{:S(2)}) async-start(bf16[64,8,512]{2,1,0:T(8,128)(2,1)} %broadcast_select_fusion), calls=%async_computation | async-start | bytes 1048576 | tf_op jit(solution)/shard_map/all_to_all | solution.py:18
  20.3 0.1 copy.15
  20.4 14.8 %all_gather.6 = bf16[1024,504]{1,0:T(8,128)(2,1)S(1)} all-gather(bf16[128,504]{1,0:T(8,128)(2,1)S(1)} %bitcast.69), channel_id=1, replica_groups=mesh['field'=64,'x'=4,'core'=2] {'x','core'}, dimensions={0}, use_global_device_ids=true | all-gather | bytes 1161216 | tf_op jit(solution)/shard_map/all_gather | solution.py:61
  35.2 2.4 %all-to-all-done = bf16[64,8,512]{2,1,0:T(8,128)(2,1)S(1)} async-done(((bf16[64,8,512]{2,1,0:T(8,128)(2,1)}), bf16[64,8,512]{2,1,0:T(8,128)(2,1)S(1)}, u32[]{:S(2)}, u32[]{:S(2)}) %all-to-all-start) | async-done | bytes 524320 | tf_op jit(solution)/shard_map/all_to_all | solution.py:18
  37.7 0.3 fusion.2
  38.0 1.8 %convolution_convert_fusion = bf16[512,1024]{0,1:T(8,128)(2,1)} fusion(bf16[1024,504]{1,0:T(8,128)(2,1)S(1)} %all_gather.6, bf16[64,8,512]{2,1,0:T(8,128)(2,1)S(1)} %fusion.2, pred[63]{0:T(512)(128)(4,1)S(1)} %iota_compare_fusion), kind=kOutput, calls=%fused_computation.4 | convolution fusion | flops 529264640 | bytes 3129856 | tf_op jit(solution)/shard_map/dot_general | solution.py:70
  39.7 10.4 %all-to-all-start.1 = ((bf16[64,16,512]{2,1,0:T(8,128)(2,1)}), bf16[64,16,512]{2,1,0:T(8,128)(2,1)}, u32[]{:S(2)}, u32[]{:S(2)}) async-start(bf16[64,16,512]{2,1,0:T(8,128)(2,1)} %bitcast.68), calls=%async_computation.1 | async-start | bytes 2097152 | tf_op jit(solution)/shard_map/all_to_all | solution.py:18
  50.1 0.7 pad_add_fusion.place_ref
  50.8 2.3 %owngrad.1 = bf16[16,512]{1,0:T(8,128)(2,1)} custom-call(s32[2]{0:T(128)} %pad_add_fusion.place_ref, bf16[512,1024]{1,0:T(8,128)(2,1)} %grad_ref.1), custom_call_target="tpu_custom_call" | custom-call | tf_op jit(solution)/shard_map/owngrad/pallas_call | solution.py:30
  53.1 0.7 convert_element_type.79
  53.8 10.6 %all-gather = bf16[8,1,128]{2,1,0:T(2,128)(2,1)S(1)} all-gather(bf16[1,1,128]{2,1,0:T(2,128)(2,1)S(1)} %bitcast.72), channel_id=1, replica_groups=mesh['field'=64,'x'=4,'core'=2] {'x','core'}, dimensions={0}, use_global_device_ids=true | all-gather | bytes 2304 | tf_op jit(solution)/shard_map/all_gather | solution.py:75
  64.5 0.1 dynamic-slice_convert_fusion.3
  64.6 13.6 %all-to-all-done.1 = bf16[64,16,512]{2,1,0:T(8,128)(2,1)} async-done(((bf16[64,16,512]{2,1,0:T(8,128)(2,1)}), bf16[64,16,512]{2,1,0:T(8,128)(2,1)}, u32[]{:S(2)}, u32[]{:S(2)}) %all-to-all-start.1) | async-done | bytes 1048608 | tf_op jit(solution)/shard_map/all_to_all | solution.py:18
  78.2 1.4 convert_reduce_fusion
  79.6 0.1 multiply_convert_fusion
  79.7 1.1 broadcast_in_dim.69
  80.8 7.8 %all-to-all-start.2 = ((bf16[64,16,512]{2,1,0:T(8,128)(2,1)}), bf16[64,16,512]{2,1,0:T(8,128)(2,1)}, u32[]{:S(2)}, u32[]{:S(2)}) async-start(bf16[64,16,512]{2,1,0:T(8,128)(2,1)} %broadcast_in_dim.69), calls=%async_computation.2 | async-start | bytes 2097152 | tf_op jit(solution)/shard_map/all_to_all | solution.py:18
  88.6 1.4 copy.16
  90.0 2.9 %select_select_fusion = bf16[512,1024]{1,0:T(8,128)(2,1)} fusion(bf16[504,1024]{1,0:T(8,128)(2,1)} %bitcast.67, pred[512]{0:T(512)(128)(4,1)S(1)} %get-tuple-element.21, pred[512]{0:T(512)(128)(4,1)S(1)} %get-tuple-element.22), kind=kLoop, calls=%fused_computation.13 | loop fusion | flops 1048576 | bytes 2081792 | tf_op jit(solution)/shard_map/jit(_where)/select_n | solution.py:95
  92.9 1.0 fusion.23
  93.8 3.6 %collective-permute-start.1 = (bf16[504,512]{1,0:T(8,128)(2,1)}, bf16[504,512]{1,0:T(8,128)(2,1)}, u32[]{:S(2)}, u32[]{:S(2)}) collective-permute-start(bf16[504,512]{1,0:T(8,128)(2,1)} %fusion.23), channel_id=1, source_target_pairs={{0,1},{1,0},{2,3},{3,2},{4,5},{5,4},{6,7},{7,6},{8,9},{9,8},{10,11... | collective-permute-start | bytes 1548296 | tf_op jit(solution)/shard_map/ppermute | solution.py:73
  97.5 17.1 %all-to-all-done.2 = bf16[64,16,512]{2,1,0:T(8,128)(2,1)} async-done(((bf16[64,16,512]{2,1,0:T(8,128)(2,1)}), bf16[64,16,512]{2,1,0:T(8,128)(2,1)}, u32[]{:S(2)}, u32[]{:S(2)}) %all-to-all-start.2) | async-done | bytes 1048608 | tf_op jit(solution)/shard_map/all_to_all | solution.py:18
  114.6 2.2 %fusion.18 = f32[512,512]{1,0:T(8,128)S(1)} fusion(bf16[512,1024]{1,0:T(8,128)(2,1)} %select_select_fusion, bf16[1024,512]{1,0:T(8,128)(2,1)} %bitcast.12), kind=kOutput, calls=%fused_computation.48 | convolution fusion | flops 536870912 | bytes 3145728 | tf_op jit(solution)/shard_map/dot_general | solution.py:109
  116.8 1.9 %dynamic-slice_bitcast_fusion = bf16[4,128,512]{2,1,0:T(8,128)(2,1)} fusion(bf16[4,2,128,512]{3,2,1,0:T(8,128)(2,1)} %bitcast.18, s32[]{:T(128)S(6)} %select_n.106), kind=kLoop, calls=%fused_computation.16 | loop fusion | bytes 1048580 | tf_op jit(solution)/shard_map/jit(dynamic_index_in_dim)/squeeze | solution.py:117
  118.7 6.5 %collective-permute-start = (bf16[4,128,512]{2,1,0:T(8,128)(2,1)}, bf16[4,128,512]{2,1,0:T(8,128)(2,1)}, u32[]{:S(2)}, u32[]{:S(2)}) collective-permute-start(bf16[4,128,512]{2,1,0:T(8,128)(2,1)} %dynamic-slice_bitcast_fusion), channel_id=1, source_target_pairs={{0,1},{1,0},{2,3},{3,2},{4,5},{5,4},{6,7},{7,6},{8,9},{9,8},{10,11... | collective-permute-start | bytes 1572872 | tf_op jit(solution)/shard_map/ppermute | solution.py:118
  125.2 1.0 fusion.1
  126.2 6.4 %all-to-all-start.3 = ((bf16[64,8,512]{2,1,0:T(8,128)(2,1)}), bf16[64,8,512]{2,1,0:T(8,128)(2,1)}, u32[]{:S(2)}, u32[]{:S(2)}) async-start(bf16[64,8,512]{2,1,0:T(8,128)(2,1)} %fusion.1), calls=%async_computation.3 | async-start | bytes 1048576 | tf_op jit(solution)/shard_map/all_to_all | solution.py:18
  132.6 1.5 fusion.3
  134.2 0.0 copy-start.1
  134.2 0.0 collective-permute-done.1
  134.2 0.0 collective-permute-done
  134.2 1.7 %convolution_add_fusion = f32[4,128,504]{1,2,0:T(8,128)S(1)} fusion(f32[4,128,504]{1,2,0:T(8,128)S(1)} %fusion.3, bf16[4,128,512]{2,1,0:T(8,128)(2,1)} %collective-permute-done, bf16[504,512]{1,0:T(8,128)(2,1)} %collective-permute-done.1), kind=kOutput, calls=%fused_computation.5 | convolution fusion | flops 264499200 | bytes 3104768 | tf_op jit(solution)/shard_map/dot_general | solution.py:122
  135.9 0.1 fusion.10
  136.0 4.2 %collective-permute-start.4 = (bf16[128,504]{0,1:T(8,128)(2,1)S(1)}, bf16[128,504]{0,1:T(8,128)(2,1)S(1)}, u32[]{:S(2)}, u32[]{:S(2)}) collective-permute-start(bf16[128,504]{0,1:T(8,128)(2,1)S(1)} %get-tuple-element.9), channel_id=1, source_target_pairs={{0,6},{2,0},{4,2},{6,4},{1,7},{3,1},{5,3},{7,5},{8,14},{10,8},{12,... | collective-permute-start | bytes 387080 | tf_op jit(solution)/shard_map/ppermute | solution.py:133
  140.2 2.5 %collective-permute-start.3 = (bf16[128,504]{0,1:T(8,128)(2,1)S(1)}, bf16[128,504]{0,1:T(8,128)(2,1)S(1)}, u32[]{:S(2)}, u32[]{:S(2)}) collective-permute-start(bf16[128,504]{0,1:T(8,128)(2,1)S(1)} %get-tuple-element.8), channel_id=1, source_target_pairs={{0,4},{2,6},{4,0},{6,2},{1,5},{3,7},{5,1},{7,3},{8,12},{10,14},{12... | collective-permute-start | bytes 387080 | tf_op jit(solution)/shard_map/ppermute | solution.py:133
  142.7 1.9 %collective-permute-start.2 = (bf16[128,504]{0,1:T(8,128)(2,1)S(1)}, bf16[128,504]{0,1:T(8,128)(2,1)S(1)}, u32[]{:S(2)}, u32[]{:S(2)}) collective-permute-start(bf16[128,504]{0,1:T(8,128)(2,1)S(1)} %get-tuple-element.7), channel_id=1, source_target_pairs={{0,2},{2,4},{4,6},{6,0},{1,3},{3,5},{5,7},{7,1},{8,10},{10,12},{12... | collective-permute-start | bytes 387080 | tf_op jit(solution)/shard_map/ppermute | solution.py:133
  144.7 0.0 collective-permute-done.4
  144.7 3.5 %collective-permute-done.3 = bf16[128,504]{0,1:T(8,128)(2,1)S(1)} collective-permute-done((bf16[128,504]{0,1:T(8,128)(2,1)S(1)}, bf16[128,504]{0,1:T(8,128)(2,1)S(1)}, u32[]{:S(2)}, u32[]{:S(2)}) %collective-permute-start.3) | collective-permute-done | bytes 129056 | tf_op jit(solution)/shard_map/ppermute | solution.py:133
  148.2 3.3 %collective-permute-done.2 = bf16[128,504]{0,1:T(8,128)(2,1)S(1)} collective-permute-done((bf16[128,504]{0,1:T(8,128)(2,1)S(1)}, bf16[128,504]{0,1:T(8,128)(2,1)S(1)}, u32[]{:S(2)}, u32[]{:S(2)}) %collective-permute-start.2) | collective-permute-done | bytes 129056 | tf_op jit(solution)/shard_map/ppermute | solution.py:133
  151.4 0.8 add_bitcast_fusion
  152.2 0.0 all-to-all-done.3
  152.2 1.3 convert_select_fusion.1
  153.5 0.2 pad_maximum_fusion
  153.7 0.3 fusion
  154.0 1.3 copy.18
  (10 shorter events, 0.1 us)
Async XLA Ops:
  0.6 19.6 %copy-start = (bf16[1,504,128]{2,1,0:T(8,128)(2,1)S(1)}, bf16[1,504,128]{2,1,0:T(8,128)(2,1)}, u32[]{:S(2)}) copy-start(bf16[1,504,128]{2,1,0:T(8,128)(2,1)} %param.7) | copy-start | bytes 387076
  3.1 34.6 %all-to-all-start = ((bf16[64,8,512]{2,1,0:T(8,128)(2,1)}), bf16[64,8,512]{2,1,0:T(8,128)(2,1)S(1)}, u32[]{:S(2)}, u32[]{:S(2)}) async-start(bf16[64,8,512]{2,1,0:T(8,128)(2,1)} %broadcast_select_fusion), calls=%async_computation | async-start | bytes 1048576 | tf_op jit(solution)/shard_map/all_to_all | solution.py:18
  39.7 14.1 %copy-start.2 = (bf16[128]{0:T(256)(128)(2,1)S(1)}, bf16[128]{0:T(256)(128)(2,1)}, u32[]{:S(2)}) copy-start(bf16[128]{0:T(256)(128)(2,1)} %param.8) | copy-start | bytes 772
  39.7 38.5 %all-to-all-start.1 = ((bf16[64,16,512]{2,1,0:T(8,128)(2,1)}), bf16[64,16,512]{2,1,0:T(8,128)(2,1)}, u32[]{:S(2)}, u32[]{:S(2)}) async-start(bf16[64,16,512]{2,1,0:T(8,128)(2,1)} %bitcast.68), calls=%async_computation.1 | async-start | bytes 2097152 | tf_op jit(solution)/shard_map/all_to_all | solution.py:18
  80.8 33.7 %all-to-all-start.2 = ((bf16[64,16,512]{2,1,0:T(8,128)(2,1)}), bf16[64,16,512]{2,1,0:T(8,128)(2,1)}, u32[]{:S(2)}, u32[]{:S(2)}) async-start(bf16[64,16,512]{2,1,0:T(8,128)(2,1)} %broadcast_in_dim.69), calls=%async_computation.2 | async-start | bytes 2097152 | tf_op jit(solution)/shard_map/all_to_all | solution.py:18
  93.8 40.3 %collective-permute-start.1 = (bf16[504,512]{1,0:T(8,128)(2,1)}, bf16[504,512]{1,0:T(8,128)(2,1)}, u32[]{:S(2)}, u32[]{:S(2)}) collective-permute-start(bf16[504,512]{1,0:T(8,128)(2,1)} %fusion.23), channel_id=1, source_target_pairs={{0,1},{1,0},{2,3},{3,2},{4,5},{5,4},{6,7},{7,6},{8,9},{9,8},{10,11... | collective-permute-start | bytes 1548296 | tf_op jit(solution)/shard_map/ppermute | solution.py:73
  118.7 15.5 %collective-permute-start = (bf16[4,128,512]{2,1,0:T(8,128)(2,1)}, bf16[4,128,512]{2,1,0:T(8,128)(2,1)}, u32[]{:S(2)}, u32[]{:S(2)}) collective-permute-start(bf16[4,128,512]{2,1,0:T(8,128)(2,1)} %dynamic-slice_bitcast_fusion), channel_id=1, source_target_pairs={{0,1},{1,0},{2,3},{3,2},{4,5},{5,4},{6,7},{7,6},{8,9},{9,8},{10,11... | collective-permute-start | bytes 1572872 | tf_op jit(solution)/shard_map/ppermute | solution.py:118
  126.2 26.0 %all-to-all-start.3 = ((bf16[64,8,512]{2,1,0:T(8,128)(2,1)}), bf16[64,8,512]{2,1,0:T(8,128)(2,1)}, u32[]{:S(2)}, u32[]{:S(2)}) async-start(bf16[64,8,512]{2,1,0:T(8,128)(2,1)} %fusion.1), calls=%async_computation.3 | async-start | bytes 1048576 | tf_op jit(solution)/shard_map/all_to_all | solution.py:18
  134.2 10.5 %copy-start.1 = (s32[512,1]{0,1:T(1,128)S(1)}, s32[512,1]{0,1:T(1,128)}, u32[]{:S(2)}) copy-start(s32[512,1]{0,1:T(1,128)} %param.6) | copy-start | bytes 6148
  136.0 8.7 %collective-permute-start.4 = (bf16[128,504]{0,1:T(8,128)(2,1)S(1)}, bf16[128,504]{0,1:T(8,128)(2,1)S(1)}, u32[]{:S(2)}, u32[]{:S(2)}) collective-permute-start(bf16[128,504]{0,1:T(8,128)(2,1)S(1)} %get-tuple-element.9), channel_id=1, source_target_pairs={{0,6},{2,0},{4,2},{6,4},{1,7},{3,1},{5,3},{7,5},{8,14},{10,8},{12,... | collective-permute-start | bytes 387080 | tf_op jit(solution)/shard_map/ppermute | solution.py:133
  140.2 7.9 %collective-permute-start.3 = (bf16[128,504]{0,1:T(8,128)(2,1)S(1)}, bf16[128,504]{0,1:T(8,128)(2,1)S(1)}, u32[]{:S(2)}, u32[]{:S(2)}) collective-permute-start(bf16[128,504]{0,1:T(8,128)(2,1)S(1)} %get-tuple-element.8), channel_id=1, source_target_pairs={{0,4},{2,6},{4,0},{6,2},{1,5},{3,7},{5,1},{7,3},{8,12},{10,14},{12... | collective-permute-start | bytes 387080 | tf_op jit(solution)/shard_map/ppermute | solution.py:133
  142.7 8.7 %collective-permute-start.2 = (bf16[128,504]{0,1:T(8,128)(2,1)S(1)}, bf16[128,504]{0,1:T(8,128)(2,1)S(1)}, u32[]{:S(2)}, u32[]{:S(2)}) collective-permute-start(bf16[128,504]{0,1:T(8,128)(2,1)S(1)} %get-tuple-element.7), channel_id=1, source_target_pairs={{0,2},{2,4},{4,6},{6,0},{1,3},{3,5},{5,7},{7,1},{8,10},{10,12},{12... | collective-permute-start | bytes 387080 | tf_op jit(solution)/shard_map/ppermute | solution.py:133

commit v8 on v7

--- a/solution.py
+++ b/solution.py
@@ -106,16 +106,16 @@
     ).reshape(hidden_units, sample_rows)
 
     pair_grad = lax.optimization_barrier(
-        jnp.dot(weight_rows, slope_turned, preferred_element_type=f32)
+        jnp.dot(weight_rows, slope_turned, preferred_element_type=f32).astype(bf16)
     )
-    pair_grad = pair_grad.reshape(fields, half, sample_rows)
+    pair_grad = pair_grad.reshape(fields, half, sample_rows).astype(f32)
     outgoing = (pair_grad * mine_wide).astype(bf16)
     returned = exchange(outgoing).astype(f32)
 
     halves = slope_turned.reshape(chips, cores, shard_units, sample_rows)
     kept = lax.dynamic_index_in_dim(halves, my_core, 1, keepdims=False)
-    sent = lax.dynamic_index_in_dim(halves, 1 - my_core, 1, keepdims=False)
-    got = lax.ppermute(sent, "core", [(0, 1), (1, 0)])
+    got = lax.ppermute(slope_turned, "core", [(0, 1), (1, 0)])
+    got = lax.dynamic_index_in_dim(got.reshape(halves.shape), my_core, 1, keepdims=False)
     chip_sum = lax.dot_general(
         kept, pair_rows, (((2,), (1,)), ((), ())), preferred_element_type=f32
     )

time: 156 us -> 166 us (1.064)
  the two profiles are of different devices: /device:TPU:1 before, /device:TPU:8 now
where the time goes in v8:
time: 166 us; the launch traced here: 165 us
  waiting for transfers between devices  60.7 us (37%)
  starting transfers between devices  52.1 us (31%)
  blocking collectives  24.4 us (15%)
  other arithmetic  9.82 us (6%)
  matrix products  8.02 us (5%)
  local copies, waits for them, and re-layouts  6.56 us (4%)
  Pallas kernels  2.28 us (1%)
    all_to_all x4, waiting for transfers between devices, exchange(): lax.all_to_all(blocks, 'field', split_axis=0, concat_axis=0, tiled=True)  56.2 us
    all_to_all x4, starting transfers between devices, exchange(): lax.all_to_all(blocks, 'field', split_axis=0, concat_axis=0, tiled=True)  38.6 us
    all_gather x1, blocking collectives, body(): lax.all_gather(row_major(w_pairs[0].T), ('x', 'core'), axis=0, tiled=True)  14 us
    all_gather x1, blocking collectives, body(): bias_wide = lax.all_gather(bias_terms, ('x', 'core'), axis=0, tiled=True)  10.4 us
    ppermute x3, starting transfers between devices, body(): lax.ppermute(block, 'x', [(i, (i + step) % chips) for i in range(chips)])  9.18 us
    ppermute x3, waiting for transfers between devices, body(): lax.ppermute(block, 'x', [(i, (i + step) % chips) for i in range(chips)])  4.51 us
    unnamed x11, local copies, waits for them, and re-layouts  3.97 us
  transfers between devices with their start and end apart: 9, of which 6 were waited for; matrix products, arithmetic and copies ran while one was open for 6% of the time, Pallas kernels for 1%

profile of v8, /device:TPU:8, one launch (start us, length us, event | category | flops | bytes accessed | tf_op | source)
XLA Modules:
  0.0 164.8 jit_solution(7207753968230070358)
XLA Ops:
  0.6 0.0 copy-start.1
  0.7 1.5 copy.17
  2.2 0.9 broadcast_select_fusion
  3.1 16.6 %all-to-all-start = ((bf16[64,8,512]{2,1,0:T(8,128)(2,1)}), bf16[64,8,512]{2,1,0:T(8,128)(2,1)S(1)}, u32[]{:S(2)}, u32[]{:S(2)}) async-start(bf16[64,8,512]{2,1,0:T(8,128)(2,1)} %broadcast_select_fusion), calls=%async_computation | async-start | bytes 1048576 | tf_op jit(solution)/shard_map/all_to_all | solution.py:18
  19.7 0.1 copy.15
  19.9 14.0 %all_gather.6 = bf16[1024,504]{1,0:T(8,128)(2,1)S(1)} all-gather(bf16[128,504]{1,0:T(8,128)(2,1)S(1)} %bitcast.68), channel_id=1, replica_groups=mesh['field'=64,'x'=4,'core'=2] {'x','core'}, dimensions={0}, use_global_device_ids=true | all-gather | bytes 1161216 | tf_op jit(solution)/shard_map/all_gather | solution.py:61
  33.9 5.2 %all-to-all-done = bf16[64,8,512]{2,1,0:T(8,128)(2,1)S(1)} async-done(((bf16[64,8,512]{2,1,0:T(8,128)(2,1)}), bf16[64,8,512]{2,1,0:T(8,128)(2,1)S(1)}, u32[]{:S(2)}, u32[]{:S(2)}) %all-to-all-start) | async-done | bytes 524320 | tf_op jit(solution)/shard_map/all_to_all | solution.py:18
  39.1 0.3 fusion.1
  39.4 1.8 %convolution_convert_fusion = bf16[512,1024]{0,1:T(8,128)(2,1)} fusion(bf16[1024,504]{1,0:T(8,128)(2,1)S(1)} %all_gather.6, bf16[64,8,512]{2,1,0:T(8,128)(2,1)S(1)} %fusion.1, pred[63]{0:T(512)(128)(4,1)S(1)} %iota_compare_fusion), kind=kOutput, calls=%fused_computation.4 | convolution fusion | flops 529264640 | bytes 3129856 | tf_op jit(solution)/shard_map/dot_general | solution.py:70
  41.1 7.8 %all-to-all-start.1 = ((bf16[64,16,512]{2,1,0:T(8,128)(2,1)}), bf16[64,16,512]{2,1,0:T(8,128)(2,1)}, u32[]{:S(2)}, u32[]{:S(2)}) async-start(bf16[64,16,512]{2,1,0:T(8,128)(2,1)} %bitcast.67), calls=%async_computation.1 | async-start | bytes 2097152 | tf_op jit(solution)/shard_map/all_to_all | solution.py:18
  49.0 0.6 pad_add_fusion.place_ref
  49.6 2.3 %owngrad.1 = bf16[16,512]{1,0:T(8,128)(2,1)} custom-call(s32[2]{0:T(128)} %pad_add_fusion.place_ref, bf16[512,1024]{1,0:T(8,128)(2,1)} %grad_ref.1), custom_call_target="tpu_custom_call" | custom-call | tf_op jit(solution)/shard_map/owngrad/pallas_call | solution.py:30
  51.9 0.7 convert_element_type.88
  52.6 10.4 %all-gather = bf16[8,1,128]{2,1,0:T(2,128)(2,1)S(1)} all-gather(bf16[1,1,128]{2,1,0:T(2,128)(2,1)S(1)} %bitcast.71), channel_id=1, replica_groups=mesh['field'=64,'x'=4,'core'=2] {'x','core'}, dimensions={0}, use_global_device_ids=true | all-gather | bytes 2304 | tf_op jit(solution)/shard_map/all_gather | solution.py:75
  63.0 0.1 dynamic-slice_convert_fusion.3
  63.1 15.5 %all-to-all-done.1 = bf16[64,16,512]{2,1,0:T(8,128)(2,1)} async-done(((bf16[64,16,512]{2,1,0:T(8,128)(2,1)}), bf16[64,16,512]{2,1,0:T(8,128)(2,1)}, u32[]{:S(2)}, u32[]{:S(2)}) %all-to-all-start.1) | async-done | bytes 1048608 | tf_op jit(solution)/shard_map/all_to_all | solution.py:18
  78.6 1.4 convert_reduce_fusion
  80.0 0.1 multiply_convert_fusion
  80.1 1.1 broadcast_in_dim.69
  81.3 7.5 %all-to-all-start.2 = ((bf16[64,16,512]{2,1,0:T(8,128)(2,1)}), bf16[64,16,512]{2,1,0:T(8,128)(2,1)}, u32[]{:S(2)}, u32[]{:S(2)}) async-start(bf16[64,16,512]{2,1,0:T(8,128)(2,1)} %broadcast_in_dim.69), calls=%async_computation.2 | async-start | bytes 2097152 | tf_op jit(solution)/shard_map/all_to_all | solution.py:18
  88.8 1.4 copy.16
  90.2 2.9 %select_select_fusion = bf16[512,1024]{1,0:T(8,128)(2,1)} fusion(bf16[504,1024]{1,0:T(8,128)(2,1)} %bitcast.66, pred[512]{0:T(512)(128)(4,1)S(1)} %get-tuple-element.21, pred[512]{0:T(512)(128)(4,1)S(1)} %get-tuple-element.22), kind=kLoop, calls=%fused_computation.14 | loop fusion | flops 1048576 | bytes 2081792 | tf_op jit(solution)/shard_map/jit(_where)/select_n | solution.py:95
  93.1 24.4 %all-to-all-done.2 = bf16[64,16,512]{2,1,0:T(8,128)(2,1)} async-done(((bf16[64,16,512]{2,1,0:T(8,128)(2,1)}), bf16[64,16,512]{2,1,0:T(8,128)(2,1)}, u32[]{:S(2)}, u32[]{:S(2)}) %all-to-all-start.2) | async-done | bytes 1048608 | tf_op jit(solution)/shard_map/all_to_all | solution.py:18
  117.4 2.2 %convolution_convert_fusion.1 = bf16[512,512]{1,0:T(8,128)(2,1)S(1)} fusion(bf16[512,1024]{1,0:T(8,128)(2,1)} %select_select_fusion, bf16[1024,512]{1,0:T(8,128)(2,1)} %bitcast.12), kind=kOutput, calls=%fused_computation.11 | convolution fusion | flops 537133056 | bytes 2621440 | tf_op jit(solution)/shard_map/dot_general | solution.py:109
  119.7 0.0 copy-start.2
  119.7 1.1 fusion.2
  120.7 6.7 %all-to-all-start.3 = ((bf16[64,8,512]{2,1,0:T(8,128)(2,1)}), bf16[64,8,512]{2,1,0:T(8,128)(2,1)S(1)}, u32[]{:S(2)}, u32[]{:S(2)}) async-start(bf16[64,8,512]{2,1,0:T(8,128)(2,1)} %fusion.2), calls=%async_computation.3 | async-start | bytes 1048576 | tf_op jit(solution)/shard_map/all_to_all | solution.py:18
  127.4 1.9 %collective-permute-start = (bf16[1024,512]{1,0:T(8,128)(2,1)}, bf16[1024,512]{1,0:T(8,128)(2,1)}, u32[]{:S(2)}, u32[]{:S(2)}) collective-permute-start(bf16[1024,512]{1,0:T(8,128)(2,1)} %bitcast.12), channel_id=1, source_target_pairs={{0,1},{1,0},{2,3},{3,2},{4,5},{5,4},{6,7},{7,6},{8,9},{9,8},{10,11... | collective-permute-start | bytes 3145736 | tf_op jit(solution)/shard_map/ppermute | solution.py:117
  129.4 0.1 fusion.24
  129.6 2.4 %collective-permute-start.1 = (bf16[504,512]{1,0:T(8,128)(2,1)S(1)}, bf16[504,512]{1,0:T(8,128)(2,1)S(1)}, u32[]{:S(2)}, u32[]{:S(2)}) collective-permute-start(bf16[504,512]{1,0:T(8,128)(2,1)S(1)} %fusion.24), channel_id=1, source_target_pairs={{0,1},{1,0},{2,3},{3,2},{4,5},{5,4},{6,7},{7,6},{8,9},{9,8},{10,11... | collective-permute-start | bytes 1548296 | tf_op jit(solution)/shard_map/ppermute | solution.py:73
  132.0 2.5 %fusion.4 = f32[4,128,504]{1,2,0:T(8,128)} fusion(bf16[4,2,128,512]{3,2,1,0:T(8,128)(2,1)} %bitcast.19, s32[]{:T(128)S(6)} %select_n.103, bf16[64,8,512]{2,1,0:T(8,128)(2,1)S(1)} %fusion.1, pred[63]{0:T(512)(128)(4,1)S(1)} %iota_compare_fusion), kind=kOutput, calls=%fused_computation.16 | convolution fusion | flops 264499200 | bytes 2589188 | tf_op jit(solution)/shard_map/dot_general | solution.py:119
  134.5 11.1 %all-to-all-done.3 = bf16[64,8,512]{2,1,0:T(8,128)(2,1)S(1)} async-done(((bf16[64,8,512]{2,1,0:T(8,128)(2,1)}), bf16[64,8,512]{2,1,0:T(8,128)(2,1)S(1)}, u32[]{:S(2)}, u32[]{:S(2)}) %all-to-all-start.3) | async-done | bytes 524320 | tf_op jit(solution)/shard_map/all_to_all | solution.py:18
  145.5 0.3 convert_select_fusion.1
  145.8 0.0 copy-start
  145.9 0.2 pad_maximum_fusion
  146.1 0.0 collective-permute-done.1
  146.1 0.0 collective-permute-done
  146.1 1.0 copy-done
  147.1 1.5 convolution_add_fusion
  148.6 0.1 fusion.12
  148.7 4.5 %collective-permute-start.4 = (bf16[128,504]{0,1:T(8,128)(2,1)S(1)}, bf16[128,504]{0,1:T(8,128)(2,1)S(1)}, u32[]{:S(2)}, u32[]{:S(2)}) collective-permute-start(bf16[128,504]{0,1:T(8,128)(2,1)S(1)} %get-tuple-element.9), channel_id=1, source_target_pairs={{0,6},{2,0},{4,2},{6,4},{1,7},{3,1},{5,3},{7,5},{8,14},{10,8},{12,... | collective-permute-start | bytes 387080 | tf_op jit(solution)/shard_map/ppermute | solution.py:133
  153.2 2.8 %collective-permute-start.3 = (bf16[128,504]{0,1:T(8,128)(2,1)S(1)}, bf16[128,504]{0,1:T(8,128)(2,1)S(1)}, u32[]{:S(2)}, u32[]{:S(2)}) collective-permute-start(bf16[128,504]{0,1:T(8,128)(2,1)S(1)} %get-tuple-element.8), channel_id=1, source_target_pairs={{0,4},{2,6},{4,0},{6,2},{1,5},{3,7},{5,1},{7,3},{8,12},{10,14},{12... | collective-permute-start | bytes 387080 | tf_op jit(solution)/shard_map/ppermute | solution.py:133
  156.0 1.9 %collective-permute-start.2 = (bf16[128,504]{0,1:T(8,128)(2,1)S(1)}, bf16[128,504]{0,1:T(8,128)(2,1)S(1)}, u32[]{:S(2)}, u32[]{:S(2)}) collective-permute-start(bf16[128,504]{0,1:T(8,128)(2,1)S(1)} %get-tuple-element.7), channel_id=1, source_target_pairs={{0,2},{2,4},{4,6},{6,0},{1,3},{3,5},{5,7},{7,1},{8,10},{10,12},{12... | collective-permute-start | bytes 387080 | tf_op jit(solution)/shard_map/ppermute | solution.py:133
  157.9 0.3 fusion
  158.2 1.3 copy.18
  159.5 2.0 %collective-permute-done.3 = bf16[128,504]{0,1:T(8,128)(2,1)S(1)} collective-permute-done((bf16[128,504]{0,1:T(8,128)(2,1)S(1)}, bf16[128,504]{0,1:T(8,128)(2,1)S(1)}, u32[]{:S(2)}, u32[]{:S(2)}) %collective-permute-start.3) | collective-permute-done | bytes 129056 | tf_op jit(solution)/shard_map/ppermute | solution.py:133
  161.5 2.5 %collective-permute-done.2 = bf16[128,504]{0,1:T(8,128)(2,1)S(1)} collective-permute-done((bf16[128,504]{0,1:T(8,128)(2,1)S(1)}, bf16[128,504]{0,1:T(8,128)(2,1)S(1)}, u32[]{:S(2)}, u32[]{:S(2)}) %collective-permute-start.2) | collective-permute-done | bytes 129056 | tf_op jit(solution)/shard_map/ppermute | solution.py:133
  164.0 0.8 add_bitcast_fusion
  (11 shorter events, 0.1 us)
Async XLA Ops:
  0.6 19.1 %copy-start.1 = (bf16[1,504,128]{2,1,0:T(8,128)(2,1)S(1)}, bf16[1,504,128]{2,1,0:T(8,128)(2,1)}, u32[]{:S(2)}) copy-start(bf16[1,504,128]{2,1,0:T(8,128)(2,1)} %param.7) | copy-start | bytes 387076
  3.1 36.0 %all-to-all-start = ((bf16[64,8,512]{2,1,0:T(8,128)(2,1)}), bf16[64,8,512]{2,1,0:T(8,128)(2,1)S(1)}, u32[]{:S(2)}, u32[]{:S(2)}) async-start(bf16[64,8,512]{2,1,0:T(8,128)(2,1)} %broadcast_select_fusion), calls=%async_computation | async-start | bytes 1048576 | tf_op jit(solution)/shard_map/all_to_all | solution.py:18
  41.1 11.5 %copy-start.3 = (bf16[128]{0:T(256)(128)(2,1)S(1)}, bf16[128]{0:T(256)(128)(2,1)}, u32[]{:S(2)}) copy-start(bf16[128]{0:T(256)(128)(2,1)} %param.8) | copy-start | bytes 772
  41.1 37.5 %all-to-all-start.1 = ((bf16[64,16,512]{2,1,0:T(8,128)(2,1)}), bf16[64,16,512]{2,1,0:T(8,128)(2,1)}, u32[]{:S(2)}, u32[]{:S(2)}) async-start(bf16[64,16,512]{2,1,0:T(8,128)(2,1)} %bitcast.67), calls=%async_computation.1 | async-start | bytes 2097152 | tf_op jit(solution)/shard_map/all_to_all | solution.py:18
  81.3 36.1 %all-to-all-start.2 = ((bf16[64,16,512]{2,1,0:T(8,128)(2,1)}), bf16[64,16,512]{2,1,0:T(8,128)(2,1)}, u32[]{:S(2)}, u32[]{:S(2)}) async-start(bf16[64,16,512]{2,1,0:T(8,128)(2,1)} %broadcast_in_dim.69), calls=%async_computation.2 | async-start | bytes 2097152 | tf_op jit(solution)/shard_map/all_to_all | solution.py:18
  119.7 9.7 %copy-start.2 = (s32[512,1]{0,1:T(1,128)S(1)}, s32[512,1]{0,1:T(1,128)}, u32[]{:S(2)}) copy-start(s32[512,1]{0,1:T(1,128)} %param.6) | copy-start | bytes 6148
  120.7 24.8 %all-to-all-start.3 = ((bf16[64,8,512]{2,1,0:T(8,128)(2,1)}), bf16[64,8,512]{2,1,0:T(8,128)(2,1)S(1)}, u32[]{:S(2)}, u32[]{:S(2)}) async-start(bf16[64,8,512]{2,1,0:T(8,128)(2,1)} %fusion.2), calls=%async_computation.3 | async-start | bytes 1048576 | tf_op jit(solution)/shard_map/all_to_all | solution.py:18
  127.4 18.7 %collective-permute-start = (bf16[1024,512]{1,0:T(8,128)(2,1)}, bf16[1024,512]{1,0:T(8,128)(2,1)}, u32[]{:S(2)}, u32[]{:S(2)}) collective-permute-start(bf16[1024,512]{1,0:T(8,128)(2,1)} %bitcast.12), channel_id=1, source_target_pairs={{0,1},{1,0},{2,3},{3,2},{4,5},{5,4},{6,7},{7,6},{8,9},{9,8},{10,11... | collective-permute-start | bytes 3145736 | tf_op jit(solution)/shard_map/ppermute | solution.py:117
  129.6 16.5 %collective-permute-start.1 = (bf16[504,512]{1,0:T(8,128)(2,1)S(1)}, bf16[504,512]{1,0:T(8,128)(2,1)S(1)}, u32[]{:S(2)}, u32[]{:S(2)}) collective-permute-start(bf16[504,512]{1,0:T(8,128)(2,1)S(1)} %fusion.24), channel_id=1, source_target_pairs={{0,1},{1,0},{2,3},{3,2},{4,5},{5,4},{6,7},{7,6},{8,9},{9,8},{10,11... | collective-permute-start | bytes 1548296 | tf_op jit(solution)/shard_map/ppermute | solution.py:73
  145.8 1.2 copy-start
  148.7 10.8 %collective-permute-start.4 = (bf16[128,504]{0,1:T(8,128)(2,1)S(1)}, bf16[128,504]{0,1:T(8,128)(2,1)S(1)}, u32[]{:S(2)}, u32[]{:S(2)}) collective-permute-start(bf16[128,504]{0,1:T(8,128)(2,1)S(1)} %get-tuple-element.9), channel_id=1, source_target_pairs={{0,6},{2,0},{4,2},{6,4},{1,7},{3,1},{5,3},{7,5},{8,14},{10,8},{12,... | collective-permute-start | bytes 387080 | tf_op jit(solution)/shard_map/ppermute | solution.py:133
  153.2 8.3 %collective-permute-start.3 = (bf16[128,504]{0,1:T(8,128)(2,1)S(1)}, bf16[128,504]{0,1:T(8,128)(2,1)S(1)}, u32[]{:S(2)}, u32[]{:S(2)}) collective-permute-start(bf16[128,504]{0,1:T(8,128)(2,1)S(1)} %get-tuple-element.8), channel_id=1, source_target_pairs={{0,4},{2,6},{4,0},{6,2},{1,5},{3,7},{5,1},{7,3},{8,12},{10,14},{12... | collective-permute-start | bytes 387080 | tf_op jit(solution)/shard_map/ppermute | solution.py:133
  156.0 8.1 %collective-permute-start.2 = (bf16[128,504]{0,1:T(8,128)(2,1)S(1)}, bf16[128,504]{0,1:T(8,128)(2,1)S(1)}, u32[]{:S(2)}, u32[]{:S(2)}) collective-permute-start(bf16[128,504]{0,1:T(8,128)(2,1)S(1)} %get-tuple-element.7), channel_id=1, source_target_pairs={{0,2},{2,4},{4,6},{6,0},{1,3},{3,5},{5,7},{7,1},{8,10},{10,12},{12... | collective-permute-start | bytes 387080 | tf_op jit(solution)/shard_map/ppermute | solution.py:133

commit v9 on v8

--- a/solution.py
+++ b/solution.py
@@ -135,12 +135,14 @@
         )
         weight_total = weight_total + chip_got.astype(f32)
 
-    local = pair_grad * received_wide
+    root = jnp.sqrt(counts[:, 0].astype(f32))[None, None, :]
+    late_grad, _ = lax.optimization_barrier((pair_grad.astype(bf16), outgoing))
+    local = lax.optimization_barrier((late_grad.astype(f32) * received_wide / root).astype(bf16))
+    returned = (returned / root).astype(bf16)
     full = jnp.concatenate(
         [jnp.where(upper, returned, local), jnp.where(upper, local, returned)], 1
     )
-    full = full / jnp.sqrt(counts[:, 0].astype(f32))[None, None, :]
-    turned = row_major(full.astype(bf16).reshape(fields * depth, sample_rows))
+    turned = row_major(full.reshape(fields * depth, sample_rows))
     entry_grad = turned.T[:, None, :]
     return entry_grad, weight_total.T[None]
 

time: 166 us -> 165 us (level)
    unnamed x11 -> x9, local copies, waits for them, and re-layouts: 3.97 us -> 2.98 us
where the time goes in v9:
time: 165 us; the launch traced here: 164 us
  waiting for transfers between devices  60.8 us (37%)
  starting transfers between devices  52.1 us (32%)
  blocking collectives  24.4 us (15%)
  other arithmetic  10.4 us (6%)
  matrix products  7.21 us (4%)
  local copies, waits for them, and re-layouts  5.57 us (3%)
  Pallas kernels  2.28 us (1%)
    all_to_all x4, waiting for transfers between devices, exchange(): lax.all_to_all(blocks, 'field', split_axis=0, concat_axis=0, tiled=True)  56.1 us
    all_to_all x4, starting transfers between devices, exchange(): lax.all_to_all(blocks, 'field', split_axis=0, concat_axis=0, tiled=True)  38.6 us
    all_gather x1, blocking collectives, body(): lax.all_gather(row_major(w_pairs[0].T), ('x', 'core'), axis=0, tiled=True)  14 us
    all_gather x1, blocking collectives, body(): bias_wide = lax.all_gather(bias_terms, ('x', 'core'), axis=0, tiled=True)  10.4 us
    ppermute x3, starting transfers between devices, body(): lax.ppermute(block, 'x', [(i, (i + step) % chips) for i in range(chips)])  9.18 us
    ppermute x3, waiting for transfers between devices, body(): lax.ppermute(block, 'x', [(i, (i + step) % chips) for i in range(chips)])  4.65 us
  transfers between devices with their start and end apart: 9, of which 6 were waited for; matrix products, arithmetic and copies ran while one was open for 6% of the time, Pallas kernels for 1%

profile of v9, /device:TPU:8, one launch (start us, length us, event | category | flops | bytes accessed | tf_op | source)
XLA Modules:
  0.0 163.7 jit_solution(12425875316044342138)
XLA Ops:
  0.6 1.5 copy.17
  2.2 0.0 copy-start
  2.2 0.9 broadcast_select_fusion.2
  3.1 16.6 %all-to-all-start = ((bf16[64,8,512]{2,1,0:T(8,128)(2,1)}), bf16[64,8,512]{2,1,0:T(8,128)(2,1)S(1)}, u32[]{:S(2)}, u32[]{:S(2)}) async-start(bf16[64,8,512]{2,1,0:T(8,128)(2,1)} %broadcast_select_fusion.2), calls=%async_computation | async-start | bytes 1048576 | tf_op jit(solution)/shard_map/all_to_all | solution.py:18
  19.7 0.1 copy.15
  19.9 14.0 %all_gather.6 = bf16[1024,504]{1,0:T(8,128)(2,1)S(1)} all-gather(bf16[128,504]{1,0:T(8,128)(2,1)S(1)} %bitcast.64), channel_id=1, replica_groups=mesh['field'=64,'x'=4,'core'=2] {'x','core'}, dimensions={0}, use_global_device_ids=true | all-gather | bytes 1161216 | tf_op jit(solution)/shard_map/all_gather | solution.py:61
  33.9 5.2 %all-to-all-done = bf16[64,8,512]{2,1,0:T(8,128)(2,1)S(1)} async-done(((bf16[64,8,512]{2,1,0:T(8,128)(2,1)}), bf16[64,8,512]{2,1,0:T(8,128)(2,1)S(1)}, u32[]{:S(2)}, u32[]{:S(2)}) %all-to-all-start) | async-done | bytes 524320 | tf_op jit(solution)/shard_map/all_to_all | solution.py:18
  39.1 0.3 fusion.1
  39.4 1.8 %convolution_convert_fusion = bf16[512,1024]{0,1:T(8,128)(2,1)} fusion(bf16[1024,504]{1,0:T(8,128)(2,1)S(1)} %all_gather.6, bf16[64,8,512]{2,1,0:T(8,128)(2,1)S(1)} %fusion.1, pred[63]{0:T(512)(128)(4,1)S(1)} %iota_compare_fusion), kind=kOutput, calls=%fused_computation.1 | convolution fusion | flops 529264640 | bytes 3129856 | tf_op jit(solution)/shard_map/dot_general | solution.py:70
  41.1 7.7 %all-to-all-start.1 = ((bf16[64,16,512]{2,1,0:T(8,128)(2,1)}), bf16[64,16,512]{2,1,0:T(8,128)(2,1)}, u32[]{:S(2)}, u32[]{:S(2)}) async-start(bf16[64,16,512]{2,1,0:T(8,128)(2,1)} %bitcast.63), calls=%async_computation.1 | async-start | bytes 2097152 | tf_op jit(solution)/shard_map/all_to_all | solution.py:18
  48.8 0.0 copy-start.2
  48.9 0.7 pad_add_fusion.place_ref
  49.5 2.3 %owngrad.1 = bf16[16,512]{1,0:T(8,128)(2,1)} custom-call(s32[2]{0:T(128)} %pad_add_fusion.place_ref, bf16[512,1024]{1,0:T(8,128)(2,1)} %grad_ref.1), custom_call_target="tpu_custom_call" | custom-call | tf_op jit(solution)/shard_map/owngrad/pallas_call | solution.py:30
  51.8 0.7 convert_element_type.91
  52.5 10.4 %all-gather = bf16[8,1,128]{2,1,0:T(2,128)(2,1)S(1)} all-gather(bf16[1,1,128]{2,1,0:T(2,128)(2,1)S(1)} %bitcast.68), channel_id=1, replica_groups=mesh['field'=64,'x'=4,'core'=2] {'x','core'}, dimensions={0}, use_global_device_ids=true | all-gather | bytes 2304 | tf_op jit(solution)/shard_map/all_gather | solution.py:75
  62.9 0.1 dynamic-slice_convert_fusion.3
  63.0 15.5 %all-to-all-done.1 = bf16[64,16,512]{2,1,0:T(8,128)(2,1)} async-done(((bf16[64,16,512]{2,1,0:T(8,128)(2,1)}), bf16[64,16,512]{2,1,0:T(8,128)(2,1)}, u32[]{:S(2)}, u32[]{:S(2)}) %all-to-all-start.1) | async-done | bytes 1048608 | tf_op jit(solution)/shard_map/all_to_all | solution.py:18
  78.5 1.4 convert_reduce_fusion
  79.9 0.1 multiply_convert_fusion
  80.0 1.1 broadcast_in_dim.66
  81.1 7.5 %all-to-all-start.2 = ((bf16[64,16,512]{2,1,0:T(8,128)(2,1)}), bf16[64,16,512]{2,1,0:T(8,128)(2,1)}, u32[]{:S(2)}, u32[]{:S(2)}) async-start(bf16[64,16,512]{2,1,0:T(8,128)(2,1)} %broadcast_in_dim.66), calls=%async_computation.2 | async-start | bytes 2097152 | tf_op jit(solution)/shard_map/all_to_all | solution.py:18
  88.6 1.4 copy.16
  90.0 2.9 %select_select_fusion = bf16[512,1024]{1,0:T(8,128)(2,1)} fusion(bf16[504,1024]{1,0:T(8,128)(2,1)} %bitcast.61, pred[512]{0:T(512)(128)(4,1)S(1)} %get-tuple-element.23, pred[512]{0:T(512)(128)(4,1)S(1)} %get-tuple-element.24), kind=kLoop, calls=%fused_computation.13 | loop fusion | flops 1048576 | bytes 2081792 | tf_op jit(solution)/shard_map/jit(_where)/select_n | solution.py:95
  92.9 24.4 %all-to-all-done.2 = bf16[64,16,512]{2,1,0:T(8,128)(2,1)} async-done(((bf16[64,16,512]{2,1,0:T(8,128)(2,1)}), bf16[64,16,512]{2,1,0:T(8,128)(2,1)}, u32[]{:S(2)}, u32[]{:S(2)}) %all-to-all-start.2) | async-done | bytes 1048608 | tf_op jit(solution)/shard_map/all_to_all | solution.py:18
  117.2 2.2 %convolution_convert_fusion.1 = bf16[512,512]{1,0:T(8,128)(2,1)S(1)} fusion(bf16[512,1024]{1,0:T(8,128)(2,1)} %select_select_fusion, bf16[1024,512]{1,0:T(8,128)(2,1)} %bitcast.12), kind=kOutput, calls=%fused_computation.6 | convolution fusion | flops 537133056 | bytes 2621440 | tf_op jit(solution)/shard_map/dot_general | solution.py:109
  119.5 1.1 fusion
  120.6 6.8 %all-to-all-start.3 = ((bf16[64,8,512]{2,1,0:T(8,128)(2,1)}), bf16[64,8,512]{2,1,0:T(8,128)(2,1)S(1)}, u32[]{:S(2)}, u32[]{:S(2)}) async-start(bf16[64,8,512]{2,1,0:T(8,128)(2,1)} %fusion), calls=%async_computation.3 | async-start | bytes 1048576 | tf_op jit(solution)/shard_map/all_to_all | solution.py:18
  127.4 0.0 copy-done.1
  127.4 1.9 %collective-permute-start = (bf16[1024,512]{1,0:T(8,128)(2,1)}, bf16[1024,512]{1,0:T(8,128)(2,1)}, u32[]{:S(2)}, u32[]{:S(2)}) collective-permute-start(bf16[1024,512]{1,0:T(8,128)(2,1)} %bitcast.12), channel_id=1, source_target_pairs={{0,1},{1,0},{2,3},{3,2},{4,5},{5,4},{6,7},{7,6},{8,9},{9,8},{10,11... | collective-permute-start | bytes 3145736 | tf_op jit(solution)/shard_map/ppermute | solution.py:117
  129.4 0.9 fusion.25
  130.3 2.4 %collective-permute-start.1 = (bf16[504,512]{1,0:T(8,128)(2,1)}, bf16[504,512]{1,0:T(8,128)(2,1)}, u32[]{:S(2)}, u32[]{:S(2)}) collective-permute-start(bf16[504,512]{1,0:T(8,128)(2,1)} %fusion.25), channel_id=1, source_target_pairs={{0,1},{1,0},{2,3},{3,2},{4,5},{5,4},{6,7},{7,6},{8,9},{9,8},{10,11... | collective-permute-start | bytes 1548296 | tf_op jit(solution)/shard_map/ppermute | solution.py:73
  132.7 0.2 fusion.3
  132.9 1.5 fusion.5
  134.4 11.1 %all-to-all-done.3 = bf16[64,8,512]{2,1,0:T(8,128)(2,1)S(1)} async-done(((bf16[64,8,512]{2,1,0:T(8,128)(2,1)}), bf16[64,8,512]{2,1,0:T(8,128)(2,1)S(1)}, u32[]{:S(2)}, u32[]{:S(2)}) %all-to-all-start.3) | async-done | bytes 524320 | tf_op jit(solution)/shard_map/all_to_all | solution.py:18
  145.5 0.3 broadcast_select_fusion.1
  145.8 0.0 collective-permute-done.1
  145.8 0.0 collective-permute-done
  145.8 1.7 %convolution_add_fusion = f32[4,128,504]{1,2,0:T(8,128)S(1)} fusion(f32[4,128,504]{1,2,0:T(8,128)S(1)} %fusion.5, bf16[4,2,128,512]{3,2,1,0:T(8,128)(2,1)} %bitcast.21, s32[]{:T(128)S(6)} %select_n.102, bf16[504,512]{1,0:T(8,128)(2,1)} %collective-permute-done.1), kind=kOutput, calls=%fused_computation.2 | convolution fusion | flops 264499200 | bytes 3104772 | tf_op jit(solution)/shard_map/dot_general | solution.py:122
  147.5 0.1 fusion.13
  147.6 4.5 %collective-permute-start.4 = (bf16[128,504]{0,1:T(8,128)(2,1)S(1)}, bf16[128,504]{0,1:T(8,128)(2,1)S(1)}, u32[]{:S(2)}, u32[]{:S(2)}) collective-permute-start(bf16[128,504]{0,1:T(8,128)(2,1)S(1)} %get-tuple-element.11), channel_id=1, source_target_pairs={{0,6},{2,0},{4,2},{6,4},{1,7},{3,1},{5,3},{7,5},{8,14},{10,8},{12,... | collective-permute-start | bytes 387080 | tf_op jit(solution)/shard_map/ppermute | solution.py:133
  152.1 2.8 %collective-permute-start.3 = (bf16[128,504]{0,1:T(8,128)(2,1)S(1)}, bf16[128,504]{0,1:T(8,128)(2,1)S(1)}, u32[]{:S(2)}, u32[]{:S(2)}) collective-permute-start(bf16[128,504]{0,1:T(8,128)(2,1)S(1)} %get-tuple-element.10), channel_id=1, source_target_pairs={{0,4},{2,6},{4,0},{6,2},{1,5},{3,7},{5,1},{7,3},{8,12},{10,14},{12... | collective-permute-start | bytes 387080 | tf_op jit(solution)/shard_map/ppermute | solution.py:133
  154.8 1.9 %collective-permute-start.2 = (bf16[128,504]{0,1:T(8,128)(2,1)S(1)}, bf16[128,504]{0,1:T(8,128)(2,1)S(1)}, u32[]{:S(2)}, u32[]{:S(2)}) collective-permute-start(bf16[128,504]{0,1:T(8,128)(2,1)S(1)} %get-tuple-element.9), channel_id=1, source_target_pairs={{0,2},{2,4},{4,6},{6,0},{1,3},{3,5},{5,7},{7,1},{8,10},{10,12},{12... | collective-permute-start | bytes 387080 | tf_op jit(solution)/shard_map/ppermute | solution.py:133
  156.8 0.1 pad_maximum_fusion
  156.9 1.3 copy.18
  158.2 0.0 collective-permute-done.4
  158.2 2.2 %collective-permute-done.3 = bf16[128,504]{0,1:T(8,128)(2,1)S(1)} collective-permute-done((bf16[128,504]{0,1:T(8,128)(2,1)S(1)}, bf16[128,504]{0,1:T(8,128)(2,1)S(1)}, u32[]{:S(2)}, u32[]{:S(2)}) %collective-permute-start.3) | collective-permute-done | bytes 129056 | tf_op jit(solution)/shard_map/ppermute | solution.py:133
  160.4 2.5 %collective-permute-done.2 = bf16[128,504]{0,1:T(8,128)(2,1)S(1)} collective-permute-done((bf16[128,504]{0,1:T(8,128)(2,1)S(1)}, bf16[128,504]{0,1:T(8,128)(2,1)S(1)}, u32[]{:S(2)}, u32[]{:S(2)}) %collective-permute-start.2) | collective-permute-done | bytes 129056 | tf_op jit(solution)/shard_map/ppermute | solution.py:133
  162.9 0.8 add_bitcast_fusion
  (9 shorter events, 0.1 us)
Async XLA Ops:
  2.2 17.5 %copy-start = (bf16[1,504,128]{2,1,0:T(8,128)(2,1)S(1)}, bf16[1,504,128]{2,1,0:T(8,128)(2,1)}, u32[]{:S(2)}) copy-start(bf16[1,504,128]{2,1,0:T(8,128)(2,1)} %param.7) | copy-start | bytes 387076
  3.1 36.0 %all-to-all-start = ((bf16[64,8,512]{2,1,0:T(8,128)(2,1)}), bf16[64,8,512]{2,1,0:T(8,128)(2,1)S(1)}, u32[]{:S(2)}, u32[]{:S(2)}) async-start(bf16[64,8,512]{2,1,0:T(8,128)(2,1)} %broadcast_select_fusion.2), calls=%async_computation | async-start | bytes 1048576 | tf_op jit(solution)/shard_map/all_to_all | solution.py:18
  41.1 37.4 %all-to-all-start.1 = ((bf16[64,16,512]{2,1,0:T(8,128)(2,1)}), bf16[64,16,512]{2,1,0:T(8,128)(2,1)}, u32[]{:S(2)}, u32[]{:S(2)}) async-start(bf16[64,16,512]{2,1,0:T(8,128)(2,1)} %bitcast.63), calls=%async_computation.1 | async-start | bytes 2097152 | tf_op jit(solution)/shard_map/all_to_all | solution.py:18
  48.8 3.7 %copy-start.2 = (bf16[128]{0:T(256)(128)(2,1)S(1)}, bf16[128]{0:T(256)(128)(2,1)}, u32[]{:S(2)}) copy-start(bf16[128]{0:T(256)(128)(2,1)} %param.8) | copy-start | bytes 772
  81.1 36.1 %all-to-all-start.2 = ((bf16[64,16,512]{2,1,0:T(8,128)(2,1)}), bf16[64,16,512]{2,1,0:T(8,128)(2,1)}, u32[]{:S(2)}, u32[]{:S(2)}) async-start(bf16[64,16,512]{2,1,0:T(8,128)(2,1)} %broadcast_in_dim.66), calls=%async_computation.2 | async-start | bytes 2097152 | tf_op jit(solution)/shard_map/all_to_all | solution.py:18
  120.6 6.9 %copy-start.1 = (s32[512,1]{0,1:T(1,128)S(1)}, s32[512,1]{0,1:T(1,128)}, u32[]{:S(2)}) copy-start(s32[512,1]{0,1:T(1,128)} %param.6) | copy-start | bytes 6148
  120.6 24.9 %all-to-all-start.3 = ((bf16[64,8,512]{2,1,0:T(8,128)(2,1)}), bf16[64,8,512]{2,1,0:T(8,128)(2,1)S(1)}, u32[]{:S(2)}, u32[]{:S(2)}) async-start(bf16[64,8,512]{2,1,0:T(8,128)(2,1)} %fusion), calls=%async_computation.3 | async-start | bytes 1048576 | tf_op jit(solution)/shard_map/all_to_all | solution.py:18
  127.4 18.3 %collective-permute-start = (bf16[1024,512]{1,0:T(8,128)(2,1)}, bf16[1024,512]{1,0:T(8,128)(2,1)}, u32[]{:S(2)}, u32[]{:S(2)}) collective-permute-start(bf16[1024,512]{1,0:T(8,128)(2,1)} %bitcast.12), channel_id=1, source_target_pairs={{0,1},{1,0},{2,3},{3,2},{4,5},{5,4},{6,7},{7,6},{8,9},{9,8},{10,11... | collective-permute-start | bytes 3145736 | tf_op jit(solution)/shard_map/ppermute | solution.py:117
  130.3 15.5 %collective-permute-start.1 = (bf16[504,512]{1,0:T(8,128)(2,1)}, bf16[504,512]{1,0:T(8,128)(2,1)}, u32[]{:S(2)}, u32[]{:S(2)}) collective-permute-start(bf16[504,512]{1,0:T(8,128)(2,1)} %fusion.25), channel_id=1, source_target_pairs={{0,1},{1,0},{2,3},{3,2},{4,5},{5,4},{6,7},{7,6},{8,9},{9,8},{10,11... | collective-permute-start | bytes 1548296 | tf_op jit(solution)/shard_map/ppermute | solution.py:73
  147.6 10.7 %collective-permute-start.4 = (bf16[128,504]{0,1:T(8,128)(2,1)S(1)}, bf16[128,504]{0,1:T(8,128)(2,1)S(1)}, u32[]{:S(2)}, u32[]{:S(2)}) collective-permute-start(bf16[128,504]{0,1:T(8,128)(2,1)S(1)} %get-tuple-element.11), channel_id=1, source_target_pairs={{0,6},{2,0},{4,2},{6,4},{1,7},{3,1},{5,3},{7,5},{8,14},{10,8},{12,... | collective-permute-start | bytes 387080 | tf_op jit(solution)/shard_map/ppermute | solution.py:133
  152.1 8.3 %collective-permute-start.3 = (bf16[128,504]{0,1:T(8,128)(2,1)S(1)}, bf16[128,504]{0,1:T(8,128)(2,1)S(1)}, u32[]{:S(2)}, u32[]{:S(2)}) collective-permute-start(bf16[128,504]{0,1:T(8,128)(2,1)S(1)} %get-tuple-element.10), channel_id=1, source_target_pairs={{0,4},{2,6},{4,0},{6,2},{1,5},{3,7},{5,1},{7,3},{8,12},{10,14},{12... | collective-permute-start | bytes 387080 | tf_op jit(solution)/shard_map/ppermute | solution.py:133
  154.8 8.1 %collective-permute-start.2 = (bf16[128,504]{0,1:T(8,128)(2,1)S(1)}, bf16[128,504]{0,1:T(8,128)(2,1)S(1)}, u32[]{:S(2)}, u32[]{:S(2)}) collective-permute-start(bf16[128,504]{0,1:T(8,128)(2,1)S(1)} %get-tuple-element.9), channel_id=1, source_target_pairs={{0,2},{2,4},{4,6},{6,0},{1,3},{3,5},{5,7},{7,1},{8,10},{10,12},{12... | collective-permute-start | bytes 387080 | tf_op jit(solution)/shard_map/ppermute | solution.py:133
